TPU v7x, 32 devices: a whole 2x2x4 slice. The times are simulated.
32 devices in a mesh: layer: 4 (over y, x), token: 4 (over z), fhalf: 2 (over core).
Axes of the slice: x: 2, y: 2, z: 4, core: 2. Of those that a mesh axis runs over, the one named last changes fastest.
Arguments:
- hidden_slab: bfloat16 [4096, 32768], P('token', ('layer', 'fhalf')), may hold values from -27 to 27, as said below
- current_block: float32 [32768, 64], P(('layer', 'fhalf')), may hold values from -6 to 6
- direction: float32 [32768, 64], P(('layer', 'fhalf')), may hold values from -3 to 3
Outputs:
- new_block: float32 [32768, 64], P(('layer', 'fhalf'))
- new_direction: float32 [32768, 64], P(('layer', 'fhalf'))
- ritz_values: float32 [64], replicated
Inputs may be any that keep to these rules, and one draw needn't show every extreme that they name: `hidden_slab`: hidden states of the joined layers.
All inputs are finite; a program needn't handle non-finite values.
Results may differ from a plain program's by a relative error of at most 0.0023.
The roundings to bfloat16 on the way count: a program that leaves them out, or rounds other values in their place, can miss the bound.
Values may be sent and summed in bfloat16 or wider, within the bound.
No kernel may reach another device: no remote copies, remote signals or barrier semaphores. Data moves between devices by JAX's collectives and lax.ppermute only.
A program may use at most 64 MiB of HBM per device.

v0:
```python
import jax
import jax.numpy as jnp
from jax import lax
from jax.experimental import pallas as pl
from jax.experimental.pallas import tpu as pltpu
from jax.sharding import PartitionSpec as P

NSUB = 6
SPREAD = 1e-4
LARGE = 1e30
HIGHEST = lax.Precision.HIGHEST


def exact_transposed(left, right):
    return lax.dot_general(
        left, right, (((0,), (0,)), ((), ())), precision=HIGHEST, preferred_element_type=jnp.float32
    )


def exact_rows(left, right):
    return lax.dot_general(
        left, right, (((1,), (1,)), ((), ())), precision=HIGHEST, preferred_element_type=jnp.float32
    )


def product(left, right):
    return jnp.dot(left, right, precision=HIGHEST, preferred_element_type=jnp.float32)


def identity(rows, columns):
    down = lax.broadcasted_iota(jnp.int32, (rows, columns), 0)
    across = lax.broadcasted_iota(jnp.int32, (rows, columns), 1)
    return jnp.where(down == across, 1.0, 0.0).astype(jnp.float32)


def factor_inverse(gram):
    size = gram.shape[0]
    wide = jnp.concatenate([gram, identity(size, size)], axis=1)
    tile = (8, 2 * size)
    rows = [wide[8 * g : 8 * g + 8] for g in range(size // 8)]
    sub = lax.broadcasted_iota(jnp.int32, tile, 0)
    done = []
    low = high = total = None
    for g in range(size // 8):
        live = rows[g:]
        panel = [[jnp.broadcast_to(r[:, 8 * g + j : 8 * g + j + 1], tile) for r in live] for j in range(8)]
        scale = None
        for j in range(8):
            head = panel[j][0]
            pivot = jnp.broadcast_to(head[j : j + 1], tile)
            inverse = 1.0 / pivot
            row = jnp.broadcast_to(live[0][j : j + 1], tile)
            factors = [value * inverse for value in panel[j]]
            factors[0] = jnp.where(sub > j, factors[0], 0.0)
            for i in range(j + 1, 8):
                other = jnp.broadcast_to(head[i : i + 1], tile)
                panel[i] = [value - f * other for value, f in zip(panel[i], factors)]
            live = [value - f * row for value, f in zip(live, factors)]
            scale = pivot if scale is None else jnp.where(sub >= j, pivot, scale)
            low = pivot if low is None else jnp.minimum(low, pivot)
            high = pivot if high is None else jnp.maximum(high, pivot)
            total = pivot if total is None else total + pivot
        rows[g:] = live
        done.append(live[0] * lax.rsqrt(scale))
    return jnp.concatenate(done, axis=0)[:, size:], low, high, total


def whiten_kernel(gram_ref, out_ref):
    cols = gram_ref.shape[0] // 3

    def block(i, j):
        return gram_ref[cols * i : cols * i + cols, cols * j : cols * j + cols]

    first = factor_inverse(block(0, 0))[0]
    lower_10 = exact_rows(block(1, 0), first)
    lower_20 = exact_rows(block(2, 0), first)
    second = factor_inverse(block(1, 1) - exact_rows(lower_10, lower_10))[0]
    lower_21 = exact_rows(block(2, 1) - exact_rows(lower_20, lower_10), second)
    third = factor_inverse(block(2, 2) - exact_rows(lower_20, lower_20) - exact_rows(lower_21, lower_21))[0]
    inverse_10 = -product(second, product(lower_10, first))
    inverse_20 = -product(third, product(lower_20, first) + product(lower_21, inverse_10))
    inverse_21 = -product(third, product(lower_21, second))
    zero = jnp.zeros((cols, cols), jnp.float32)
    out_ref[...] = jnp.concatenate(
        [
            jnp.concatenate([first, zero, zero], axis=1),
            jnp.concatenate([inverse_10, second, zero], axis=1),
            jnp.concatenate([inverse_20, inverse_21, third], axis=1),
        ],
        axis=0,
    )


def whiten_rows(gram_matrix):
    return pl.pallas_call(
        whiten_kernel, out_shape=jax.ShapeDtypeStruct(gram_matrix.shape, jnp.float32), name="whiten"
    )(gram_matrix)


def ritz_kernel(whiten_ref, raw_ref, coeffs_ref, values_ref, matrix_ref, power_ref, turned_ref, basis_ref):
    size, cols = turned_ref.shape
    power_ref[...] = product(whiten_ref[...], raw_ref[...])
    matrix_ref[...] = exact_rows(power_ref[...], whiten_ref[...])
    matrix_ref[...] = 0.5 * (matrix_ref[...] + matrix_ref[...].T)
    power_ref[...] = product(matrix_ref[...], matrix_ref[...])
    power_ref[...] = product(power_ref[...], matrix_ref[...])

    def sweep(step_ref, count):
        basis_ref[...] = identity(size, cols)

        def turn(_, good):
            turned_ref[...] = product(step_ref[...], basis_ref[...])
            turned = turned_ref[...]
            inverse, low, high, total = factor_inverse(exact_transposed(turned, turned))
            basis_ref[...] = exact_rows(turned_ref[...], inverse)
            fine = jnp.logical_and(low > SPREAD * high, total < LARGE)
            return jnp.minimum(good, jnp.where(fine, 1.0, 0.0))

        return lax.fori_loop(0, count, turn, jnp.ones((8, 2 * cols), jnp.float32))

    good = jnp.min(sweep(power_ref, NSUB // 3))

    @pl.when(good < 0.5)
    def _():
        sweep(matrix_ref, NSUB)

    values_ref[...] = jnp.sum(
        basis_ref[...] * product(matrix_ref[...], basis_ref[...]), axis=0, keepdims=True
    )
    down = lax.broadcasted_iota(jnp.int32, (size, cols), 0)
    coeffs_ref[:, :cols] = exact_transposed(whiten_ref[...], basis_ref[...])
    coeffs_ref[:, cols:] = exact_transposed(
        whiten_ref[...], jnp.where(down >= cols, basis_ref[...], 0.0)
    )


def ritz_of(whiten, ritz_raw):
    size = ritz_raw.shape[0]
    cols = size // 3
    return pl.pallas_call(
        ritz_kernel,
        out_shape=(
            jax.ShapeDtypeStruct((size, 2 * cols), jnp.float32),
            jax.ShapeDtypeStruct((1, cols), jnp.float32),
        ),
        scratch_shapes=[
            pltpu.VMEM((size, size), jnp.float32),
            pltpu.VMEM((size, size), jnp.float32),
            pltpu.VMEM((size, cols), jnp.float32),
            pltpu.VMEM((size, cols), jnp.float32),
        ],
        name="ritz",
    )(whiten, ritz_raw)


def rounded(value):
    return lax.reduce_precision(value, exponent_bits=8, mantissa_bits=7)


def swap(value, axis, step):
    return lax.ppermute(value, axis, [(i, i ^ step) for i in range(lax.axis_size(axis))])


def steps_of(axis):
    size = lax.axis_size(axis)
    if size & (size - 1):
        raise ValueError(axis)
    return [1 << bit for bit in range(size.bit_length() - 1)]


def reduce_all(value, axis):
    for step in steps_of(axis):
        value = value + swap(value, axis, step)
    return value


def side_of(axis, step):
    return (lax.axis_index(axis) // step) % 2


def reduce_halves(value, axis):
    for step in steps_of(axis):
        half = value.shape[1] // 2
        side = side_of(axis, step)
        kept = lax.dynamic_slice_in_dim(value, side * half, half, 1)
        sent = lax.dynamic_slice_in_dim(value, (1 - side) * half, half, 1)
        value = kept + swap(sent, axis, step)
    return value


def own_part(value, axis):
    for step in steps_of(axis):
        half = value.shape[1] // 2
        value = lax.dynamic_slice_in_dim(value, side_of(axis, step) * half, half, 1)
    return value


def gather_halves(value, axis):
    for step in reversed(steps_of(axis)):
        other = swap(value, axis, step)
        first = side_of(axis, step) == 0
        value = jnp.concatenate([jnp.where(first, value, other), jnp.where(first, other, value)], axis=1)
    return value


def local(hidden_slab, current_block, direction):
    tok_rows, half_width = hidden_slab.shape
    cols = current_block.shape[1]
    feat_total = half_width * lax.axis_size("layer") * lax.axis_size("fhalf")
    token_total = tok_rows * lax.axis_size("token")
    x_rows = current_block.T
    d_rows = direction.T
    start_b = jnp.concatenate([x_rows, d_rows], axis=0).astype(jnp.bfloat16)
    start_part = lax.dot_general(
        start_b, hidden_slab, (((1,), (1,)), ((), ())), preferred_element_type=jnp.float32
    )
    x_probe = reduce_all(reduce_halves(start_part[:cols], "fhalf"), "layer")
    x_probe_b = x_probe.astype(jnp.bfloat16)
    block_probe = gather_halves(x_probe_b, "fhalf")
    ritz_block = lax.dot_general(
        block_probe, block_probe, (((1,), (1,)), ((), ())), preferred_element_type=jnp.float32
    )
    ritz_block = reduce_all(ritz_block, "token") / (token_total * feat_total)
    image_part = jnp.dot(block_probe, hidden_slab, preferred_element_type=jnp.float32)
    image = reduce_halves(image_part, "token") / token_total
    x_own = own_part(x_rows, "token")
    d_own = own_part(d_rows, "token")
    residual = image - exact_transposed(ritz_block, x_own)
    residual_hi = rounded(residual)
    residual_b = residual_hi.astype(jnp.bfloat16)
    residual_lo = (residual - residual_hi).astype(jnp.bfloat16)
    search_b = gather_halves(residual_b, "token")
    search_lo = gather_halves(residual_lo, "token")
    d_probe = reduce_all(reduce_halves(start_part[cols:], "fhalf"), "layer")
    own = jnp.concatenate([x_own, residual, d_own], axis=0)
    gram_part = exact_rows(own, own)
    gram_matrix = reduce_all(reduce_all(gram_part, "layer"), "fhalf")
    gram_matrix = reduce_all(gram_matrix, "token") / feat_total
    whiten = whiten_rows(gram_matrix)
    r_part = lax.dot_general(
        search_b, hidden_slab, (((1,), (1,)), ((), ())), preferred_element_type=jnp.float32
    )
    r_probe = reduce_all(reduce_halves(r_part, "fhalf"), "layer")
    probes = jnp.concatenate([x_probe, r_probe, d_probe], axis=0)
    ritz_part = exact_rows(probes, rounded(probes))
    ritz_raw = reduce_all(reduce_all(ritz_part, "fhalf"), "token") / (token_total * feat_total)
    all_coeffs, ritz_values = ritz_of(whiten, ritz_raw)
    residual_rows = search_b.astype(jnp.float32) + search_lo.astype(jnp.float32)
    search_basis = jnp.concatenate([x_rows, residual_rows, d_rows], axis=0)
    moved = exact_transposed(all_coeffs, search_basis)
    return (moved[:cols].T, moved[cols:].T, ritz_values[0])


def solution(mesh):
    return jax.shard_map(
        local,
        mesh=mesh,
        in_specs=(
            P("token", ("layer", "fhalf")),
            P(("layer", "fhalf"), None),
            P(("layer", "fhalf"), None),
        ),
        out_specs=(P(("layer", "fhalf"), None), P(("layer", "fhalf"), None), P()),
        check_vma=False,
    )
```

profile of v0, /device:TPU:0, one launch (start us, length us, event | category | flops | bytes accessed | tf_op | source)
XLA Modules:
  0.0 140.0 jit_solution(7489366727262381910)
XLA Ops:
  0.6 1.7 %bitcast_convert_fusion = (bf16[64,4096]{1,0:T(8,128)(2,1)S(1)}, bf16[64,4096]{1,0:T(8,128)(2,1)S(1)}) fusion(f32[4096,64]{0,1:T(8,128)} %param.5, f32[4096,64]{0,1:T(8,128)} %param.4), kind=kLoop, calls=%fused_computation.73 | loop fusion | flops 524288 | bytes 3145728 | tf_op jit(solution)/shard_map/convert.1
  2.3 6.3 %fusion.6 = f32[128,1024]{1,0:T(8,128)S(1)} fusion(bf16[1024,4096]{1,0:T(8,128)(2,1)} %param.3, bf16[64,4096]{1,0:T(8,128)(2,1)S(1)} %get-tuple-element.28, bf16[64,4096]{1,0:T(8,128)(2,1)S(1)} %get-tuple-element.29), kind=kOutput, calls=%fused_computation.8 | convolution fusion | flops 1075838976 | bytes 9961472 | tf_op jit(solution)/shard_map/dot_general | solution.py:214
  8.7 0.5 collective-permute-start
  9.2 1.0 collective-permute-done
  10.2 2.9 %collective-permute-start.1 = (f32[64,512]{1,0:T(8,128)S(1)}, f32[64,512]{1,0:T(8,128)S(1)}, u32[]{:S(2)}, u32[]{:S(2)}) collective-permute-start(f32[64,512]{1,0:T(8,128)S(1)} %dynamic-slice_add_fusion.3), channel_id=1, source_target_pairs={{0,8},{8,0},{16,24},{24,16},{1,9},{9,1},{17,25},{25,17},{2,10},{10... | collective-permute-start | bytes 393224 | tf_op jit(solution)/shard_map/ppermute | solution.py:161
  13.1 3.8 %collective-permute-done.1 = f32[64,512]{1,0:T(8,128)S(1)} collective-permute-done((f32[64,512]{1,0:T(8,128)S(1)}, f32[64,512]{1,0:T(8,128)S(1)}, u32[]{:S(2)}, u32[]{:S(2)}) %collective-permute-start.1) | collective-permute-done | bytes 131104 | tf_op jit(solution)/shard_map/ppermute | solution.py:161
  16.9 1.8 %collective-permute-start.2 = (f32[64,512]{1,0:T(8,128)S(1)}, f32[64,512]{1,0:T(8,128)S(1)}, u32[]{:S(2)}, u32[]{:S(2)}) collective-permute-start(f32[64,512]{1,0:T(8,128)S(1)} %add.131), channel_id=1, source_target_pairs={{0,16},{8,24},{16,0},{24,8},{1,17},{9,25},{17,1},{25,9},{2,18},{10... | collective-permute-start | bytes 393224 | tf_op jit(solution)/shard_map/ppermute | solution.py:161
  18.8 3.3 %collective-permute-done.2 = f32[64,512]{1,0:T(8,128)S(1)} collective-permute-done((f32[64,512]{1,0:T(8,128)S(1)}, f32[64,512]{1,0:T(8,128)S(1)}, u32[]{:S(2)}, u32[]{:S(2)}) %collective-permute-start.2) | collective-permute-done | bytes 131104 | tf_op jit(solution)/shard_map/ppermute | solution.py:161
  22.0 0.7 fusion.43
  22.7 1.3 collective-permute-done.3
  24.0 4.9 %fusion.30 = f32[64,4096]{1,0:T(8,128)S(1)} fusion(bf16[1024,4096]{1,0:T(8,128)(2,1)} %param.3, bf16[64,512]{1,0:T(8,128)(2,1)S(1)} %get-tuple-element.24, bf16[64,512]{1,0:T(8,128)(2,1)S(1)} %get-tuple-element.23), kind=kOutput, calls=%fused_computation.54 | convolution fusion | flops 537133056 | bytes 9568256 | tf_op jit(solution)/shard_map/dot_general | solution.py:224
  28.9 0.0 copy-start
  28.9 0.0 copy-start.1
  29.0 0.8 constant_dynamic-slice_fusion.3
  29.8 1.8 %collective-permute-start.4 = (f32[64,2048]{1,0:T(8,128)}, f32[64,2048]{1,0:T(8,128)}, u32[]{:S(2)}, u32[]{:S(2)}) collective-permute-start(f32[64,2048]{1,0:T(8,128)} %constant_dynamic-slice_fusion.3), channel_id=1, source_target_pairs={{0,2},{2,0},{4,6},{6,4},{1,3},{3,1},{5,7},{7,5},{8,10},{10,8},{12,... | collective-permute-start | bytes 1572872 | tf_op jit(solution)/shard_map/ppermute | solution.py:161
  31.6 12.6 %collective-permute-done.4 = f32[64,2048]{1,0:T(8,128)} collective-permute-done((f32[64,2048]{1,0:T(8,128)}, f32[64,2048]{1,0:T(8,128)}, u32[]{:S(2)}, u32[]{:S(2)}) %collective-permute-start.4) | collective-permute-done | bytes 524320 | tf_op jit(solution)/shard_map/ppermute | solution.py:161
  44.1 1.1 dynamic-slice_add_fusion
  45.2 0.8 copy-done.2
  46.0 2.8 %collective-permute-start.5 = (f32[64,1024]{1,0:T(8,128)S(1)}, f32[64,1024]{1,0:T(8,128)S(1)}, u32[]{:S(2)}, u32[]{:S(2)}) collective-permute-start(f32[64,1024]{1,0:T(8,128)S(1)} %constant_dynamic-slice_fusion.2), channel_id=1, source_target_pairs={{0,4},{2,6},{4,0},{6,2},{1,5},{3,7},{5,1},{7,3},{8,12},{10,14},{12... | collective-permute-start | bytes 786440 | tf_op jit(solution)/shard_map/ppermute | solution.py:161
  48.9 0.2 fusion.29
  49.0 1.6 %collective-permute-start.6 = (f32[64,64]{1,0:T(8,128)S(1)}, f32[64,64]{1,0:T(8,128)S(1)}, u32[]{:S(2)}, u32[]{:S(2)}) collective-permute-start(f32[64,64]{1,0:T(8,128)S(1)} %fusion.29), channel_id=1, source_target_pairs={{0,2},{2,0},{4,6},{6,4},{1,3},{3,1},{5,7},{7,5},{8,10},{10,8},{12,... | collective-permute-start | bytes 49160 | tf_op jit(solution)/shard_map/ppermute | solution.py:161
  50.7 4.0 %collective-permute-done.6 = f32[64,64]{1,0:T(8,128)S(1)} collective-permute-done((f32[64,64]{1,0:T(8,128)S(1)}, f32[64,64]{1,0:T(8,128)S(1)}, u32[]{:S(2)}, u32[]{:S(2)}) %collective-permute-start.6) | collective-permute-done | bytes 16416 | tf_op jit(solution)/shard_map/ppermute | solution.py:161
  54.7 2.4 %collective-permute-start.7 = (f32[64,64]{1,0:T(8,128)S(1)}, f32[64,64]{1,0:T(8,128)S(1)}, u32[]{:S(2)}, u32[]{:S(2)}) collective-permute-start(f32[64,64]{1,0:T(8,128)S(1)} %add.137), channel_id=1, source_target_pairs={{0,4},{2,6},{4,0},{6,2},{1,5},{3,7},{5,1},{7,3},{8,12},{10,14},{12... | collective-permute-start | bytes 49160 | tf_op jit(solution)/shard_map/ppermute | solution.py:161
  57.0 4.6 %collective-permute-done.7 = f32[64,64]{1,0:T(8,128)S(1)} collective-permute-done((f32[64,64]{1,0:T(8,128)S(1)}, f32[64,64]{1,0:T(8,128)S(1)}, u32[]{:S(2)}, u32[]{:S(2)}) %collective-permute-start.7) | collective-permute-done | bytes 16416 | tf_op jit(solution)/shard_map/ppermute | solution.py:161
  61.7 1.5 %fusion.24 = (bf16[64,1024]{1,0:T(8,128)(2,1)S(1)}, bf16[64,1024]{1,0:T(8,128)(2,1)S(1)}, f32[64,1024]{1,0:T(8,128)S(1)}) fusion(f32[4096,64]{0,1:T(8,128)S(1)} %copy-done, s32[]{:T(128)S(6)} %add.126, f32[64,64]{1,0:T(8,128)S(1)} %add.137, f32[64,64]{1,0:T(8,128)S(1)} %collective-permute-done.7, f32[64,1024]{1,0:T(8,128)S(1)} %collective-permute-done.5, ...), kind=kOutput, calls=%fused_computation.31 | convolution fusion | flops 50798592 | bytes 1376264 | tf_op jit(solution)/shard_map/dot_general | solution.py:15
  63.2 0.3 collective-permute-start.13
  63.5 0.7 constant_dynamic-slice_fusion
  64.2 0.2 dynamic-slice_bitcast_fusion
  64.4 7.5 %collective-permute-done.13 = bf16[64,1024]{1,0:T(8,128)(2,1)S(1)} collective-permute-done((bf16[64,1024]{1,0:T(8,128)(2,1)S(1)}, bf16[64,1024]{1,0:T(8,128)(2,1)S(1)}, u32[]{:S(2)}, u32[]{:S(2)}) %collective-permute-start.13) | collective-permute-done | bytes 131104 | tf_op jit(solution)/shard_map/ppermute | solution.py:161
  71.9 0.1 collective-permute-start.14
  72.0 0.8 fusion.10
  72.8 1.6 %collective-permute-start.8 = (f32[192,192]{1,0:T(8,128)S(1)}, f32[192,192]{1,0:T(8,128)S(1)}, u32[]{:S(2)}, u32[]{:S(2)}) collective-permute-start(f32[192,192]{1,0:T(8,128)S(1)} %fusion.10), channel_id=1, source_target_pairs={{0,8},{8,0},{16,24},{24,16},{1,9},{9,1},{17,25},{25,17},{2,10},{10... | collective-permute-start | bytes 442376 | tf_op jit(solution)/shard_map/ppermute | solution.py:161
  74.4 0.6 collective-permute-start.19
  75.0 1.7 %collective-permute-start.24 = (bf16[64,1024]{1,0:T(8,128)(2,1)S(1)}, bf16[64,1024]{1,0:T(8,128)(2,1)S(1)}, u32[]{:S(2)}, u32[]{:S(2)}) collective-permute-start(bf16[64,1024]{1,0:T(8,128)(2,1)S(1)} %get-tuple-element.19), channel_id=1, source_target_pairs={{0,4},{2,6},{4,0},{6,2},{1,5},{3,7},{5,1},{7,3},{8,12},{10,14},{12... | collective-permute-start | bytes 393224 | tf_op jit(solution)/shard_map/ppermute | solution.py:161
  76.8 2.7 %collective-permute-done.8 = f32[192,192]{1,0:T(8,128)S(1)} collective-permute-done((f32[192,192]{1,0:T(8,128)S(1)}, f32[192,192]{1,0:T(8,128)S(1)}, u32[]{:S(2)}, u32[]{:S(2)}) %collective-permute-start.8) | collective-permute-done | bytes 147488 | tf_op jit(solution)/shard_map/ppermute | solution.py:161
  79.5 1.6 %collective-permute-start.9 = (f32[192,192]{1,0:T(8,128)S(1)}, f32[192,192]{1,0:T(8,128)S(1)}, u32[]{:S(2)}, u32[]{:S(2)}) collective-permute-start(f32[192,192]{1,0:T(8,128)S(1)} %add.139), channel_id=1, source_target_pairs={{0,16},{8,24},{16,0},{24,8},{1,17},{9,25},{17,1},{25,9},{2,18},{10... | collective-permute-start | bytes 442376 | tf_op jit(solution)/shard_map/ppermute | solution.py:161
  81.1 0.1 broadcast_select_fusion.3
  81.2 6.1 %fusion.23 = f32[64,1024]{1,0:T(8,128)S(1)} fusion(bf16[1024,4096]{1,0:T(8,128)(2,1)} %param.3, bf16[64,2048]{1,0:T(8,128)(2,1)S(1)} %get-tuple-element.14, bf16[64,2048]{1,0:T(8,128)(2,1)S(1)} %get-tuple-element.13), kind=kOutput, calls=%fused_computation.30 | convolution fusion | flops 537919488 | bytes 9175040 | tf_op jit(solution)/shard_map/dot_general | solution.py:240
  87.3 0.1 collective-permute-start.15
  87.4 0.6 collective-permute-start.10
  88.0 0.7 collective-permute-done.15
  88.7 1.6 %collective-permute-start.16 = (f32[64,512]{1,0:T(8,128)S(1)}, f32[64,512]{1,0:T(8,128)S(1)}, u32[]{:S(2)}, u32[]{:S(2)}) collective-permute-start(f32[64,512]{1,0:T(8,128)S(1)} %dynamic-slice_add_fusion.2), channel_id=1, source_target_pairs={{0,8},{8,0},{16,24},{24,16},{1,9},{9,1},{17,25},{25,17},{2,10},{10... | collective-permute-start | bytes 393224 | tf_op jit(solution)/shard_map/ppermute | solution.py:161
  90.3 1.2 collective-permute-start.25
  91.5 0.6 collective-permute-start.20
  92.0 2.3 %collective-permute-done.16 = f32[64,512]{1,0:T(8,128)S(1)} collective-permute-done((f32[64,512]{1,0:T(8,128)S(1)}, f32[64,512]{1,0:T(8,128)S(1)}, u32[]{:S(2)}, u32[]{:S(2)}) %collective-permute-start.16) | collective-permute-done | bytes 131104 | tf_op jit(solution)/shard_map/ppermute | solution.py:161
  94.3 0.6 collective-permute-start.17
  94.9 1.8 %collective-permute-done.20 = f32[64,512]{1,0:T(8,128)S(1)} collective-permute-done((f32[64,512]{1,0:T(8,128)S(1)}, f32[64,512]{1,0:T(8,128)S(1)}, u32[]{:S(2)}, u32[]{:S(2)}) %collective-permute-start.20) | collective-permute-done | bytes 131104 | tf_op jit(solution)/shard_map/ppermute | solution.py:161
  96.8 0.8 collective-permute-start.11
  97.6 1.8 %collective-permute-done.17 = f32[64,512]{1,0:T(8,128)S(1)} collective-permute-done((f32[64,512]{1,0:T(8,128)S(1)}, f32[64,512]{1,0:T(8,128)S(1)}, u32[]{:S(2)}, u32[]{:S(2)}) %collective-permute-start.17) | collective-permute-done | bytes 131104 | tf_op jit(solution)/shard_map/ppermute | solution.py:161
  99.4 0.5 fusion.16
  99.9 0.1 collective-permute-start.21
  100.0 0.1 broadcast_select_fusion.1
  100.1 2.5 %collective-permute-done.11 = f32[192,192]{1,0:T(8,128)S(1)} collective-permute-done((f32[192,192]{1,0:T(8,128)S(1)}, f32[192,192]{1,0:T(8,128)S(1)}, u32[]{:S(2)}, u32[]{:S(2)}) %collective-permute-start.11) | collective-permute-done | bytes 147488 | tf_op jit(solution)/shard_map/ppermute | solution.py:161
  102.7 2.3 %collective-permute-start.12 = (f32[192,192]{1,0:T(8,128)S(1)}, f32[192,192]{1,0:T(8,128)S(1)}, u32[]{:S(2)}, u32[]{:S(2)}) collective-permute-start(f32[192,192]{1,0:T(8,128)S(1)} %add.142), channel_id=1, source_target_pairs={{0,4},{2,6},{4,0},{6,2},{1,5},{3,7},{5,1},{7,3},{8,12},{10,14},{12... | collective-permute-start | bytes 442376 | tf_op jit(solution)/shard_map/ppermute | solution.py:161
  105.0 1.6 %collective-permute-start.22 = (f32[192,192]{1,0:T(8,128)S(1)}, f32[192,192]{1,0:T(8,128)S(1)}, u32[]{:S(2)}, u32[]{:S(2)}) collective-permute-start(f32[192,192]{1,0:T(8,128)S(1)} %add.150), channel_id=1, source_target_pairs={{0,2},{2,0},{4,6},{6,4},{1,3},{3,1},{5,7},{7,5},{8,10},{10,8},{12,... | collective-permute-start | bytes 442376 | tf_op jit(solution)/shard_map/ppermute | solution.py:161
  106.6 0.1 convert_add_fusion
  106.7 8.6 %collective-permute-done.22 = f32[192,192]{1,0:T(8,128)S(1)} collective-permute-done((f32[192,192]{1,0:T(8,128)S(1)}, f32[192,192]{1,0:T(8,128)S(1)}, u32[]{:S(2)}, u32[]{:S(2)}) %collective-permute-start.22) | collective-permute-done | bytes 147488 | tf_op jit(solution)/shard_map/ppermute | solution.py:161
  115.4 0.1 collective-permute-start.23
  115.4 0.7 add_multiply_fusion.1.gram_ref
  116.2 8.8 %whiten.1.whiten_ref = f32[192,192]{1,0:T(8,128)} custom-call(f32[192,192]{1,0:T(8,128)} %add_multiply_fusion.1.gram_ref), custom_call_target="tpu_custom_call" | custom-call | tf_op jit(solution)/shard_map/whiten/pallas_call | solution.py:95
  125.0 0.7 add_multiply_fusion.raw_ref
  125.7 9.9 %ritz.1 = (f32[192,128]{1,0:T(8,128)}, f32[1,64]{1,0:T(1,128)}) custom-call(f32[192,192]{1,0:T(8,128)} %whiten.1.whiten_ref, f32[192,192]{1,0:T(8,128)} %add_multiply_fusion.raw_ref), custom_call_target="tpu_custom_call" | custom-call | tf_op jit(solution)/shard_map/ritz/pallas_call | solution.py:140
  135.6 2.9 %fusion = f32[128,4096]{1,0:T(8,128)S(1)} fusion(f32[192,128]{1,0:T(8,128)} %get-tuple-element.5, f32[64,4096]{1,0:T(8,128)S(1)} %bitcast.18, f32[64,4096]{1,0:T(8,128)S(1)} %convert_add_fusion, f32[64,4096]{1,0:T(8,128)S(1)} %bitcast.17), kind=kOutput, calls=%fused_computation | convolution fusion | flops 1209532416 | bytes 5341184 | tf_op jit(solution)/shard_map/dot_general | solution.py:15
  138.5 1.5 %slice_bitcast_fusion = (f32[4096,64]{0,1:T(8,128)}, f32[4096,64]{0,1:T(8,128)}) fusion(f32[128,4096]{1,0:T(8,128)S(1)} %fusion), kind=kLoop, calls=%fused_computation.6 | loop fusion | bytes 4194304 | tf_op jit(solution)/shard_map/transpose | solution.py:251
  (42 shorter events, 0.5 us)
Async XLA Ops:
  8.7 1.5 %collective-permute-start = (f32[64,512]{1,0:T(8,128)S(1)}, f32[64,512]{1,0:T(8,128)S(1)}, u32[]{:S(2)}, u32[]{:S(2)}) collective-permute-start(f32[64,512]{1,0:T(8,128)S(1)} %constant_dynamic-slice_fusion.4), channel_id=1, source_target_pairs={{0,1},{1,0},{2,3},{3,2},{4,5},{5,4},{6,7},{7,6},{8,9},{9,8},{10,11... | collective-permute-start | bytes 393224 | tf_op jit(solution)/shard_map/ppermute | solution.py:161
  10.2 6.7 %collective-permute-start.1 = (f32[64,512]{1,0:T(8,128)S(1)}, f32[64,512]{1,0:T(8,128)S(1)}, u32[]{:S(2)}, u32[]{:S(2)}) collective-permute-start(f32[64,512]{1,0:T(8,128)S(1)} %dynamic-slice_add_fusion.3), channel_id=1, source_target_pairs={{0,8},{8,0},{16,24},{24,16},{1,9},{9,1},{17,25},{25,17},{2,10},{10... | collective-permute-start | bytes 393224 | tf_op jit(solution)/shard_map/ppermute | solution.py:161
  16.9 5.1 %collective-permute-start.2 = (f32[64,512]{1,0:T(8,128)S(1)}, f32[64,512]{1,0:T(8,128)S(1)}, u32[]{:S(2)}, u32[]{:S(2)}) collective-permute-start(f32[64,512]{1,0:T(8,128)S(1)} %add.131), channel_id=1, source_target_pairs={{0,16},{8,24},{16,0},{24,8},{1,17},{9,25},{17,1},{25,9},{2,18},{10... | collective-permute-start | bytes 393224 | tf_op jit(solution)/shard_map/ppermute | solution.py:161
  22.7 1.3 collective-permute-start.3
  28.9 32.7 %copy-start = (f32[4096,64]{0,1:T(8,128)S(1)}, f32[4096,64]{0,1:T(8,128)}, u32[]{:S(2)}) copy-start(f32[4096,64]{0,1:T(8,128)} %param.4) | copy-start | bytes 3145732
  28.9 35.2 %copy-start.1 = (f32[4096,64]{0,1:T(8,128)S(1)}, f32[4096,64]{0,1:T(8,128)}, u32[]{:S(2)}) copy-start(f32[4096,64]{0,1:T(8,128)} %param.5) | copy-start | bytes 3145732
  29.8 14.3 %collective-permute-start.4 = (f32[64,2048]{1,0:T(8,128)}, f32[64,2048]{1,0:T(8,128)}, u32[]{:S(2)}, u32[]{:S(2)}) collective-permute-start(f32[64,2048]{1,0:T(8,128)} %constant_dynamic-slice_fusion.3), channel_id=1, source_target_pairs={{0,2},{2,0},{4,6},{6,4},{1,3},{3,1},{5,7},{7,5},{8,10},{10,8},{12,... | collective-permute-start | bytes 1572872 | tf_op jit(solution)/shard_map/ppermute | solution.py:161
  45.2 0.8 copy-start.2
  46.0 15.6 %collective-permute-start.5 = (f32[64,1024]{1,0:T(8,128)S(1)}, f32[64,1024]{1,0:T(8,128)S(1)}, u32[]{:S(2)}, u32[]{:S(2)}) collective-permute-start(f32[64,1024]{1,0:T(8,128)S(1)} %constant_dynamic-slice_fusion.2), channel_id=1, source_target_pairs={{0,4},{2,6},{4,0},{6,2},{1,5},{3,7},{5,1},{7,3},{8,12},{10,14},{12... | collective-permute-start | bytes 786440 | tf_op jit(solution)/shard_map/ppermute | solution.py:161
  49.0 5.6 %collective-permute-start.6 = (f32[64,64]{1,0:T(8,128)S(1)}, f32[64,64]{1,0:T(8,128)S(1)}, u32[]{:S(2)}, u32[]{:S(2)}) collective-permute-start(f32[64,64]{1,0:T(8,128)S(1)} %fusion.29), channel_id=1, source_target_pairs={{0,2},{2,0},{4,6},{6,4},{1,3},{3,1},{5,7},{7,5},{8,10},{10,8},{12,... | collective-permute-start | bytes 49160 | tf_op jit(solution)/shard_map/ppermute | solution.py:161
  54.7 7.0 %collective-permute-start.7 = (f32[64,64]{1,0:T(8,128)S(1)}, f32[64,64]{1,0:T(8,128)S(1)}, u32[]{:S(2)}, u32[]{:S(2)}) collective-permute-start(f32[64,64]{1,0:T(8,128)S(1)} %add.137), channel_id=1, source_target_pairs={{0,4},{2,6},{4,0},{6,2},{1,5},{3,7},{5,1},{7,3},{8,12},{10,14},{12... | collective-permute-start | bytes 49160 | tf_op jit(solution)/shard_map/ppermute | solution.py:161
  63.2 8.7 %collective-permute-start.13 = (bf16[64,1024]{1,0:T(8,128)(2,1)S(1)}, bf16[64,1024]{1,0:T(8,128)(2,1)S(1)}, u32[]{:S(2)}, u32[]{:S(2)}) collective-permute-start(bf16[64,1024]{1,0:T(8,128)(2,1)S(1)} %get-tuple-element.20), channel_id=1, source_target_pairs={{0,4},{2,6},{4,0},{6,2},{1,5},{3,7},{5,1},{7,3},{8,12},{10,14},{12... | collective-permute-start | bytes 393224 | tf_op jit(solution)/shard_map/ppermute | solution.py:161
  64.2 10.2 %collective-permute-start.18 = (f32[64,512]{1,0:T(8,128)}, f32[64,512]{1,0:T(8,128)S(1)}, u32[]{:S(2)}, u32[]{:S(2)}) collective-permute-start(f32[64,512]{1,0:T(8,128)} %constant_dynamic-slice_fusion), channel_id=1, source_target_pairs={{0,1},{1,0},{2,3},{3,2},{4,5},{5,4},{6,7},{7,6},{8,9},{9,8},{10,11... | collective-permute-start | bytes 393224 | tf_op jit(solution)/shard_map/ppermute | solution.py:161
  71.9 9.1 %collective-permute-start.14 = (bf16[64,2048]{1,0:T(8,128)(2,1)S(1)}, bf16[64,2048]{1,0:T(8,128)(2,1)S(1)}, u32[]{:S(2)}, u32[]{:S(2)}) collective-permute-start(bf16[64,2048]{1,0:T(8,128)(2,1)S(1)} %pad_maximum_fusion.2), channel_id=1, source_target_pairs={{0,2},{2,0},{4,6},{6,4},{1,3},{3,1},{5,7},{7,5},{8,10},{10,8},{12,... | collective-permute-start | bytes 786440 | tf_op jit(solution)/shard_map/ppermute | solution.py:161
  72.8 6.6 %collective-permute-start.8 = (f32[192,192]{1,0:T(8,128)S(1)}, f32[192,192]{1,0:T(8,128)S(1)}, u32[]{:S(2)}, u32[]{:S(2)}) collective-permute-start(f32[192,192]{1,0:T(8,128)S(1)} %fusion.10), channel_id=1, source_target_pairs={{0,8},{8,0},{16,24},{24,16},{1,9},{9,1},{17,25},{25,17},{2,10},{10... | collective-permute-start | bytes 442376 | tf_op jit(solution)/shard_map/ppermute | solution.py:161
  74.4 17.0 %collective-permute-start.19 = (f32[64,512]{1,0:T(8,128)S(1)}, f32[64,512]{1,0:T(8,128)S(1)}, u32[]{:S(2)}, u32[]{:S(2)}) collective-permute-start(f32[64,512]{1,0:T(8,128)S(1)} %dynamic-slice_add_fusion.1), channel_id=1, source_target_pairs={{0,8},{8,0},{16,24},{24,16},{1,9},{9,1},{17,25},{25,17},{2,10},{10... | collective-permute-start | bytes 393224 | tf_op jit(solution)/shard_map/ppermute | solution.py:161
  75.0 12.3 %collective-permute-start.24 = (bf16[64,1024]{1,0:T(8,128)(2,1)S(1)}, bf16[64,1024]{1,0:T(8,128)(2,1)S(1)}, u32[]{:S(2)}, u32[]{:S(2)}) collective-permute-start(bf16[64,1024]{1,0:T(8,128)(2,1)S(1)} %get-tuple-element.19), channel_id=1, source_target_pairs={{0,4},{2,6},{4,0},{6,2},{1,5},{3,7},{5,1},{7,3},{8,12},{10,14},{12... | collective-permute-start | bytes 393224 | tf_op jit(solution)/shard_map/ppermute | solution.py:161
  79.5 7.9 %collective-permute-start.9 = (f32[192,192]{1,0:T(8,128)S(1)}, f32[192,192]{1,0:T(8,128)S(1)}, u32[]{:S(2)}, u32[]{:S(2)}) collective-permute-start(f32[192,192]{1,0:T(8,128)S(1)} %add.139), channel_id=1, source_target_pairs={{0,16},{8,24},{16,0},{24,8},{1,17},{9,25},{17,1},{25,9},{2,18},{10... | collective-permute-start | bytes 442376 | tf_op jit(solution)/shard_map/ppermute | solution.py:161
  87.2 12.2 %copy-start.3 = (f32[64,512]{1,0:T(8,128)S(1)}, f32[64,512]{1,0:T(8,128)}, u32[]{:S(2)}) copy-start(f32[64,512]{1,0:T(8,128)} %get-tuple-element.8) | copy-start | bytes 393220
  87.3 1.4 %collective-permute-start.15 = (f32[64,512]{1,0:T(8,128)S(1)}, f32[64,512]{1,0:T(8,128)S(1)}, u32[]{:S(2)}, u32[]{:S(2)}) collective-permute-start(f32[64,512]{1,0:T(8,128)S(1)} %constant_dynamic-slice_fusion.1), channel_id=1, source_target_pairs={{0,1},{1,0},{2,3},{3,2},{4,5},{5,4},{6,7},{7,6},{8,9},{9,8},{10,11... | collective-permute-start | bytes 393224 | tf_op jit(solution)/shard_map/ppermute | solution.py:161
  87.4 9.3 %collective-permute-start.10 = (f32[192,192]{1,0:T(8,128)S(1)}, f32[192,192]{1,0:T(8,128)S(1)}, u32[]{:S(2)}, u32[]{:S(2)}) collective-permute-start(f32[192,192]{1,0:T(8,128)S(1)} %add.140), channel_id=1, source_target_pairs={{0,1},{1,0},{2,3},{3,2},{4,5},{5,4},{6,7},{7,6},{8,9},{9,8},{10,11... | collective-permute-start | bytes 442376 | tf_op jit(solution)/shard_map/ppermute | solution.py:161
  88.7 5.6 %collective-permute-start.16 = (f32[64,512]{1,0:T(8,128)S(1)}, f32[64,512]{1,0:T(8,128)S(1)}, u32[]{:S(2)}, u32[]{:S(2)}) collective-permute-start(f32[64,512]{1,0:T(8,128)S(1)} %dynamic-slice_add_fusion.2), channel_id=1, source_target_pairs={{0,8},{8,0},{16,24},{24,16},{1,9},{9,1},{17,25},{25,17},{2,10},{10... | collective-permute-start | bytes 393224 | tf_op jit(solution)/shard_map/ppermute | solution.py:161
  90.3 9.7 %collective-permute-start.25 = (bf16[64,2048]{1,0:T(8,128)(2,1)S(1)}, bf16[64,2048]{1,0:T(8,128)(2,1)S(1)}, u32[]{:S(2)}, u32[]{:S(2)}) collective-permute-start(bf16[64,2048]{1,0:T(8,128)(2,1)S(1)} %pad_maximum_fusion.3), channel_id=1, source_target_pairs={{0,2},{2,0},{4,6},{6,4},{1,3},{3,1},{5,7},{7,5},{8,10},{10,8},{12,... | collective-permute-start | bytes 786440 | tf_op jit(solution)/shard_map/ppermute | solution.py:161
  91.5 5.2 %collective-permute-start.20 = (f32[64,512]{1,0:T(8,128)S(1)}, f32[64,512]{1,0:T(8,128)S(1)}, u32[]{:S(2)}, u32[]{:S(2)}) collective-permute-start(f32[64,512]{1,0:T(8,128)S(1)} %add.148), channel_id=1, source_target_pairs={{0,16},{8,24},{16,0},{24,8},{1,17},{9,25},{17,1},{25,9},{2,18},{10... | collective-permute-start | bytes 393224 | tf_op jit(solution)/shard_map/ppermute | solution.py:161
  94.3 5.0 %collective-permute-start.17 = (f32[64,512]{1,0:T(8,128)S(1)}, f32[64,512]{1,0:T(8,128)S(1)}, u32[]{:S(2)}, u32[]{:S(2)}) collective-permute-start(f32[64,512]{1,0:T(8,128)S(1)} %add.145), channel_id=1, source_target_pairs={{0,16},{8,24},{16,0},{24,8},{1,17},{9,25},{17,1},{25,9},{2,18},{10... | collective-permute-start | bytes 393224 | tf_op jit(solution)/shard_map/ppermute | solution.py:161
  96.8 5.9 %collective-permute-start.11 = (f32[192,192]{1,0:T(8,128)S(1)}, f32[192,192]{1,0:T(8,128)S(1)}, u32[]{:S(2)}, u32[]{:S(2)}) collective-permute-start(f32[192,192]{1,0:T(8,128)S(1)} %add.141), channel_id=1, source_target_pairs={{0,2},{2,0},{4,6},{6,4},{1,3},{3,1},{5,7},{7,5},{8,10},{10,8},{12,... | collective-permute-start | bytes 442376 | tf_op jit(solution)/shard_map/ppermute | solution.py:161
  99.9 5.1 %collective-permute-start.21 = (f32[192,192]{1,0:T(8,128)S(1)}, f32[192,192]{1,0:T(8,128)S(1)}, u32[]{:S(2)}, u32[]{:S(2)}) collective-permute-start(f32[192,192]{1,0:T(8,128)S(1)} %fusion.16), channel_id=1, source_target_pairs={{0,1},{1,0},{2,3},{3,2},{4,5},{5,4},{6,7},{7,6},{8,9},{9,8},{10,11... | collective-permute-start | bytes 442376 | tf_op jit(solution)/shard_map/ppermute | solution.py:161
  102.7 12.8 %collective-permute-start.12 = (f32[192,192]{1,0:T(8,128)S(1)}, f32[192,192]{1,0:T(8,128)S(1)}, u32[]{:S(2)}, u32[]{:S(2)}) collective-permute-start(f32[192,192]{1,0:T(8,128)S(1)} %add.142), channel_id=1, source_target_pairs={{0,4},{2,6},{4,0},{6,2},{1,5},{3,7},{5,1},{7,3},{8,12},{10,14},{12... | collective-permute-start | bytes 442376 | tf_op jit(solution)/shard_map/ppermute | solution.py:161
  105.0 10.3 %collective-permute-start.22 = (f32[192,192]{1,0:T(8,128)S(1)}, f32[192,192]{1,0:T(8,128)S(1)}, u32[]{:S(2)}, u32[]{:S(2)}) collective-permute-start(f32[192,192]{1,0:T(8,128)S(1)} %add.150), channel_id=1, source_target_pairs={{0,2},{2,0},{4,6},{6,4},{1,3},{3,1},{5,7},{7,5},{8,10},{10,8},{12,... | collective-permute-start | bytes 442376 | tf_op jit(solution)/shard_map/ppermute | solution.py:161
  115.4 9.6 %collective-permute-start.23 = (f32[192,192]{1,0:T(8,128)S(1)}, f32[192,192]{1,0:T(8,128)S(1)}, u32[]{:S(2)}, u32[]{:S(2)}) collective-permute-start(f32[192,192]{1,0:T(8,128)S(1)} %add.151), channel_id=1, source_target_pairs={{0,4},{2,6},{4,0},{6,2},{1,5},{3,7},{5,1},{7,3},{8,12},{10,14},{12... | collective-permute-start | bytes 442376 | tf_op jit(solution)/shard_map/ppermute | solution.py:161
where the time goes:
time: 140 us
  waiting for transfers between devices  58.4 us (42%)
  starting transfers between devices  29.1 us (21%)
  matrix products  23.1 us (16%)
  Pallas kernels  18.7 us (13%)
  other arithmetic  5.56 us (4%)
  local copies, waits for them, and re-layouts  4.06 us (3%)
    ppermute x26, waiting for transfers between devices, swap(): lax.ppermute(value, axis, [(i, i ^ step) for i in range(lax.axis_size(axi...  58.4 us
    ppermute x26, starting transfers between devices, swap(): lax.ppermute(value, axis, [(i, i ^ step) for i in range(lax.axis_size(axi...  29.1 us
    pallas_call x1, Pallas kernels, ritz_of(): pl.pallas_call(ritz_kernel, out_shape=(jax.ShapeDtypeStruct((size, 2 * co...  9.89 us
    pallas_call x1, Pallas kernels, whiten_rows(): pl.pallas_call(whiten_kernel, out_shape=jax.ShapeDtypeStruct(gram_matrix....  8.85 us
    dot_general x1, matrix products, local(): lax.dot_general(start_b, hidden_slab, (((1,), (1,)), ((), ())), preferred...  6.26 us
    dot_general x1, matrix products, local(): lax.dot_general(search_b, hidden_slab, (((1,), (1,)), ((), ())), preferre...  6.05 us
    dot_general x1, matrix products, local(): jnp.dot(block_probe, hidden_slab, preferred_element_type=jnp.float32)  4.95 us
    dot_general x2, matrix products, exact_transposed(): lax.dot_general(left, right, (((0,), (0,)), ((), ())), precision=HIGHEST,...  4.36 us
  transfers between devices with their start and end apart: 26, of which 15 were waited for; matrix products, arithmetic and copies ran while one was open for 7% of the time, Pallas kernels for 6%

commit v1 on v0

--- a/solution.py
+++ b/solution.py
@@ -6,6 +6,7 @@
 from jax.sharding import PartitionSpec as P
 
 NSUB = 6
+CHUNKS = 2
 SPREAD = 1e-4
 LARGE = 1e30
 HIGHEST = lax.Precision.HIGHEST
@@ -65,41 +66,56 @@
     return jnp.concatenate(done, axis=0)[:, size:], low, high, total
 
 
-def whiten_kernel(gram_ref, out_ref):
-    cols = gram_ref.shape[0] // 3
-
-    def block(i, j):
-        return gram_ref[cols * i : cols * i + cols, cols * j : cols * j + cols]
-
-    first = factor_inverse(block(0, 0))[0]
-    lower_10 = exact_rows(block(1, 0), first)
-    lower_20 = exact_rows(block(2, 0), first)
-    second = factor_inverse(block(1, 1) - exact_rows(lower_10, lower_10))[0]
-    lower_21 = exact_rows(block(2, 1) - exact_rows(lower_20, lower_10), second)
-    third = factor_inverse(block(2, 2) - exact_rows(lower_20, lower_20) - exact_rows(lower_21, lower_21))[0]
-    inverse_10 = -product(second, product(lower_10, first))
-    inverse_20 = -product(third, product(lower_20, first) + product(lower_21, inverse_10))
-    inverse_21 = -product(third, product(lower_21, second))
-    zero = jnp.zeros((cols, cols), jnp.float32)
-    out_ref[...] = jnp.concatenate(
-        [
-            jnp.concatenate([first, zero, zero], axis=1),
-            jnp.concatenate([inverse_10, second, zero], axis=1),
-            jnp.concatenate([inverse_20, inverse_21, third], axis=1),
-        ],
-        axis=0,
-    )
-
-
-def whiten_rows(gram_matrix):
+def whiten_given_kernel(gram_ref, out_ref):
+    cols = gram_ref.shape[0] // 2
+    first = factor_inverse(gram_ref[:cols, :cols])[0]
+    lower = exact_rows(gram_ref[cols:, :cols], first)
+    second = factor_inverse(gram_ref[cols:, cols:] - exact_rows(lower, lower))[0]
+    out_ref[:cols, :cols] = first
+    out_ref[:cols, cols:] = jnp.zeros((cols, cols), jnp.float32)
+    out_ref[cols:, :cols] = -product(second, product(lower, first))
+    out_ref[cols:, cols:] = second
+
+
+def whiten_given(gram_matrix):
     return pl.pallas_call(
-        whiten_kernel, out_shape=jax.ShapeDtypeStruct(gram_matrix.shape, jnp.float32), name="whiten"
+        whiten_given_kernel,
+        out_shape=jax.ShapeDtypeStruct(gram_matrix.shape, jnp.float32),
+        cost_estimate=pl.CostEstimate(flops=4_000_000_000, transcendentals=0, bytes_accessed=131072),
+        name="whiten_given",
     )(gram_matrix)
 
 
-def ritz_kernel(whiten_ref, raw_ref, coeffs_ref, values_ref, matrix_ref, power_ref, turned_ref, basis_ref):
+def whiten_rest_kernel(given_ref, gram_ref, out_ref):
+    cols, size = gram_ref.shape
+    lower = exact_rows(gram_ref[:, : size - cols], given_ref[...])
+    last = factor_inverse(gram_ref[:, size - cols :] - exact_rows(lower, lower))[0]
+    out_ref[:, : size - cols] = -product(last, product(lower, given_ref[...]))
+    out_ref[:, size - cols :] = last
+
+
+def whiten_rest(given, gram_rows):
+    return pl.pallas_call(
+        whiten_rest_kernel,
+        out_shape=jax.ShapeDtypeStruct(gram_rows.shape, jnp.float32),
+        cost_estimate=pl.CostEstimate(flops=3_000_000_000, transcendentals=0, bytes_accessed=131072),
+        name="whiten_rest",
+    )(given, gram_rows)
+
+
+def ritz_kernel(
+    given_ref, rest_ref, raw_given_ref, raw_rest_ref, coeffs_ref, values_ref,
+    whiten_ref, matrix_ref, power_ref, turned_ref, basis_ref,
+):
     size, cols = turned_ref.shape
-    power_ref[...] = product(whiten_ref[...], raw_ref[...])
+    rest = size - cols
+    whiten_ref[:rest, :rest] = given_ref[...]
+    whiten_ref[:rest, rest:] = jnp.zeros((rest, cols), jnp.float32)
+    whiten_ref[rest:, :] = rest_ref[...]
+    matrix_ref[:rest, :rest] = 0.5 * (raw_given_ref[...] + raw_given_ref[...].T)
+    matrix_ref[rest:, :] = raw_rest_ref[...]
+    matrix_ref[:rest, rest:] = raw_rest_ref[:, :rest].T
+    power_ref[...] = product(whiten_ref[...], matrix_ref[...])
     matrix_ref[...] = exact_rows(power_ref[...], whiten_ref[...])
     matrix_ref[...] = 0.5 * (matrix_ref[...] + matrix_ref[...].T)
     power_ref[...] = product(matrix_ref[...], matrix_ref[...])
@@ -134,9 +150,8 @@
     )
 
 
-def ritz_of(whiten, ritz_raw):
-    size = ritz_raw.shape[0]
-    cols = size // 3
+def ritz_of(given, rest, raw_given, raw_rest):
+    cols, size = rest.shape
     return pl.pallas_call(
         ritz_kernel,
         out_shape=(
@@ -146,11 +161,13 @@
         scratch_shapes=[
             pltpu.VMEM((size, size), jnp.float32),
             pltpu.VMEM((size, size), jnp.float32),
+            pltpu.VMEM((size, size), jnp.float32),
             pltpu.VMEM((size, cols), jnp.float32),
             pltpu.VMEM((size, cols), jnp.float32),
         ],
+        cost_estimate=pl.CostEstimate(flops=10_000_000_000, transcendentals=0, bytes_accessed=524288),
         name="ritz",
-    )(whiten, ritz_raw)
+    )(given, rest, raw_given, raw_rest)
 
 
 def rounded(value):
@@ -169,6 +186,10 @@
 
 
 def reduce_all(value, axis):
+    size = lax.axis_size(axis)
+    if size == 4:
+        near, far, across = (swap(value, axis, step) for step in (1, 2, 3))
+        return (value + near) + (far + across)
     for step in steps_of(axis):
         value = value + swap(value, axis, step)
     return value
@@ -203,6 +224,12 @@
     return value
 
 
+def probe_of(rows_b, slab_part):
+    return lax.dot_general(
+        rows_b, slab_part, (((1,), (1,)), ((), ())), preferred_element_type=jnp.float32
+    )
+
+
 def local(hidden_slab, current_block, direction):
     tok_rows, half_width = hidden_slab.shape
     cols = current_block.shape[1]
@@ -210,45 +237,64 @@
     token_total = tok_rows * lax.axis_size("token")
     x_rows = current_block.T
     d_rows = direction.T
-    start_b = jnp.concatenate([x_rows, d_rows], axis=0).astype(jnp.bfloat16)
-    start_part = lax.dot_general(
-        start_b, hidden_slab, (((1,), (1,)), ((), ())), preferred_element_type=jnp.float32
-    )
-    x_probe = reduce_all(reduce_halves(start_part[:cols], "fhalf"), "layer")
-    x_probe_b = x_probe.astype(jnp.bfloat16)
-    block_probe = gather_halves(x_probe_b, "fhalf")
-    ritz_block = lax.dot_general(
-        block_probe, block_probe, (((1,), (1,)), ((), ())), preferred_element_type=jnp.float32
-    )
-    ritz_block = reduce_all(ritz_block, "token") / (token_total * feat_total)
-    image_part = jnp.dot(block_probe, hidden_slab, preferred_element_type=jnp.float32)
-    image = reduce_halves(image_part, "token") / token_total
-    x_own = own_part(x_rows, "token")
-    d_own = own_part(d_rows, "token")
-    residual = image - exact_transposed(ritz_block, x_own)
-    residual_hi = rounded(residual)
-    residual_b = residual_hi.astype(jnp.bfloat16)
-    residual_lo = (residual - residual_hi).astype(jnp.bfloat16)
-    search_b = gather_halves(residual_b, "token")
-    search_lo = gather_halves(residual_lo, "token")
-    d_probe = reduce_all(reduce_halves(start_part[cols:], "fhalf"), "layer")
-    own = jnp.concatenate([x_own, residual, d_own], axis=0)
-    gram_part = exact_rows(own, own)
-    gram_matrix = reduce_all(reduce_all(gram_part, "layer"), "fhalf")
-    gram_matrix = reduce_all(gram_matrix, "token") / feat_total
-    whiten = whiten_rows(gram_matrix)
-    r_part = lax.dot_general(
-        search_b, hidden_slab, (((1,), (1,)), ((), ())), preferred_element_type=jnp.float32
-    )
+    given_rows = jnp.concatenate([x_rows, d_rows], axis=0)
+    chunk = half_width // CHUNKS
+    slabs = [hidden_slab[:, chunk * c : chunk * c + chunk] for c in range(CHUNKS)]
+    given_part = probe_of(given_rows.astype(jnp.bfloat16), hidden_slab)
+    x_probe = reduce_all(reduce_halves(given_part[:cols], "fhalf"), "layer")
+    x_probe_b = rounded(x_probe)
+    block_probe = gather_halves(x_probe_b.astype(jnp.bfloat16), "fhalf")
+    ritz_block = reduce_all(probe_of(block_probe, block_probe), "token") / (token_total * feat_total)
+    images = [
+        reduce_halves(jnp.dot(block_probe, slab, preferred_element_type=jnp.float32), "token")
+        for slab in slabs
+    ]
+    given_own = [
+        own_part(given_rows[:, chunk * c : chunk * c + chunk], "token") for c in range(CHUNKS)
+    ]
+    residuals = [
+        image / token_total - exact_transposed(ritz_block, own[:cols])
+        for image, own in zip(images, given_own)
+    ]
+    highs = [rounded(residual) for residual in residuals]
+    search = [gather_halves(high.astype(jnp.bfloat16), "token") for high in highs]
+    r_part = sum(probe_of(rows, slab) for rows, slab in zip(search, slabs))
     r_probe = reduce_all(reduce_halves(r_part, "fhalf"), "layer")
-    probes = jnp.concatenate([x_probe, r_probe, d_probe], axis=0)
-    ritz_part = exact_rows(probes, rounded(probes))
-    ritz_raw = reduce_all(reduce_all(ritz_part, "fhalf"), "token") / (token_total * feat_total)
-    all_coeffs, ritz_values = ritz_of(whiten, ritz_raw)
-    residual_rows = search_b.astype(jnp.float32) + search_lo.astype(jnp.float32)
-    search_basis = jnp.concatenate([x_rows, residual_rows, d_rows], axis=0)
-    moved = exact_transposed(all_coeffs, search_basis)
-    return (moved[:cols].T, moved[cols:].T, ritz_values[0])
+    d_half = reduce_halves(given_part[cols:], "fhalf")
+    d_probe = reduce_all(d_half, "layer")
+    gram_given = reduce_all(reduce_all(exact_rows(given_rows, given_rows), "fhalf"), "layer")
+    given_inverse = whiten_given(gram_given / feat_total)
+    given_probe = jnp.concatenate([x_probe, d_probe], axis=0)
+    given_probe_b = jnp.concatenate([x_probe_b, rounded(d_probe)], axis=0)
+    raw_given = exact_rows(given_probe, given_probe_b)
+    raw_given = reduce_all(reduce_all(raw_given, "fhalf"), "token") / (token_total * feat_total)
+    gram_rest = sum(
+        exact_rows(residual, jnp.concatenate([own, residual], axis=0))
+        for residual, own in zip(residuals, given_own)
+    )
+    gram_rest = reduce_all(reduce_all(reduce_all(gram_rest, "fhalf"), "layer"), "token")
+    rest_inverse = whiten_rest(given_inverse, gram_rest / feat_total)
+    r_probe_b = rounded(r_probe)
+    raw_rest = jnp.concatenate(
+        [
+            0.5 * (exact_rows(r_probe, given_probe_b) + exact_rows(r_probe_b, given_probe)),
+            exact_rows(r_probe, r_probe_b),
+        ],
+        axis=1,
+    )
+    raw_rest = reduce_all(reduce_all(raw_rest, "fhalf"), "token") / (token_total * feat_total)
+    all_coeffs, ritz_values = ritz_of(given_inverse, rest_inverse, raw_given, raw_rest)
+    lows = [
+        gather_halves((residual - high).astype(jnp.bfloat16), "token")
+        for residual, high in zip(residuals, highs)
+    ]
+    residual_rows = jnp.concatenate(
+        [high.astype(jnp.float32) + low.astype(jnp.float32) for high, low in zip(search, lows)], axis=1
+    )
+    search_basis = jnp.concatenate([given_rows, residual_rows], axis=0)
+    new_block = exact_transposed(all_coeffs[:, :cols], search_basis)
+    new_direction = exact_transposed(all_coeffs[:, cols:], search_basis)
+    return (new_block.T, new_direction.T, ritz_values[0])
 
 
 def solution(mesh):

time: 140 us -> 165 us (1.18)
  starting transfers between devices: 29.1 us -> 49.9 us
  waiting for transfers between devices: 58.4 us -> 41.3 us
  matrix products: 23.1 us -> 33.3 us
  other arithmetic: 5.56 us -> 14.8 us
    ppermute x26 -> x47, starting transfers between devices: 29.1 us -> 49.9 us  [swap(): lax.ppermute(value, axis, [(i, i ^ step) for i in range(lax.axis_size(axi...]
    ppermute x26 -> x47, waiting for transfers between devices: 58.4 us -> 41.3 us  [swap(): lax.ppermute(value, axis, [(i, i ^ step) for i in range(lax.axis_size(axi...]
    dot_general x2 -> x4, matrix products: 4.36 us -> 7.96 us  [exact_transposed(): lax.dot_general(left, right, (((0,), (0,)), ((), ())), precision=HIGHEST,...]
    dot_general x2 -> x7, matrix products: 1.31 us -> 4.85 us  [exact_rows(): lax.dot_general(left, right, (((1,), (1,)), ((), ())), precision=HIGHEST,...]
    dot_general x4 -> x6, matrix products: 17.4 us -> 20.5 us  [the longest x4 14.4 us: probe_of(): lax.dot_general(rows_b, slab_part, (((1,), (1,)), ((), ())), preferred_el...]
    concatenate x2 -> x4, other arithmetic: 0.04 us -> 2.65 us  [gather_halves(): jnp.concatenate([jnp.where(first, value, other), jnp.where(first, other,...]
    concatenate x0 -> x3, other arithmetic: none -> 2.47 us  [the longest x2 2.46 us: local(): given_rows = jnp.concatenate([x_rows, d_rows], axis=0)]
    slice x1 -> x2, local copies, waits for them, and re-layouts: 0.04 us -> 1.94 us  [the longest x1 1.9 us: local(): given_rows[:, chunk * c:chunk * c + chunk]]
  transfers between devices with their start and end apart: 26 -> 47, of which waited for: 15 -> 17; matrix products, arithmetic and copies ran while one was open for 7% -> 22% of each run, Pallas kernels for 6% -> 6%
where the time goes in v1:
time: 165 us; the launch traced here: 164 us
  starting transfers between devices  49.9 us (30%)
  waiting for transfers between devices  41.3 us (25%)
  matrix products  33.3 us (20%)
  Pallas kernels  20.2 us (12%)
  other arithmetic  14.8 us (9%)
  local copies, waits for them, and re-layouts  3.47 us (2%)
    ppermute x47, starting transfers between devices, swap(): lax.ppermute(value, axis, [(i, i ^ step) for i in range(lax.axis_size(axi...  49.9 us
    ppermute x47, waiting for transfers between devices, swap(): lax.ppermute(value, axis, [(i, i ^ step) for i in range(lax.axis_size(axi...  41.3 us
    dot_general x4, matrix products, probe_of(): lax.dot_general(rows_b, slab_part, (((1,), (1,)), ((), ())), preferred_el...  14.4 us
    pallas_call x1, Pallas kernels, ritz_of(): pl.pallas_call(ritz_kernel, out_shape=(jax.ShapeDtypeStruct((size, 2 * co...  10.2 us
    dot_general x4, matrix products, exact_transposed(): lax.dot_general(left, right, (((0,), (0,)), ((), ())), precision=HIGHEST,...  7.96 us
    dot_general x2, matrix products, local(): jnp.dot(block_probe, slab, preferred_element_type=jnp.float32)  6.11 us
    pallas_call x1, Pallas kernels, whiten_given(): pl.pallas_call(whiten_given_kernel, out_shape=jax.ShapeDtypeStruct(gram_m...  6.03 us
    dot_general x7, matrix products, exact_rows(): lax.dot_general(left, right, (((1,), (1,)), ((), ())), precision=HIGHEST,...  4.85 us
  transfers between devices with their start and end apart: 47, of which 17 were waited for; matrix products, arithmetic and copies ran while one was open for 22% of the time, Pallas kernels for 6%

profile of v1, /device:TPU:0, one launch (start us, length us, event | category | flops | bytes accessed | tf_op | source)
XLA Modules:
  0.0 164.1 jit_solution(11848122900099211239)
XLA Ops:
  0.7 7.1 %fusion.16 = f32[128,1024]{1,0:T(8,128)S(1)} fusion(bf16[1024,4096]{1,0:T(8,128)(2,1)} %param.3, f32[64,4096]{1,0:T(8,128)} %bitcast.10, f32[64,4096]{1,0:T(8,128)} %bitcast.15), kind=kOutput, calls=%fused_computation.22 | convolution fusion | flops 1075838976 | bytes 11010048 | tf_op jit(solution)/shard_map/dot_general | solution.py:228
  7.8 0.7 constant_dynamic-slice_fusion.6
  9.0 0.7 constant_dynamic-slice_fusion.1
  9.7 2.4 %fusion.10 = f32[128,128]{1,0:T(8,128)} fusion(f32[64,4096]{1,0:T(8,128)S(1)} %bitcast.11, f32[64,4096]{1,0:T(8,128)S(1)} %bitcast.16), kind=kOutput, calls=%fused_computation.16 | convolution fusion | flops 805830656 | bytes 2162688 | tf_op jit(solution)/shard_map/dot_general | solution.py:22
  12.6 1.9 %pad_slice_fusion.1 = (f32[128,2048]{1,0:T(8,128)}, f32[128,2048]{1,0:T(8,128)S(1)}, f32[128,2048]{1,0:T(8,128)}, f32[128,2048]{1,0:T(8,128)}) fusion(f32[64,4096]{1,0:T(8,128)S(1)} %bitcast.12, f32[64,4096]{1,0:T(8,128)S(1)} %bitcast.17), kind=kLoop, calls=%fused_computation.10 | loop fusion | bytes 6291456 | tf_op jit(solution)/shard_map/slice | solution.py:253
  14.5 1.2 dynamic-slice_maximum_fusion
  15.7 1.3 dynamic-slice_maximum_fusion.1
  17.0 0.9 add.215
  17.9 2.6 %collective-permute-start.21 = (f32[128,128]{1,0:T(8,128)S(1)}, f32[128,128]{1,0:T(8,128)S(1)}, u32[]{:S(2)}, u32[]{:S(2)}) collective-permute-start(f32[128,128]{1,0:T(8,128)S(1)} %add.215), channel_id=1, source_target_pairs={{0,8},{8,0},{16,24},{24,16},{1,9},{9,1},{17,25},{25,17},{2,10},{10... | collective-permute-start | bytes 196616 | tf_op jit(solution)/shard_map/ppermute | solution.py:178
  20.5 1.5 collective-permute-start.22
  22.0 1.0 dynamic-slice_add_fusion.4
  23.0 2.0 %collective-permute-start.1 = (f32[64,512]{1,0:T(8,128)S(1)}, f32[64,512]{1,0:T(8,128)S(1)}, u32[]{:S(2)}, u32[]{:S(2)}) collective-permute-start(f32[64,512]{1,0:T(8,128)S(1)} %dynamic-slice_add_fusion.4), channel_id=1, source_target_pairs={{0,8},{8,0},{16,24},{24,16},{1,9},{9,1},{17,25},{25,17},{2,10},{10... | collective-permute-start | bytes 393224 | tf_op jit(solution)/shard_map/ppermute | solution.py:178
  25.0 1.5 collective-permute-start.2
  26.5 1.0 dynamic-slice_add_fusion.3
  27.6 1.9 %collective-permute-start.32 = (f32[64,512]{1,0:T(8,128)S(1)}, f32[64,512]{1,0:T(8,128)S(1)}, u32[]{:S(2)}, u32[]{:S(2)}) collective-permute-start(f32[64,512]{1,0:T(8,128)S(1)} %dynamic-slice_add_fusion.3), channel_id=1, source_target_pairs={{0,8},{8,0},{16,24},{24,16},{1,9},{9,1},{17,25},{25,17},{2,10},{10... | collective-permute-start | bytes 393224 | tf_op jit(solution)/shard_map/ppermute | solution.py:178
  29.6 1.5 collective-permute-start.33
  31.1 0.6 add_multiply_fusion.3.gram_ref
  31.8 6.0 %whiten_given.1.given_ref = f32[128,128]{1,0:T(8,128)} custom-call(f32[128,128]{1,0:T(8,128)} %add_multiply_fusion.3.gram_ref), custom_call_target="tpu_custom_call" | custom-call | flops 4000000000 | bytes 131072 | tf_op jit(solution)/shard_map/whiten_given/pallas_call | solution.py:81
  37.9 0.9 fusion.54
  39.0 4.7 %collective-permute-done.34 = f32[64,512]{1,0:T(8,128)S(1)} collective-permute-done((f32[64,512]{1,0:T(8,128)S(1)}, f32[64,512]{1,0:T(8,128)S(1)}, u32[]{:S(2)}, u32[]{:S(2)}) %collective-permute-start.34) | collective-permute-done | bytes 131104 | tf_op jit(solution)/shard_map/ppermute | solution.py:178
  43.7 1.0 fusion.55
  45.3 1.6 collective-permute-start.7
  46.9 2.5 %collective-permute-start.8 = (f32[64,64]{1,0:T(8,128)S(1)}, f32[64,64]{1,0:T(8,128)S(1)}, u32[]{:S(2)}, u32[]{:S(2)}) collective-permute-start(f32[64,64]{1,0:T(8,128)S(1)} %fusion.38), channel_id=1, source_target_pairs={{0,4},{2,6},{4,0},{6,2},{1,5},{3,7},{5,1},{7,3},{8,12},{10,14},{12... | collective-permute-start | bytes 49160 | tf_op jit(solution)/shard_map/ppermute | solution.py:178
  49.7 3.1 %fusion.2 = f32[64,2048]{1,0:T(8,128)S(1)} fusion(bf16[1024,4096]{1,0:T(8,128)(2,1)} %param.3, bf16[64,512]{1,0:T(8,128)(2,1)S(1)} %get-tuple-element.38, bf16[64,512]{1,0:T(8,128)(2,1)S(1)} %get-tuple-element.37), kind=kOutput, calls=%fused_computation.2 | convolution fusion | flops 268697600 | bytes 4849664 | tf_op jit(solution)/shard_map/dot_general | solution.py:249
  52.8 3.1 %fusion.6 = f32[64,2048]{1,0:T(8,128)S(1)} fusion(bf16[1024,4096]{1,0:T(8,128)(2,1)} %param.3, bf16[64,512]{1,0:T(8,128)(2,1)S(1)} %get-tuple-element.38, bf16[64,512]{1,0:T(8,128)(2,1)S(1)} %get-tuple-element.37), kind=kOutput, calls=%fused_computation.6 | convolution fusion | flops 268697600 | bytes 4849664 | tf_op jit(solution)/shard_map/dot_general | solution.py:249
  55.9 0.7 collective-permute-start.36
  56.6 3.4 %collective-permute-start.37 = (f32[128,128]{1,0:T(8,128)S(1)}, f32[128,128]{1,0:T(8,128)S(1)}, u32[]{:S(2)}, u32[]{:S(2)}) collective-permute-start(f32[128,128]{1,0:T(8,128)S(1)} %add.231), channel_id=1, source_target_pairs={{0,4},{2,6},{4,0},{6,2},{1,5},{3,7},{5,1},{7,3},{8,12},{10,14},{12... | collective-permute-start | bytes 196616 | tf_op jit(solution)/shard_map/ppermute | solution.py:178
  60.8 1.7 %collective-permute-start.5 = (f32[64,1024]{1,0:T(8,128)S(1)}, f32[64,1024]{1,0:T(8,128)S(1)}, u32[]{:S(2)}, u32[]{:S(2)}) collective-permute-start(f32[64,1024]{1,0:T(8,128)S(1)} %constant_dynamic-slice_fusion.5), channel_id=1, source_target_pairs={{0,2},{2,0},{4,6},{6,4},{1,3},{3,1},{5,7},{7,5},{8,10},{10,8},{12,... | collective-permute-start | bytes 786440 | tf_op jit(solution)/shard_map/ppermute | solution.py:178
  62.5 1.3 collective-permute-done.37
  63.8 3.2 %collective-permute-done.38 = f32[128,128]{1,0:T(8,128)S(1)} collective-permute-done((f32[128,128]{1,0:T(8,128)S(1)}, f32[128,128]{1,0:T(8,128)S(1)}, u32[]{:S(2)}, u32[]{:S(2)}) %collective-permute-start.38) | collective-permute-done | bytes 65568 | tf_op jit(solution)/shard_map/ppermute | solution.py:178
  67.7 3.2 %collective-permute-done.14 = f32[64,1024]{1,0:T(8,128)S(1)} collective-permute-done((f32[64,1024]{1,0:T(8,128)S(1)}, f32[64,1024]{1,0:T(8,128)S(1)}, u32[]{:S(2)}, u32[]{:S(2)}) %collective-permute-start.14) | collective-permute-done | bytes 262176 | tf_op jit(solution)/shard_map/ppermute | solution.py:178
  71.0 2.4 %collective-permute-start.15 = (f32[64,512]{1,0:T(8,128)S(1)}, f32[64,512]{1,0:T(8,128)S(1)}, u32[]{:S(2)}, u32[]{:S(2)}) collective-permute-start(f32[64,512]{1,0:T(8,128)S(1)} %constant_dynamic-slice_fusion.2), channel_id=1, source_target_pairs={{0,4},{2,6},{4,0},{6,2},{1,5},{3,7},{5,1},{7,3},{8,12},{10,14},{12... | collective-permute-start | bytes 393224 | tf_op jit(solution)/shard_map/ppermute | solution.py:178
  73.3 4.6 %collective-permute-done.5 = f32[64,1024]{1,0:T(8,128)S(1)} collective-permute-done((f32[64,1024]{1,0:T(8,128)S(1)}, f32[64,1024]{1,0:T(8,128)S(1)}, u32[]{:S(2)}, u32[]{:S(2)}) %collective-permute-start.5) | collective-permute-done | bytes 262176 | tf_op jit(solution)/shard_map/ppermute | solution.py:178
  78.7 2.7 %collective-permute-start.16 = (bf16[64,512]{1,0:T(8,128)(2,1)S(1)}, bf16[64,512]{1,0:T(8,128)(2,1)S(1)}, u32[]{:S(2)}, u32[]{:S(2)}) collective-permute-start(bf16[64,512]{1,0:T(8,128)(2,1)S(1)} %get-tuple-element.13), channel_id=1, source_target_pairs={{0,4},{2,6},{4,0},{6,2},{1,5},{3,7},{5,1},{7,3},{8,12},{10,14},{12... | collective-permute-start | bytes 196616 | tf_op jit(solution)/shard_map/ppermute | solution.py:178
  81.9 4.3 %collective-permute-done.6 = f32[64,512]{1,0:T(8,128)S(1)} collective-permute-done((f32[64,512]{1,0:T(8,128)S(1)}, f32[64,512]{1,0:T(8,128)S(1)}, u32[]{:S(2)}, u32[]{:S(2)}) %collective-permute-start.6) | collective-permute-done | bytes 131104 | tf_op jit(solution)/shard_map/ppermute | solution.py:178
  87.4 2.9 %collective-permute-start.12 = (bf16[64,512]{1,0:T(8,128)(2,1)S(1)}, bf16[64,512]{1,0:T(8,128)(2,1)S(1)}, u32[]{:S(2)}, u32[]{:S(2)}) collective-permute-start(bf16[64,512]{1,0:T(8,128)(2,1)S(1)} %fusion.30), channel_id=1, source_target_pairs={{0,4},{2,6},{4,0},{6,2},{1,5},{3,7},{5,1},{7,3},{8,12},{10,14},{12... | collective-permute-start | bytes 196616 | tf_op jit(solution)/shard_map/ppermute | solution.py:178
  91.5 5.7 %collective-permute-done.10 = bf16[64,512]{1,0:T(8,128)(2,1)S(1)} collective-permute-done((bf16[64,512]{1,0:T(8,128)(2,1)S(1)}, bf16[64,512]{1,0:T(8,128)(2,1)S(1)}, u32[]{:S(2)}, u32[]{:S(2)}) %collective-permute-start.10) | collective-permute-done | bytes 65568 | tf_op jit(solution)/shard_map/ppermute | solution.py:178
  97.7 0.7 pad_maximum_fusion.15
  98.7 0.7 pad_maximum_fusion.13
  99.8 1.6 collective-permute-start.11
  101.4 0.7 pad_maximum_fusion.14
  102.6 1.9 %collective-permute-start.29 = (f32[64,192]{1,0:T(8,128)S(1)}, f32[64,192]{1,0:T(8,128)S(1)}, u32[]{:S(2)}, u32[]{:S(2)}) collective-permute-start(f32[64,192]{1,0:T(8,128)S(1)} %add_add_fusion.3), channel_id=1, source_target_pairs={{0,4},{2,6},{4,0},{6,2},{1,5},{3,7},{5,1},{7,3},{8,12},{10,14},{12... | collective-permute-start | bytes 147464 | tf_op jit(solution)/shard_map/ppermute | solution.py:178
  104.5 2.3 %collective-permute-start.30 = (f32[64,192]{1,0:T(8,128)S(1)}, f32[64,192]{1,0:T(8,128)S(1)}, u32[]{:S(2)}, u32[]{:S(2)}) collective-permute-start(f32[64,192]{1,0:T(8,128)S(1)} %add_add_fusion.3), channel_id=1, source_target_pairs={{0,6},{2,4},{4,2},{6,0},{1,7},{3,5},{5,3},{7,1},{8,14},{10,12},{12... | collective-permute-start | bytes 147464 | tf_op jit(solution)/shard_map/ppermute | solution.py:178
  106.9 0.7 pad_maximum_fusion.16
  107.5 2.9 %collective-permute-done.28 = f32[64,192]{1,0:T(8,128)S(1)} collective-permute-done((f32[64,192]{1,0:T(8,128)S(1)}, f32[64,192]{1,0:T(8,128)S(1)}, u32[]{:S(2)}, u32[]{:S(2)}) %collective-permute-start.28) | collective-permute-done | bytes 49184 | tf_op jit(solution)/shard_map/ppermute | solution.py:178
  110.5 2.0 %collective-permute-start.19 = (bf16[64,1024]{1,0:T(8,128)(2,1)}, bf16[64,1024]{1,0:T(8,128)(2,1)S(1)}, u32[]{:S(2)}, u32[]{:S(2)}) collective-permute-start(bf16[64,1024]{1,0:T(8,128)(2,1)} %pad_maximum_fusion.16), channel_id=1, source_target_pairs={{0,2},{2,0},{4,6},{6,4},{1,3},{3,1},{5,7},{7,5},{8,10},{10,8},{12,... | collective-permute-start | bytes 393224 | tf_op jit(solution)/shard_map/ppermute | solution.py:178
  113.1 4.0 %whiten_rest.1.rest_ref = f32[64,192]{1,0:T(8,128)} custom-call(f32[128,128]{1,0:T(8,128)} %whiten_given.1.given_ref, f32[64,192]{1,0:T(8,128)} %add_multiply_fusion.2.gram_ref), custom_call_target="tpu_custom_call" | custom-call | flops 3000000000 | bytes 131072 | tf_op jit(solution)/shard_map/whiten_rest/pallas_call | solution.py:98
  117.2 3.6 %fusion = f32[64,1024]{1,0:T(8,128)S(1)} fusion(bf16[1024,4096]{1,0:T(8,128)(2,1)} %param.3, bf16[64,1024]{1,0:T(8,128)(2,1)S(1)} %get-tuple-element.26, bf16[64,1024]{1,0:T(8,128)(2,1)S(1)} %get-tuple-element.25), kind=kOutput, calls=%fused_computation | convolution fusion | flops 268959744 | bytes 4718592 | tf_op jit(solution)/shard_map/dot_general | solution.py:228
  120.8 3.6 %fusion.12 = f32[64,1024]{1,0:T(8,128)S(1)} fusion(f32[64,1024]{1,0:T(8,128)S(1)} %fusion, bf16[1024,4096]{1,0:T(8,128)(2,1)} %param.3, bf16[64,1024]{1,0:T(8,128)(2,1)S(1)} %get-tuple-element.22, bf16[64,1024]{1,0:T(8,128)(2,1)S(1)} %get-tuple-element.21), kind=kOutput, calls=%fused_computation.18 | convolution fusion | flops 269025280 | bytes 4980736 | tf_op jit(solution)/shard_map/dot_general | solution.py:228
  124.5 1.0 broadcast_select_fusion.5
  125.9 0.7 collective-permute-start.40
  126.6 1.1 collective-permute-start.41
  127.7 1.7 %collective-permute-start.42 = (f32[64,512]{1,0:T(8,128)S(1)}, f32[64,512]{1,0:T(8,128)S(1)}, u32[]{:S(2)}, u32[]{:S(2)}) collective-permute-start(f32[64,512]{1,0:T(8,128)S(1)} %dynamic-slice_add_fusion.2), channel_id=1, source_target_pairs={{0,24},{8,16},{16,8},{24,0},{1,25},{9,17},{17,9},{25,1},{2,26},{10... | collective-permute-start | bytes 393224 | tf_op jit(solution)/shard_map/ppermute | solution.py:178
  129.4 0.8 convert_add_fusion.1
  130.3 2.0 %collective-permute-done.40 = f32[64,512]{1,0:T(8,128)S(1)} collective-permute-done((f32[64,512]{1,0:T(8,128)S(1)}, f32[64,512]{1,0:T(8,128)S(1)}, u32[]{:S(2)}, u32[]{:S(2)}) %collective-permute-start.40) | collective-permute-done | bytes 131104 | tf_op jit(solution)/shard_map/ppermute | solution.py:178
  132.3 2.4 %collective-permute-done.41 = f32[64,512]{1,0:T(8,128)S(1)} collective-permute-done((f32[64,512]{1,0:T(8,128)S(1)}, f32[64,512]{1,0:T(8,128)S(1)}, u32[]{:S(2)}, u32[]{:S(2)}) %collective-permute-start.41) | collective-permute-done | bytes 131104 | tf_op jit(solution)/shard_map/ppermute | solution.py:178
  136.0 1.2 collective-permute-done.43
  137.3 2.5 %collective-permute-start.45 = (f32[64,192]{1,0:T(8,128)S(1)}, f32[64,192]{1,0:T(8,128)S(1)}, u32[]{:S(2)}, u32[]{:S(2)}) collective-permute-start(f32[64,192]{1,0:T(8,128)S(1)} %fusion.53), channel_id=1, source_target_pairs={{0,4},{2,6},{4,0},{6,2},{1,5},{3,7},{5,1},{7,3},{8,12},{10,14},{12... | collective-permute-start | bytes 147464 | tf_op jit(solution)/shard_map/ppermute | solution.py:178
  139.7 1.9 %collective-permute-start.46 = (f32[64,192]{1,0:T(8,128)S(1)}, f32[64,192]{1,0:T(8,128)S(1)}, u32[]{:S(2)}, u32[]{:S(2)}) collective-permute-start(f32[64,192]{1,0:T(8,128)S(1)} %fusion.53), channel_id=1, source_target_pairs={{0,6},{2,4},{4,2},{6,0},{1,7},{3,5},{5,3},{7,1},{8,14},{10,12},{12... | collective-permute-start | bytes 147464 | tf_op jit(solution)/shard_map/ppermute | solution.py:178
  141.7 0.7 collective-permute-done.44
  142.4 3.5 %collective-permute-done.45 = f32[64,192]{1,0:T(8,128)S(1)} collective-permute-done((f32[64,192]{1,0:T(8,128)S(1)}, f32[64,192]{1,0:T(8,128)S(1)}, u32[]{:S(2)}, u32[]{:S(2)}) %collective-permute-start.45) | collective-permute-done | bytes 49184 | tf_op jit(solution)/shard_map/ppermute | solution.py:178
  146.6 10.2 %ritz.1 = (f32[192,128]{1,0:T(8,128)}, f32[1,64]{1,0:T(1,128)}) custom-call(f32[128,128]{1,0:T(8,128)} %whiten_given.1.given_ref, f32[64,192]{1,0:T(8,128)} %whiten_rest.1.rest_ref, f32[128,128]{1,0:T(8,128)} %add_multiply_fusion.1.raw_given_ref, f32[64,192]{1,0:T(8,128)} %add_multiply_fusion.raw_rest_ref), custom_call_target="tpu_custom_call" | custom-call | flops 10000000000 | bytes 524288 | tf_op jit(solution)/shard_map/ritz/pallas_call | solution.py:155
  156.7 4.2 %fusion.8 = f32[4096,64]{0,1:T(8,128)} fusion(f32[64,2048]{1,0:T(8,128)S(1)} %convert_add_fusion, f32[64,2048]{1,0:T(8,128)S(1)} %copy-done.4, f32[64,4096]{1,0:T(8,128)S(1)} %bitcast.13, f32[64,4096]{1,0:T(8,128)S(1)} %bitcast.18, f32[192,128]{1,0:T(8,128)} %get-tuple-element.5), kind=kOutput, calls=%fused_computation.14 | convolution fusion | flops 606339072 | bytes 4292608 | tf_op jit(solution)/shard_map/dot_general | solution.py:16
  160.9 3.2 %fusion.9 = f32[4096,64]{0,1:T(8,128)} fusion(f32[64,2048]{1,0:T(8,128)S(1)} %convert_add_fusion, f32[64,2048]{1,0:T(8,128)S(1)} %copy-done.4, f32[64,4096]{1,0:T(8,128)S(1)} %bitcast.14, f32[64,4096]{1,0:T(8,128)S(1)} %bitcast.19, f32[192,128]{1,0:T(8,128)S(1)} %copy-done.5), kind=kOutput, calls=%fused_computation.15 | convolution fusion | flops 606339072 | bytes 4292608 | tf_op jit(solution)/shard_map/dot_general | solution.py:16
  (110 shorter events, 12.4 us)
Async XLA Ops:
  0.6 9.1 %copy-start = (f32[4096,64]{0,1:T(8,128)S(1)}, f32[4096,64]{0,1:T(8,128)}, u32[]{:S(2)}) copy-start(f32[4096,64]{0,1:T(8,128)} %param.5) | copy-start | bytes 3145732
  0.7 9.1 %copy-start.1 = (f32[4096,64]{0,1:T(8,128)S(1)}, f32[4096,64]{0,1:T(8,128)}, u32[]{:S(2)}) copy-start(f32[4096,64]{0,1:T(8,128)} %param.4) | copy-start | bytes 3145732
  7.8 4.8 %copy-start.3 = (f32[64,1024]{1,0:T(8,128)}, f32[64,1024]{1,0:T(8,128)S(1)}, u32[]{:S(2)}) copy-start(f32[64,1024]{1,0:T(8,128)S(1)} %get-tuple-element.20) | copy-start | bytes 786436
  7.8 6.7 %copy-start.2 = (f32[64,1024]{1,0:T(8,128)}, f32[64,1024]{1,0:T(8,128)S(1)}, u32[]{:S(2)}) copy-start(f32[64,1024]{1,0:T(8,128)S(1)} %get-tuple-element.19) | copy-start | bytes 786436
  8.6 13.5 %collective-permute-start = (f32[64,512]{1,0:T(8,128)}, f32[64,512]{1,0:T(8,128)}, u32[]{:S(2)}, u32[]{:S(2)}) collective-permute-start(f32[64,512]{1,0:T(8,128)} %constant_dynamic-slice_fusion.6), channel_id=1, source_target_pairs={{0,1},{1,0},{2,3},{3,2},{4,5},{5,4},{6,7},{7,6},{8,9},{9,8},{10,11... | collective-permute-start | bytes 393224 | tf_op jit(solution)/shard_map/ppermute | solution.py:178
  9.7 15.4 %collective-permute-start.31 = (f32[64,512]{1,0:T(8,128)}, f32[64,512]{1,0:T(8,128)}, u32[]{:S(2)}, u32[]{:S(2)}) collective-permute-start(f32[64,512]{1,0:T(8,128)} %constant_dynamic-slice_fusion.1), channel_id=1, source_target_pairs={{0,1},{1,0},{2,3},{3,2},{4,5},{5,4},{6,7},{7,6},{8,9},{9,8},{10,11... | collective-permute-start | bytes 393224 | tf_op jit(solution)/shard_map/ppermute | solution.py:178
  12.2 4.9 %collective-permute-start.20 = (f32[128,128]{1,0:T(8,128)}, f32[128,128]{1,0:T(8,128)}, u32[]{:S(2)}, u32[]{:S(2)}) collective-permute-start(f32[128,128]{1,0:T(8,128)} %fusion.10), channel_id=1, source_target_pairs={{0,1},{1,0},{2,3},{3,2},{4,5},{5,4},{6,7},{7,6},{8,9},{9,8},{10,11... | collective-permute-start | bytes 196616 | tf_op jit(solution)/shard_map/ppermute | solution.py:178
  17.9 9.6 %collective-permute-start.21 = (f32[128,128]{1,0:T(8,128)S(1)}, f32[128,128]{1,0:T(8,128)S(1)}, u32[]{:S(2)}, u32[]{:S(2)}) collective-permute-start(f32[128,128]{1,0:T(8,128)S(1)} %add.215), channel_id=1, source_target_pairs={{0,8},{8,0},{16,24},{24,16},{1,9},{9,1},{17,25},{25,17},{2,10},{10... | collective-permute-start | bytes 196616 | tf_op jit(solution)/shard_map/ppermute | solution.py:178
  20.5 7.2 %collective-permute-start.22 = (f32[128,128]{1,0:T(8,128)S(1)}, f32[128,128]{1,0:T(8,128)S(1)}, u32[]{:S(2)}, u32[]{:S(2)}) collective-permute-start(f32[128,128]{1,0:T(8,128)S(1)} %add.215), channel_id=1, source_target_pairs={{0,16},{8,24},{16,0},{24,8},{1,17},{9,25},{17,1},{25,9},{2,18},{10... | collective-permute-start | bytes 196616 | tf_op jit(solution)/shard_map/ppermute | solution.py:178
  22.0 7.6 %collective-permute-start.23 = (f32[128,128]{1,0:T(8,128)S(1)}, f32[128,128]{1,0:T(8,128)S(1)}, u32[]{:S(2)}, u32[]{:S(2)}) collective-permute-start(f32[128,128]{1,0:T(8,128)S(1)} %add.215), channel_id=1, source_target_pairs={{0,24},{8,16},{16,8},{24,0},{1,25},{9,17},{17,9},{25,1},{2,26},{10... | collective-permute-start | bytes 196616 | tf_op jit(solution)/shard_map/ppermute | solution.py:178
  23.0 14.8 %collective-permute-start.1 = (f32[64,512]{1,0:T(8,128)S(1)}, f32[64,512]{1,0:T(8,128)S(1)}, u32[]{:S(2)}, u32[]{:S(2)}) collective-permute-start(f32[64,512]{1,0:T(8,128)S(1)} %dynamic-slice_add_fusion.4), channel_id=1, source_target_pairs={{0,8},{8,0},{16,24},{24,16},{1,9},{9,1},{17,25},{25,17},{2,10},{10... | collective-permute-start | bytes 393224 | tf_op jit(solution)/shard_map/ppermute | solution.py:178
  25.0 12.9 %collective-permute-start.2 = (f32[64,512]{1,0:T(8,128)S(1)}, f32[64,512]{1,0:T(8,128)S(1)}, u32[]{:S(2)}, u32[]{:S(2)}) collective-permute-start(f32[64,512]{1,0:T(8,128)S(1)} %dynamic-slice_add_fusion.4), channel_id=1, source_target_pairs={{0,16},{8,24},{16,0},{24,8},{1,17},{9,25},{17,1},{25,9},{2,18},{10... | collective-permute-start | bytes 393224 | tf_op jit(solution)/shard_map/ppermute | solution.py:178
  27.5 10.3 %collective-permute-start.3 = (f32[64,512]{1,0:T(8,128)S(1)}, f32[64,512]{1,0:T(8,128)}, u32[]{:S(2)}, u32[]{:S(2)}) collective-permute-start(f32[64,512]{1,0:T(8,128)S(1)} %dynamic-slice_add_fusion.4), channel_id=1, source_target_pairs={{0,24},{8,16},{16,8},{24,0},{1,25},{9,17},{17,9},{25,1},{2,26},{10... | collective-permute-start | bytes 393224 | tf_op jit(solution)/shard_map/ppermute | solution.py:178
  27.6 11.3 %collective-permute-start.32 = (f32[64,512]{1,0:T(8,128)S(1)}, f32[64,512]{1,0:T(8,128)S(1)}, u32[]{:S(2)}, u32[]{:S(2)}) collective-permute-start(f32[64,512]{1,0:T(8,128)S(1)} %dynamic-slice_add_fusion.3), channel_id=1, source_target_pairs={{0,8},{8,0},{16,24},{24,16},{1,9},{9,1},{17,25},{25,17},{2,10},{10... | collective-permute-start | bytes 393224 | tf_op jit(solution)/shard_map/ppermute | solution.py:178
  29.6 9.4 %collective-permute-start.33 = (f32[64,512]{1,0:T(8,128)S(1)}, f32[64,512]{1,0:T(8,128)}, u32[]{:S(2)}, u32[]{:S(2)}) collective-permute-start(f32[64,512]{1,0:T(8,128)S(1)} %dynamic-slice_add_fusion.3), channel_id=1, source_target_pairs={{0,16},{8,24},{16,0},{24,8},{1,17},{9,25},{17,1},{25,9},{2,18},{10... | collective-permute-start | bytes 393224 | tf_op jit(solution)/shard_map/ppermute | solution.py:178
  37.8 5.9 %collective-permute-start.34 = (f32[64,512]{1,0:T(8,128)S(1)}, f32[64,512]{1,0:T(8,128)S(1)}, u32[]{:S(2)}, u32[]{:S(2)}) collective-permute-start(f32[64,512]{1,0:T(8,128)S(1)} %dynamic-slice_add_fusion.3), channel_id=1, source_target_pairs={{0,24},{8,16},{16,8},{24,0},{1,25},{9,17},{17,9},{25,1},{2,26},{10... | collective-permute-start | bytes 393224 | tf_op jit(solution)/shard_map/ppermute | solution.py:178
  38.9 6.2 %collective-permute-start.4 = (bf16[64,512]{1,0:T(8,128)(2,1)S(1)}, bf16[64,512]{1,0:T(8,128)(2,1)S(1)}, u32[]{:S(2)}, u32[]{:S(2)}) collective-permute-start(bf16[64,512]{1,0:T(8,128)(2,1)S(1)} %reduce-precision_convert_fusion.2), channel_id=1, source_target_pairs={{0,1},{1,0},{2,3},{3,2},{4,5},{5,4},{6,7},{7,6},{8,9},{9,8},{10,11... | collective-permute-start | bytes 196616 | tf_op jit(solution)/shard_map/ppermute | solution.py:178
  45.0 10.9 %collective-permute-start.35 = (f32[128,128]{1,0:T(8,128)S(1)}, f32[128,128]{1,0:T(8,128)S(1)}, u32[]{:S(2)}, u32[]{:S(2)}) collective-permute-start(f32[128,128]{1,0:T(8,128)S(1)} %fusion.25), channel_id=1, source_target_pairs={{0,1},{1,0},{2,3},{3,2},{4,5},{5,4},{6,7},{7,6},{8,9},{9,8},{10,11... | collective-permute-start | bytes 196616 | tf_op jit(solution)/shard_map/ppermute | solution.py:178
  45.3 14.8 %collective-permute-start.7 = (f32[64,64]{1,0:T(8,128)S(1)}, f32[64,64]{1,0:T(8,128)S(1)}, u32[]{:S(2)}, u32[]{:S(2)}) collective-permute-start(f32[64,64]{1,0:T(8,128)S(1)} %fusion.38), channel_id=1, source_target_pairs={{0,2},{2,0},{4,6},{6,4},{1,3},{3,1},{5,7},{7,5},{8,10},{10,8},{12,... | collective-permute-start | bytes 49160 | tf_op jit(solution)/shard_map/ppermute | solution.py:178
  46.9 13.6 %collective-permute-start.8 = (f32[64,64]{1,0:T(8,128)S(1)}, f32[64,64]{1,0:T(8,128)S(1)}, u32[]{:S(2)}, u32[]{:S(2)}) collective-permute-start(f32[64,64]{1,0:T(8,128)S(1)} %fusion.38), channel_id=1, source_target_pairs={{0,4},{2,6},{4,0},{6,2},{1,5},{3,7},{5,1},{7,3},{8,12},{10,14},{12... | collective-permute-start | bytes 49160 | tf_op jit(solution)/shard_map/ppermute | solution.py:178
  49.4 11.3 %collective-permute-start.9 = (f32[64,64]{1,0:T(8,128)S(1)}, f32[64,64]{1,0:T(8,128)S(1)}, u32[]{:S(2)}, u32[]{:S(2)}) collective-permute-start(f32[64,64]{1,0:T(8,128)S(1)} %fusion.38), channel_id=1, source_target_pairs={{0,6},{2,4},{4,2},{6,0},{1,7},{3,5},{5,3},{7,1},{8,14},{10,12},{12... | collective-permute-start | bytes 49160 | tf_op jit(solution)/shard_map/ppermute | solution.py:178
  55.9 6.6 %collective-permute-start.36 = (f32[128,128]{1,0:T(8,128)S(1)}, f32[128,128]{1,0:T(8,128)S(1)}, u32[]{:S(2)}, u32[]{:S(2)}) collective-permute-start(f32[128,128]{1,0:T(8,128)S(1)} %add.231), channel_id=1, source_target_pairs={{0,2},{2,0},{4,6},{6,4},{1,3},{3,1},{5,7},{7,5},{8,10},{10,8},{12,... | collective-permute-start | bytes 196616 | tf_op jit(solution)/shard_map/ppermute | solution.py:178
  56.6 7.2 %collective-permute-start.37 = (f32[128,128]{1,0:T(8,128)S(1)}, f32[128,128]{1,0:T(8,128)S(1)}, u32[]{:S(2)}, u32[]{:S(2)}) collective-permute-start(f32[128,128]{1,0:T(8,128)S(1)} %add.231), channel_id=1, source_target_pairs={{0,4},{2,6},{4,0},{6,2},{1,5},{3,7},{5,1},{7,3},{8,12},{10,14},{12... | collective-permute-start | bytes 196616 | tf_op jit(solution)/shard_map/ppermute | solution.py:178
  60.1 6.9 %collective-permute-start.38 = (f32[128,128]{1,0:T(8,128)S(1)}, f32[128,128]{1,0:T(8,128)S(1)}, u32[]{:S(2)}, u32[]{:S(2)}) collective-permute-start(f32[128,128]{1,0:T(8,128)S(1)} %add.231), channel_id=1, source_target_pairs={{0,6},{2,4},{4,2},{6,0},{1,7},{3,5},{5,3},{7,1},{8,14},{10,12},{12... | collective-permute-start | bytes 196616 | tf_op jit(solution)/shard_map/ppermute | solution.py:178
  60.5 10.4 %collective-permute-start.14 = (f32[64,1024]{1,0:T(8,128)S(1)}, f32[64,1024]{1,0:T(8,128)S(1)}, u32[]{:S(2)}, u32[]{:S(2)}) collective-permute-start(f32[64,1024]{1,0:T(8,128)S(1)} %constant_dynamic-slice_fusion.3), channel_id=1, source_target_pairs={{0,2},{2,0},{4,6},{6,4},{1,3},{3,1},{5,7},{7,5},{8,10},{10,8},{12,... | collective-permute-start | bytes 786440 | tf_op jit(solution)/shard_map/ppermute | solution.py:178
  60.8 17.2 %collective-permute-start.5 = (f32[64,1024]{1,0:T(8,128)S(1)}, f32[64,1024]{1,0:T(8,128)S(1)}, u32[]{:S(2)}, u32[]{:S(2)}) collective-permute-start(f32[64,1024]{1,0:T(8,128)S(1)} %constant_dynamic-slice_fusion.5), channel_id=1, source_target_pairs={{0,2},{2,0},{4,6},{6,4},{1,3},{3,1},{5,7},{7,5},{8,10},{10,8},{12,... | collective-permute-start | bytes 786440 | tf_op jit(solution)/shard_map/ppermute | solution.py:178
  71.0 7.4 %collective-permute-start.15 = (f32[64,512]{1,0:T(8,128)S(1)}, f32[64,512]{1,0:T(8,128)S(1)}, u32[]{:S(2)}, u32[]{:S(2)}) collective-permute-start(f32[64,512]{1,0:T(8,128)S(1)} %constant_dynamic-slice_fusion.2), channel_id=1, source_target_pairs={{0,4},{2,6},{4,0},{6,2},{1,5},{3,7},{5,1},{7,3},{8,12},{10,14},{12... | collective-permute-start | bytes 393224 | tf_op jit(solution)/shard_map/ppermute | solution.py:178
  78.0 8.1 %collective-permute-start.6 = (f32[64,512]{1,0:T(8,128)S(1)}, f32[64,512]{1,0:T(8,128)S(1)}, u32[]{:S(2)}, u32[]{:S(2)}) collective-permute-start(f32[64,512]{1,0:T(8,128)S(1)} %constant_dynamic-slice_fusion.4), channel_id=1, source_target_pairs={{0,4},{2,6},{4,0},{6,2},{1,5},{3,7},{5,1},{7,3},{8,12},{10,14},{12... | collective-permute-start | bytes 393224 | tf_op jit(solution)/shard_map/ppermute | solution.py:178
  78.7 12.3 %collective-permute-start.16 = (bf16[64,512]{1,0:T(8,128)(2,1)S(1)}, bf16[64,512]{1,0:T(8,128)(2,1)S(1)}, u32[]{:S(2)}, u32[]{:S(2)}) collective-permute-start(bf16[64,512]{1,0:T(8,128)(2,1)S(1)} %get-tuple-element.13), channel_id=1, source_target_pairs={{0,4},{2,6},{4,0},{6,2},{1,5},{3,7},{5,1},{7,3},{8,12},{10,14},{12... | collective-permute-start | bytes 196616 | tf_op jit(solution)/shard_map/ppermute | solution.py:178
  87.0 3.4 %collective-permute-start.24 = (f32[64,192]{1,0:T(8,128)S(1)}, f32[64,192]{1,0:T(8,128)S(1)}, u32[]{:S(2)}, u32[]{:S(2)}) collective-permute-start(f32[64,192]{1,0:T(8,128)S(1)} %convolution_add_fusion), channel_id=1, source_target_pairs={{0,1},{1,0},{2,3},{3,2},{4,5},{5,4},{6,7},{7,6},{8,9},{9,8},{10,11... | collective-permute-start | bytes 147464 | tf_op jit(solution)/shard_map/ppermute | solution.py:178
  87.3 9.9 %collective-permute-start.10 = (bf16[64,512]{1,0:T(8,128)(2,1)S(1)}, bf16[64,512]{1,0:T(8,128)(2,1)S(1)}, u32[]{:S(2)}, u32[]{:S(2)}) collective-permute-start(bf16[64,512]{1,0:T(8,128)(2,1)S(1)} %get-tuple-element.11), channel_id=1, source_target_pairs={{0,4},{2,6},{4,0},{6,2},{1,5},{3,7},{5,1},{7,3},{8,12},{10,14},{12... | collective-permute-start | bytes 196616 | tf_op jit(solution)/shard_map/ppermute | solution.py:178
  87.4 11.2 %collective-permute-start.12 = (bf16[64,512]{1,0:T(8,128)(2,1)S(1)}, bf16[64,512]{1,0:T(8,128)(2,1)S(1)}, u32[]{:S(2)}, u32[]{:S(2)}) collective-permute-start(bf16[64,512]{1,0:T(8,128)(2,1)S(1)} %fusion.30), channel_id=1, source_target_pairs={{0,4},{2,6},{4,0},{6,2},{1,5},{3,7},{5,1},{7,3},{8,12},{10,14},{12... | collective-permute-start | bytes 196616 | tf_op jit(solution)/shard_map/ppermute | solution.py:178
  90.3 9.5 %collective-permute-start.18 = (bf16[64,512]{1,0:T(8,128)(2,1)S(1)}, bf16[64,512]{1,0:T(8,128)(2,1)S(1)}, u32[]{:S(2)}, u32[]{:S(2)}) collective-permute-start(bf16[64,512]{1,0:T(8,128)(2,1)S(1)} %fusion.31), channel_id=1, source_target_pairs={{0,4},{2,6},{4,0},{6,2},{1,5},{3,7},{5,1},{7,3},{8,12},{10,14},{12... | collective-permute-start | bytes 196616 | tf_op jit(solution)/shard_map/ppermute | solution.py:178
  90.4 11.7 %collective-permute-start.25 = (f32[64,192]{1,0:T(8,128)S(1)}, f32[64,192]{1,0:T(8,128)S(1)}, u32[]{:S(2)}, u32[]{:S(2)}) collective-permute-start(f32[64,192]{1,0:T(8,128)S(1)} %add.220), channel_id=1, source_target_pairs={{0,8},{8,0},{16,24},{24,16},{1,9},{9,1},{17,25},{25,17},{2,10},{10... | collective-permute-start | bytes 147464 | tf_op jit(solution)/shard_map/ppermute | solution.py:178
  91.0 11.1 %collective-permute-start.26 = (f32[64,192]{1,0:T(8,128)S(1)}, f32[64,192]{1,0:T(8,128)S(1)}, u32[]{:S(2)}, u32[]{:S(2)}) collective-permute-start(f32[64,192]{1,0:T(8,128)S(1)} %add.220), channel_id=1, source_target_pairs={{0,16},{8,24},{16,0},{24,8},{1,17},{9,25},{17,1},{25,9},{2,18},{10... | collective-permute-start | bytes 147464 | tf_op jit(solution)/shard_map/ppermute | solution.py:178
  97.2 5.2 %collective-permute-start.27 = (f32[64,192]{1,0:T(8,128)S(1)}, f32[64,192]{1,0:T(8,128)S(1)}, u32[]{:S(2)}, u32[]{:S(2)}) collective-permute-start(f32[64,192]{1,0:T(8,128)S(1)} %add.220), channel_id=1, source_target_pairs={{0,24},{8,16},{16,8},{24,0},{1,25},{9,17},{17,9},{25,1},{2,26},{10... | collective-permute-start | bytes 147464 | tf_op jit(solution)/shard_map/ppermute | solution.py:178
  98.6 18.5 %collective-permute-start.17 = (bf16[64,1024]{1,0:T(8,128)(2,1)}, bf16[64,1024]{1,0:T(8,128)(2,1)S(1)}, u32[]{:S(2)}, u32[]{:S(2)}) collective-permute-start(bf16[64,1024]{1,0:T(8,128)(2,1)} %pad_maximum_fusion.15), channel_id=1, source_target_pairs={{0,2},{2,0},{4,6},{6,4},{1,3},{3,1},{5,7},{7,5},{8,10},{10,8},{12,... | collective-permute-start | bytes 393224 | tf_op jit(solution)/shard_map/ppermute | solution.py:178
  99.8 21.0 %collective-permute-start.11 = (bf16[64,1024]{1,0:T(8,128)(2,1)}, bf16[64,1024]{1,0:T(8,128)(2,1)S(1)}, u32[]{:S(2)}, u32[]{:S(2)}) collective-permute-start(bf16[64,1024]{1,0:T(8,128)(2,1)} %pad_maximum_fusion.13), channel_id=1, source_target_pairs={{0,2},{2,0},{4,6},{6,4},{1,3},{3,1},{5,7},{7,5},{8,10},{10,8},{12,... | collective-permute-start | bytes 393224 | tf_op jit(solution)/shard_map/ppermute | solution.py:178
  102.4 8.1 %collective-permute-start.28 = (f32[64,192]{1,0:T(8,128)S(1)}, f32[64,192]{1,0:T(8,128)S(1)}, u32[]{:S(2)}, u32[]{:S(2)}) collective-permute-start(f32[64,192]{1,0:T(8,128)S(1)} %add_add_fusion.3), channel_id=1, source_target_pairs={{0,2},{2,0},{4,6},{6,4},{1,3},{3,1},{5,7},{7,5},{8,10},{10,8},{12,... | collective-permute-start | bytes 147464 | tf_op jit(solution)/shard_map/ppermute | solution.py:178
  102.6 7.9 %collective-permute-start.29 = (f32[64,192]{1,0:T(8,128)S(1)}, f32[64,192]{1,0:T(8,128)S(1)}, u32[]{:S(2)}, u32[]{:S(2)}) collective-permute-start(f32[64,192]{1,0:T(8,128)S(1)} %add_add_fusion.3), channel_id=1, source_target_pairs={{0,4},{2,6},{4,0},{6,2},{1,5},{3,7},{5,1},{7,3},{8,12},{10,14},{12... | collective-permute-start | bytes 147464 | tf_op jit(solution)/shard_map/ppermute | solution.py:178
  104.5 8.0 %collective-permute-start.30 = (f32[64,192]{1,0:T(8,128)S(1)}, f32[64,192]{1,0:T(8,128)S(1)}, u32[]{:S(2)}, u32[]{:S(2)}) collective-permute-start(f32[64,192]{1,0:T(8,128)S(1)} %add_add_fusion.3), channel_id=1, source_target_pairs={{0,6},{2,4},{4,2},{6,0},{1,7},{3,5},{5,3},{7,1},{8,14},{10,12},{12... | collective-permute-start | bytes 147464 | tf_op jit(solution)/shard_map/ppermute | solution.py:178
  110.5 14.1 %collective-permute-start.13 = (bf16[64,1024]{1,0:T(8,128)(2,1)}, bf16[64,1024]{1,0:T(8,128)(2,1)}, u32[]{:S(2)}, u32[]{:S(2)}) collective-permute-start(bf16[64,1024]{1,0:T(8,128)(2,1)} %pad_maximum_fusion.14), channel_id=1, source_target_pairs={{0,2},{2,0},{4,6},{6,4},{1,3},{3,1},{5,7},{7,5},{8,10},{10,8},{12,... | collective-permute-start | bytes 393224 | tf_op jit(solution)/shard_map/ppermute | solution.py:178
  110.5 25.4 %collective-permute-start.19 = (bf16[64,1024]{1,0:T(8,128)(2,1)}, bf16[64,1024]{1,0:T(8,128)(2,1)S(1)}, u32[]{:S(2)}, u32[]{:S(2)}) collective-permute-start(bf16[64,1024]{1,0:T(8,128)(2,1)} %pad_maximum_fusion.16), channel_id=1, source_target_pairs={{0,2},{2,0},{4,6},{6,4},{1,3},{3,1},{5,7},{7,5},{8,10},{10,8},{12,... | collective-permute-start | bytes 393224 | tf_op jit(solution)/shard_map/ppermute | solution.py:178
  124.5 1.4 collective-permute-start.39
  125.9 6.4 %collective-permute-start.40 = (f32[64,512]{1,0:T(8,128)S(1)}, f32[64,512]{1,0:T(8,128)S(1)}, u32[]{:S(2)}, u32[]{:S(2)}) collective-permute-start(f32[64,512]{1,0:T(8,128)S(1)} %dynamic-slice_add_fusion.2), channel_id=1, source_target_pairs={{0,8},{8,0},{16,24},{24,16},{1,9},{9,1},{17,25},{25,17},{2,10},{10... | collective-permute-start | bytes 393224 | tf_op jit(solution)/shard_map/ppermute | solution.py:178
  126.6 8.1 %collective-permute-start.41 = (f32[64,512]{1,0:T(8,128)S(1)}, f32[64,512]{1,0:T(8,128)S(1)}, u32[]{:S(2)}, u32[]{:S(2)}) collective-permute-start(f32[64,512]{1,0:T(8,128)S(1)} %dynamic-slice_add_fusion.2), channel_id=1, source_target_pairs={{0,16},{8,24},{16,0},{24,8},{1,17},{9,25},{17,1},{25,9},{2,18},{10... | collective-permute-start | bytes 393224 | tf_op jit(solution)/shard_map/ppermute | solution.py:178
  127.7 7.0 %collective-permute-start.42 = (f32[64,512]{1,0:T(8,128)S(1)}, f32[64,512]{1,0:T(8,128)S(1)}, u32[]{:S(2)}, u32[]{:S(2)}) collective-permute-start(f32[64,512]{1,0:T(8,128)S(1)} %dynamic-slice_add_fusion.2), channel_id=1, source_target_pairs={{0,24},{8,16},{16,8},{24,0},{1,25},{9,17},{17,9},{25,1},{2,26},{10... | collective-permute-start | bytes 393224 | tf_op jit(solution)/shard_map/ppermute | solution.py:178
  135.8 1.3 collective-permute-start.43
  137.2 5.2 %collective-permute-start.44 = (f32[64,192]{1,0:T(8,128)S(1)}, f32[64,192]{1,0:T(8,128)S(1)}, u32[]{:S(2)}, u32[]{:S(2)}) collective-permute-start(f32[64,192]{1,0:T(8,128)S(1)} %fusion.53), channel_id=1, source_target_pairs={{0,2},{2,0},{4,6},{6,4},{1,3},{3,1},{5,7},{7,5},{8,10},{10,8},{12,... | collective-permute-start | bytes 147464 | tf_op jit(solution)/shard_map/ppermute | solution.py:178
  137.3 8.7 %collective-permute-start.45 = (f32[64,192]{1,0:T(8,128)S(1)}, f32[64,192]{1,0:T(8,128)S(1)}, u32[]{:S(2)}, u32[]{:S(2)}) collective-permute-start(f32[64,192]{1,0:T(8,128)S(1)} %fusion.53), channel_id=1, source_target_pairs={{0,4},{2,6},{4,0},{6,2},{1,5},{3,7},{5,1},{7,3},{8,12},{10,14},{12... | collective-permute-start | bytes 147464 | tf_op jit(solution)/shard_map/ppermute | solution.py:178
  139.7 6.2 %collective-permute-start.46 = (f32[64,192]{1,0:T(8,128)S(1)}, f32[64,192]{1,0:T(8,128)S(1)}, u32[]{:S(2)}, u32[]{:S(2)}) collective-permute-start(f32[64,192]{1,0:T(8,128)S(1)} %fusion.53), channel_id=1, source_target_pairs={{0,6},{2,4},{4,2},{6,0},{1,7},{3,5},{5,3},{7,1},{8,14},{10,12},{12... | collective-permute-start | bytes 147464 | tf_op jit(solution)/shard_map/ppermute | solution.py:178
  146.6 10.2 %copy-start.4 = (f32[64,2048]{1,0:T(8,128)S(1)}, f32[64,2048]{1,0:T(8,128)}, u32[]{:S(2)}) copy-start(f32[64,2048]{1,0:T(8,128)} %convert_add_fusion.1) | copy-start | bytes 1572868
  156.7 4.2 %copy-start.5 = (f32[192,128]{1,0:T(8,128)S(1)}, f32[192,128]{1,0:T(8,128)}, u32[]{:S(2)}) copy-start(f32[192,128]{1,0:T(8,128)} %get-tuple-element.5) | copy-start | bytes 294916

commit v2 on v1

--- a/solution.py
+++ b/solution.py
@@ -230,50 +230,86 @@
     )
 
 
+def probe_of_exact(rows_b, rows):
+    total = None
+    for _ in range(3):
+        part = rounded(rows)
+        rows = rows - part
+        term = probe_of(rows_b, part.astype(jnp.bfloat16))
+        total = term if total is None else total + term
+    return total
+
+
+def reordered(value, chunks):
+    rows, width = value.shape
+    devices = lax.axis_size("token")
+    piece = width // (chunks * devices)
+    pieces = [
+        [value[:, piece * (chunks * d + c) : piece * (chunks * d + c) + piece] for d in range(devices)]
+        for c in range(chunks)
+    ]
+    return jnp.concatenate([p for line in pieces for p in line], axis=1)
+
+
+def after(value, *earlier):
+    return lax.optimization_barrier((value, *earlier))[0]
+
+
 def local(hidden_slab, current_block, direction):
     tok_rows, half_width = hidden_slab.shape
     cols = current_block.shape[1]
     feat_total = half_width * lax.axis_size("layer") * lax.axis_size("fhalf")
     token_total = tok_rows * lax.axis_size("token")
+    ritz_scale = 1.0 / (token_total * feat_total)
     x_rows = current_block.T
     d_rows = direction.T
-    given_rows = jnp.concatenate([x_rows, d_rows], axis=0)
     chunk = half_width // CHUNKS
-    slabs = [hidden_slab[:, chunk * c : chunk * c + chunk] for c in range(CHUNKS)]
-    given_part = probe_of(given_rows.astype(jnp.bfloat16), hidden_slab)
+    starts = [chunk * c for c in range(CHUNKS)]
+    slabs = [hidden_slab[:, at : at + chunk] for at in starts]
+    given_b = jnp.concatenate([x_rows, d_rows], axis=0).astype(jnp.bfloat16)
+    given_part = probe_of(given_b, hidden_slab)
     x_probe = reduce_all(reduce_halves(given_part[:cols], "fhalf"), "layer")
     x_probe_b = rounded(x_probe)
     block_probe = gather_halves(x_probe_b.astype(jnp.bfloat16), "fhalf")
-    ritz_block = reduce_all(probe_of(block_probe, block_probe), "token") / (token_total * feat_total)
-    images = [
-        reduce_halves(jnp.dot(block_probe, slab, preferred_element_type=jnp.float32), "token")
-        for slab in slabs
-    ]
-    given_own = [
-        own_part(given_rows[:, chunk * c : chunk * c + chunk], "token") for c in range(CHUNKS)
-    ]
+    image_parts = [jnp.dot(block_probe, slab, preferred_element_type=jnp.float32) for slab in slabs]
+    late_probe = after(block_probe, image_parts[-1])
+    ritz_block = reduce_all(probe_of(late_probe, late_probe), "token") * ritz_scale
+    images = [reduce_halves(part, "token") for part in image_parts]
     residuals = [
-        image / token_total - exact_transposed(ritz_block, own[:cols])
-        for image, own in zip(images, given_own)
+        image / token_total
+        - exact_transposed(ritz_block, own_part(x_rows[:, at : at + chunk], "token"))
+        for image, at in zip(images, starts)
     ]
     highs = [rounded(residual) for residual in residuals]
     search = [gather_halves(high.astype(jnp.bfloat16), "token") for high in highs]
+    x_late, d_late = lax.optimization_barrier((x_rows, d_rows, image_parts[-1]))[:2]
+    gram_given = exact_rows(
+        jnp.concatenate([x_late, d_late], axis=0), jnp.concatenate([x_late, d_late], axis=0)
+    )
+    joined = jnp.concatenate([given_part[cols:], gram_given[:cols], gram_given[cols:]], axis=1)
+    joined = lax.psum(joined, ("layer", "fhalf"))
+    d_probe = joined[:, :tok_rows]
+    gram_given = jnp.concatenate(
+        [joined[:, tok_rows : tok_rows + 2 * cols], joined[:, tok_rows + 2 * cols :]], axis=0
+    )
+    given_inverse = whiten_given(gram_given / feat_total)
+    d_own = own_part(d_probe, "fhalf")
+    given_probe = jnp.concatenate([x_probe, d_own], axis=0)
+    given_probe_b = jnp.concatenate([x_probe_b, rounded(d_own)], axis=0)
     r_part = sum(probe_of(rows, slab) for rows, slab in zip(search, slabs))
-    r_probe = reduce_all(reduce_halves(r_part, "fhalf"), "layer")
-    d_half = reduce_halves(given_part[cols:], "fhalf")
-    d_probe = reduce_all(d_half, "layer")
-    gram_given = reduce_all(reduce_all(exact_rows(given_rows, given_rows), "fhalf"), "layer")
-    given_inverse = whiten_given(gram_given / feat_total)
-    given_probe = jnp.concatenate([x_probe, d_probe], axis=0)
-    given_probe_b = jnp.concatenate([x_probe_b, rounded(d_probe)], axis=0)
-    raw_given = exact_rows(given_probe, given_probe_b)
-    raw_given = reduce_all(reduce_all(raw_given, "fhalf"), "token") / (token_total * feat_total)
-    gram_rest = sum(
-        exact_rows(residual, jnp.concatenate([own, residual], axis=0))
-        for residual, own in zip(residuals, given_own)
-    )
-    gram_rest = reduce_all(reduce_all(reduce_all(gram_rest, "fhalf"), "layer"), "token")
-    rest_inverse = whiten_rest(given_inverse, gram_rest / feat_total)
+    search_rows = jnp.concatenate(search, axis=1)
+    gram_rest = jnp.concatenate(
+        [probe_of_exact(search_rows, x_rows), probe_of_exact(search_rows, d_rows),
+         probe_of(search_rows, search_rows)], axis=1
+    )
+    r_half = reduce_halves(r_part, "fhalf")
+    gram_rest = reduce_all(gram_rest, "fhalf")
+    r_joined = jnp.concatenate([r_half, gram_rest], axis=1)
+    raw_given = exact_rows(*lax.optimization_barrier((given_probe, given_probe_b, r_joined))[:2])
+    r_joined = reduce_all(r_joined, "layer")
+    r_probe = r_joined[:, : r_half.shape[1]]
+    gram_rest = r_joined[:, r_half.shape[1] :]
+    raw_given = reduce_all(reduce_all(raw_given, "fhalf"), "token") * ritz_scale
     r_probe_b = rounded(r_probe)
     raw_rest = jnp.concatenate(
         [
@@ -282,16 +318,16 @@
         ],
         axis=1,
     )
-    raw_rest = reduce_all(reduce_all(raw_rest, "fhalf"), "token") / (token_total * feat_total)
+    raw_rest = reduce_all(raw_rest, "fhalf")
+    rest_inverse = whiten_rest(given_inverse, after(gram_rest, raw_rest) / feat_total)
+    residual_lo = jnp.concatenate(
+        [(residual - high).astype(jnp.bfloat16) for residual, high in zip(residuals, highs)], axis=1
+    )
+    residual_lo = gather_halves(after(residual_lo, raw_rest), "token")
+    raw_rest = reduce_all(raw_rest, "token") * ritz_scale
     all_coeffs, ritz_values = ritz_of(given_inverse, rest_inverse, raw_given, raw_rest)
-    lows = [
-        gather_halves((residual - high).astype(jnp.bfloat16), "token")
-        for residual, high in zip(residuals, highs)
-    ]
-    residual_rows = jnp.concatenate(
-        [high.astype(jnp.float32) + low.astype(jnp.float32) for high, low in zip(search, lows)], axis=1
-    )
-    search_basis = jnp.concatenate([given_rows, residual_rows], axis=0)
+    residual_rows = search_rows.astype(jnp.float32) + reordered(residual_lo, CHUNKS).astype(jnp.float32)
+    search_basis = jnp.concatenate([x_rows, d_rows, residual_rows], axis=0)
     new_block = exact_transposed(all_coeffs[:, :cols], search_basis)
     new_direction = exact_transposed(all_coeffs[:, cols:], search_basis)
     return (new_block.T, new_direction.T, ritz_values[0])

time: 165 us -> 198 us (1.20)
  waiting for transfers between devices: 41.3 us -> 81.4 us
  starting transfers between devices: 49.9 us -> 34.1 us
  between operations: 1.15 us -> 14.7 us
  other arithmetic: 14.8 us -> 7.92 us
  local copies, waits for them, and re-layouts: 3.47 us -> 5.96 us
    psum x0 -> x1, waiting for transfers between devices: none -> 50.6 us  [local(): joined = lax.psum(joined, ('layer', 'fhalf'))]
    ppermute x47 -> x31, starting transfers between devices: 49.9 us -> 34.1 us  [swap(): lax.ppermute(value, axis, [(i, i ^ step) for i in range(lax.axis_size(axi...]
    ppermute x47 -> x31, waiting for transfers between devices: 41.3 us -> 30.9 us  [swap(): lax.ppermute(value, axis, [(i, i ^ step) for i in range(lax.axis_size(axi...]
    concatenate x4, other arithmetic: 2.65 us -> 0.05 us  [gather_halves(): jnp.concatenate([jnp.where(first, value, other), jnp.where(first, other,...]
    dot_general x7 -> x5, matrix products: 4.85 us -> 3.21 us  [exact_rows(): lax.dot_general(left, right, (((1,), (1,)), ((), ())), precision=HIGHEST,...]
    dot_general x4 -> x11, matrix products: 14.4 us -> 14 us  [probe_of(): lax.dot_general(rows_b, slab_part, (((1,), (1,)), ((), ())), preferred_el...]
  transfers between devices with their start and end apart: 47 -> 32, of which waited for: 17 -> 17; matrix products, arithmetic and copies ran while one was open for 22% -> 12% of each run, Pallas kernels for 6% -> 10%
where the time goes in v2:
time: 198 us; the launch traced here: 197 us
  waiting for transfers between devices  81.4 us (41%)
  starting transfers between devices  34.1 us (17%)
  matrix products  33.1 us (17%)
  Pallas kernels  20.2 us (10%)
  between operations  14.7 us (7%)
  other arithmetic  7.92 us (4%)
  local copies, waits for them, and re-layouts  5.96 us (3%)
    psum x1, waiting for transfers between devices, local(): joined = lax.psum(joined, ('layer', 'fhalf'))  50.6 us
    ppermute x31, starting transfers between devices, swap(): lax.ppermute(value, axis, [(i, i ^ step) for i in range(lax.axis_size(axi...  34.1 us
    ppermute x31, waiting for transfers between devices, swap(): lax.ppermute(value, axis, [(i, i ^ step) for i in range(lax.axis_size(axi...  30.9 us
    dot_general x11, matrix products, probe_of(): lax.dot_general(rows_b, slab_part, (((1,), (1,)), ((), ())), preferred_el...  14 us
    pallas_call x1, Pallas kernels, ritz_of(): pl.pallas_call(ritz_kernel, out_shape=(jax.ShapeDtypeStruct((size, 2 * co...  10.1 us
    dot_general x4, matrix products, exact_transposed(): lax.dot_general(left, right, (((0,), (0,)), ((), ())), precision=HIGHEST,...  8.93 us
    dot_general x2, matrix products, local(): jnp.dot(block_probe, slab, preferred_element_type=jnp.float32)  7.01 us
    pallas_call x1, Pallas kernels, whiten_given(): pl.pallas_call(whiten_given_kernel, out_shape=jax.ShapeDtypeStruct(gram_m...  6.04 us
  transfers between devices with their start and end apart: 32, of which 17 were waited for; matrix products, arithmetic and copies ran while one was open for 12% of the time, Pallas kernels for 10%

profile of v2, /device:TPU:0, one launch (start us, length us, event | category | flops | bytes accessed | tf_op | source)
XLA Modules:
  0.0 197.4 jit_solution(2417490330865765751)
XLA Ops:
  7.2 1.7 bitcast_convert_fusion
  8.9 6.3 %fusion.24 = f32[128,1024]{1,0:T(8,128)S(1)} fusion(bf16[1024,4096]{1,0:T(8,128)(2,1)} %param.3, bf16[64,4096]{1,0:T(8,128)(2,1)S(1)} %get-tuple-element.51, bf16[64,4096]{1,0:T(8,128)(2,1)S(1)} %get-tuple-element.52), kind=kOutput, calls=%fused_computation.34 | convolution fusion | flops 1075838976 | bytes 9961472 | tf_op jit(solution)/shard_map/dot_general | solution.py:228
  15.3 0.5 collective-permute-start
  15.9 1.0 collective-permute-done
  16.9 2.9 %collective-permute-start.1 = (f32[64,512]{1,0:T(8,128)S(1)}, f32[64,512]{1,0:T(8,128)S(1)}, u32[]{:S(2)}, u32[]{:S(2)}) collective-permute-start(f32[64,512]{1,0:T(8,128)S(1)} %dynamic-slice_add_fusion.3), channel_id=1, source_target_pairs={{0,8},{8,0},{16,24},{24,16},{1,9},{9,1},{17,25},{25,17},{2,10},{10... | collective-permute-start | bytes 393224 | tf_op jit(solution)/shard_map/ppermute | solution.py:178
  19.8 1.5 collective-permute-start.2
  21.3 2.4 %collective-permute-done.1 = f32[64,512]{1,0:T(8,128)S(1)} collective-permute-done((f32[64,512]{1,0:T(8,128)S(1)}, f32[64,512]{1,0:T(8,128)S(1)}, u32[]{:S(2)}, u32[]{:S(2)}) %collective-permute-start.1) | collective-permute-done | bytes 131104 | tf_op jit(solution)/shard_map/ppermute | solution.py:178
  23.7 4.2 %collective-permute-done.2 = f32[64,512]{1,0:T(8,128)S(1)} collective-permute-done((f32[64,512]{1,0:T(8,128)S(1)}, f32[64,512]{1,0:T(8,128)S(1)}, u32[]{:S(2)}, u32[]{:S(2)}) %collective-permute-start.2) | collective-permute-done | bytes 131104 | tf_op jit(solution)/shard_map/ppermute | solution.py:178
  28.0 1.1 fusion.77
  29.3 3.1 %fusion.2 = f32[64,2048]{1,0:T(8,128)S(1)} fusion(bf16[1024,4096]{1,0:T(8,128)(2,1)} %param.3, bf16[64,512]{1,0:T(8,128)(2,1)S(1)} %get-tuple-element.48, bf16[64,512]{1,0:T(8,128)(2,1)S(1)} %get-tuple-element.47), kind=kOutput, calls=%fused_computation.2 | convolution fusion | flops 268697600 | bytes 4849664 | tf_op jit(solution)/shard_map/dot_general | solution.py:274
  32.6 1.6 collective-permute-start.7
  34.3 2.6 %collective-permute-start.8 = (f32[64,64]{1,0:T(8,128)S(1)}, f32[64,64]{1,0:T(8,128)S(1)}, u32[]{:S(2)}, u32[]{:S(2)}) collective-permute-start(f32[64,64]{1,0:T(8,128)S(1)} %fusion.81), channel_id=1, source_target_pairs={{0,4},{2,6},{4,0},{6,2},{1,5},{3,7},{5,1},{7,3},{8,12},{10,14},{12... | collective-permute-start | bytes 49160 | tf_op jit(solution)/shard_map/ppermute | solution.py:178
  37.1 3.9 %fusion.6 = f32[64,2048]{1,0:T(8,128)} fusion(bf16[1024,4096]{1,0:T(8,128)(2,1)} %param.3, bf16[64,512]{1,0:T(8,128)(2,1)S(1)} %get-tuple-element.48, bf16[64,512]{1,0:T(8,128)(2,1)S(1)} %get-tuple-element.47), kind=kOutput, calls=%fused_computation.6 | convolution fusion | flops 268697600 | bytes 4849664 | tf_op jit(solution)/shard_map/dot_general | solution.py:274
  41.0 1.8 fusion.10
  42.8 0.8 pad_maximum_fusion.4
  43.6 0.7 constant_dynamic-slice_fusion.3
  44.3 0.7 collective-permute-start.12
  45.0 1.0 constant_dynamic-slice_fusion.5
  45.9 1.4 collective-permute-start.5
  47.4 50.6 %all-reduce.2.cloned.1.call-done = f32[64,1280]{1,0:T(8,128)} async-done(((f32[64,1280]{1,0:T(8,128)}), f32[64,1280]{1,0:T(8,128)}) %all-reduce.2.cloned.1.call-update) | async-done | bytes 327696 | tf_op jit(solution)/shard_map/psum | solution.py:290
  97.9 1.0 slice.99
  99.0 0.8 fusion.79
  99.8 0.6 maximum_multiply_fusion.gram_ref
  100.4 6.0 %whiten_given.1.given_ref = f32[128,128]{1,0:T(8,128)} custom-call(f32[128,128]{1,0:T(8,128)} %maximum_multiply_fusion.gram_ref), custom_call_target="tpu_custom_call" | custom-call | flops 4000000000 | bytes 131072 | tf_op jit(solution)/shard_map/whiten_given/pallas_call | solution.py:81
  106.5 1.1 dynamic-slice_add_fusion
  107.5 2.5 %collective-permute-start.13 = (f32[64,512]{1,0:T(8,128)S(1)}, f32[64,512]{1,0:T(8,128)S(1)}, u32[]{:S(2)}, u32[]{:S(2)}) collective-permute-start(f32[64,512]{1,0:T(8,128)S(1)} %constant_dynamic-slice_fusion.2), channel_id=1, source_target_pairs={{0,4},{2,6},{4,0},{6,2},{1,5},{3,7},{5,1},{7,3},{8,12},{10,14},{12... | collective-permute-start | bytes 393224 | tf_op jit(solution)/shard_map/ppermute | solution.py:178
  110.0 1.1 dynamic-slice_add_fusion.1
  111.1 0.6 collective-permute-start.6
  111.7 7.9 %collective-permute-done.13 = f32[64,512]{1,0:T(8,128)S(1)} collective-permute-done((f32[64,512]{1,0:T(8,128)S(1)}, f32[64,512]{1,0:T(8,128)S(1)}, u32[]{:S(2)}, u32[]{:S(2)}) %collective-permute-start.13) | collective-permute-done | bytes 131104 | tf_op jit(solution)/shard_map/ppermute | solution.py:178
  119.6 1.3 reduce-precision_convert_fusion.8
  121.0 0.6 collective-permute-done.6
  121.6 1.3 reduce-precision_convert_fusion.9
  122.9 2.4 %collective-permute-start.10 = (bf16[64,512]{1,0:T(8,128)(2,1)S(1)}, bf16[64,512]{1,0:T(8,128)(2,1)S(1)}, u32[]{:S(2)}, u32[]{:S(2)}) collective-permute-start(bf16[64,512]{1,0:T(8,128)(2,1)S(1)} %get-tuple-element.41), channel_id=1, source_target_pairs={{0,4},{2,6},{4,0},{6,2},{1,5},{3,7},{5,1},{7,3},{8,12},{10,14},{12... | collective-permute-start | bytes 196616 | tf_op jit(solution)/shard_map/ppermute | solution.py:178
  125.3 1.7 collective-permute-done.14
  127.4 1.6 collective-permute-done.10
  129.0 1.5 collective-permute-start.11
  130.5 2.3 %collective-permute-done.15 = bf16[64,1024]{1,0:T(8,128)(2,1)S(1)} collective-permute-done((bf16[64,1024]{1,0:T(8,128)(2,1)S(1)}, bf16[64,1024]{1,0:T(8,128)(2,1)S(1)}, u32[]{:S(2)}, u32[]{:S(2)}) %collective-permute-start.15) | collective-permute-done | bytes 131104 | tf_op jit(solution)/shard_map/ppermute | solution.py:178
  132.8 3.7 %fusion = f32[64,1024]{1,0:T(8,128)S(1)} fusion(bf16[1024,4096]{1,0:T(8,128)(2,1)} %param.3, bf16[64,1024]{1,0:T(8,128)(2,1)S(1)} %get-tuple-element.38, bf16[64,1024]{1,0:T(8,128)(2,1)S(1)} %get-tuple-element.37), kind=kOutput, calls=%fused_computation | convolution fusion | flops 268959744 | bytes 4718592 | tf_op jit(solution)/shard_map/dot_general | solution.py:228
  138.4 0.7 slice-done.1
  139.1 1.4 fusion.14
  141.3 0.5 collective-permute-start.16
  141.8 0.7 collective-permute-done.17
  142.9 1.4 collective-permute-start.18
  144.4 2.0 %collective-permute-start.20 = (f32[64,704]{1,0:T(8,128)S(1)}, f32[64,704]{1,0:T(8,128)S(1)}, u32[]{:S(2)}, u32[]{:S(2)}) collective-permute-start(f32[64,704]{1,0:T(8,128)S(1)} %pad_maximum_fusion.8), channel_id=1, source_target_pairs={{0,24},{8,16},{16,8},{24,0},{1,25},{9,17},{17,9},{25,1},{2,26},{10... | collective-permute-start | bytes 540680 | tf_op jit(solution)/shard_map/ppermute | solution.py:178
  146.9 1.2 collective-permute-done.24
  148.2 0.7 collective-permute-start.25
  148.9 2.8 %collective-permute-start.26 = (f32[128,128]{1,0:T(8,128)S(1)}, f32[128,128]{1,0:T(8,128)S(1)}, u32[]{:S(2)}, u32[]{:S(2)}) collective-permute-start(f32[128,128]{1,0:T(8,128)S(1)} %add.189), channel_id=1, source_target_pairs={{0,4},{2,6},{4,0},{6,2},{1,5},{3,7},{5,1},{7,3},{8,12},{10,14},{12... | collective-permute-start | bytes 196616 | tf_op jit(solution)/shard_map/ppermute | solution.py:178
  151.7 1.9 collective-permute-start.27
  153.5 1.8 collective-permute-done.19
  156.6 1.3 collective-permute-done.27
  157.8 0.6 add_multiply_fusion.1.raw_given_ref
  158.5 0.9 collective-permute-start.28
  159.4 1.6 collective-permute-start.29
  161.0 1.9 collective-permute-start.30
  163.0 0.6 broadcast_multiply_fusion.gram_ref
  163.6 0.8 collective-permute-start.22
  164.4 4.0 %whiten_rest.1.rest_ref = f32[64,192]{1,0:T(8,128)} custom-call(f32[128,128]{1,0:T(8,128)} %whiten_given.1.given_ref, f32[64,192]{1,0:T(8,128)} %broadcast_multiply_fusion.gram_ref), custom_call_target="tpu_custom_call" | custom-call | flops 3000000000 | bytes 131072 | tf_op jit(solution)/shard_map/whiten_rest/pallas_call | solution.py:98
  168.4 1.1 collective-permute-done.29
  169.5 0.6 add_multiply_fusion.raw_rest_ref
  170.2 2.8 %collective-permute-done.22 = bf16[64,1024]{1,0:T(8,128)(2,1)S(1)} collective-permute-done((bf16[64,1024]{1,0:T(8,128)(2,1)S(1)}, bf16[64,1024]{1,0:T(8,128)(2,1)S(1)}, u32[]{:S(2)}, u32[]{:S(2)}) %collective-permute-start.22) | collective-permute-done | bytes 131104 | tf_op jit(solution)/shard_map/ppermute | solution.py:178
  173.1 10.1 %ritz.1 = (f32[192,128]{1,0:T(8,128)}, f32[1,64]{1,0:T(1,128)}) custom-call(f32[128,128]{1,0:T(8,128)} %whiten_given.1.given_ref, f32[64,192]{1,0:T(8,128)} %whiten_rest.1.rest_ref, f32[128,128]{1,0:T(8,128)} %add_multiply_fusion.1.raw_given_ref, f32[64,192]{1,0:T(8,128)} %add_multiply_fusion.raw_rest_ref), custom_call_target="tpu_custom_call" | custom-call | flops 10000000000 | bytes 524288 | tf_op jit(solution)/shard_map/ritz/pallas_call | solution.py:155
  183.6 0.5 copy-done.5
  184.2 3.2 %fusion.8 = f32[4096,64]{0,1:T(8,128)} fusion(f32[64,4096]{1,0:T(8,128)S(1)} %convert_add_fusion, f32[64,4096]{1,0:T(8,128)S(1)} %bitcast.41, f32[64,4096]{1,0:T(8,128)S(1)} %bitcast.38, f32[192,128]{1,0:T(8,128)S(1)} %copy-done.5), kind=kOutput, calls=%fused_computation.9 | convolution fusion | flops 605552640 | bytes 4292608 | tf_op jit(solution)/shard_map/dot_general | solution.py:16
  187.4 3.2 %fusion.9 = f32[4096,64]{0,1:T(8,128)} fusion(f32[64,4096]{1,0:T(8,128)S(1)} %convert_add_fusion, f32[64,4096]{1,0:T(8,128)S(1)} %bitcast.42, f32[64,4096]{1,0:T(8,128)S(1)} %bitcast.39, f32[192,128]{1,0:T(8,128)S(1)} %copy-done.5), kind=kOutput, calls=%fused_computation.10 | convolution fusion | flops 605552640 | bytes 4292608 | tf_op jit(solution)/shard_map/dot_general | solution.py:16
  (99 shorter events, 6.7 us)
Async XLA Ops:
  7.2 90.8 %all-reduce.2.cloned.1.call-start = ((), (), s32[]{:S(2)}) async-start(), calls=%async_computation | async-start | bytes 655360 | tf_op jit(solution)/shard_map/psum | solution.py:290
  8.9 19.1 %copy-start = (f32[4096,64]{0,1:T(8,128)S(1)}, f32[4096,64]{0,1:T(8,128)}, u32[]{:S(2)}) copy-start(f32[4096,64]{0,1:T(8,128)} %param.4) | copy-start | bytes 3145732
  15.3 1.5 collective-permute-start
  16.9 6.8 %collective-permute-start.1 = (f32[64,512]{1,0:T(8,128)S(1)}, f32[64,512]{1,0:T(8,128)S(1)}, u32[]{:S(2)}, u32[]{:S(2)}) collective-permute-start(f32[64,512]{1,0:T(8,128)S(1)} %dynamic-slice_add_fusion.3), channel_id=1, source_target_pairs={{0,8},{8,0},{16,24},{24,16},{1,9},{9,1},{17,25},{25,17},{2,10},{10... | collective-permute-start | bytes 393224 | tf_op jit(solution)/shard_map/ppermute | solution.py:178
  19.8 8.1 %collective-permute-start.2 = (f32[64,512]{1,0:T(8,128)S(1)}, f32[64,512]{1,0:T(8,128)S(1)}, u32[]{:S(2)}, u32[]{:S(2)}) collective-permute-start(f32[64,512]{1,0:T(8,128)S(1)} %dynamic-slice_add_fusion.3), channel_id=1, source_target_pairs={{0,16},{8,24},{16,0},{24,8},{1,17},{9,25},{17,1},{25,9},{2,18},{10... | collective-permute-start | bytes 393224 | tf_op jit(solution)/shard_map/ppermute | solution.py:178
  21.3 6.6 %collective-permute-start.3 = (f32[64,512]{1,0:T(8,128)S(1)}, f32[64,512]{1,0:T(8,128)S(1)}, u32[]{:S(2)}, u32[]{:S(2)}) collective-permute-start(f32[64,512]{1,0:T(8,128)S(1)} %dynamic-slice_add_fusion.3), channel_id=1, source_target_pairs={{0,24},{8,16},{16,8},{24,0},{1,25},{9,17},{17,9},{25,1},{2,26},{10... | collective-permute-start | bytes 393224 | tf_op jit(solution)/shard_map/ppermute | solution.py:178
  27.9 1.3 collective-permute-start.4
  29.3 11.7 %copy-start.1 = (f32[4096,64]{0,1:T(8,128)S(1)}, f32[4096,64]{0,1:T(8,128)}, u32[]{:S(2)}) copy-start(f32[4096,64]{0,1:T(8,128)} %param.5) | copy-start | bytes 3145732
  32.4 11.1 %copy-start.4 = (f32[64,2048]{1,0:T(8,128)}, f32[64,2048]{1,0:T(8,128)S(1)}, u32[]{:S(2)}) copy-start(f32[64,2048]{1,0:T(8,128)S(1)} %fusion.2) | copy-start | bytes 1572868
  32.6 14.7 %collective-permute-start.7 = (f32[64,64]{1,0:T(8,128)S(1)}, f32[64,64]{1,0:T(8,128)S(1)}, u32[]{:S(2)}, u32[]{:S(2)}) collective-permute-start(f32[64,64]{1,0:T(8,128)S(1)} %fusion.81), channel_id=1, source_target_pairs={{0,2},{2,0},{4,6},{6,4},{1,3},{3,1},{5,7},{7,5},{8,10},{10,8},{12,... | collective-permute-start | bytes 49160 | tf_op jit(solution)/shard_map/ppermute | solution.py:178
  34.3 13.1 %collective-permute-start.8 = (f32[64,64]{1,0:T(8,128)S(1)}, f32[64,64]{1,0:T(8,128)S(1)}, u32[]{:S(2)}, u32[]{:S(2)}) collective-permute-start(f32[64,64]{1,0:T(8,128)S(1)} %fusion.81), channel_id=1, source_target_pairs={{0,4},{2,6},{4,0},{6,2},{1,5},{3,7},{5,1},{7,3},{8,12},{10,14},{12... | collective-permute-start | bytes 49160 | tf_op jit(solution)/shard_map/ppermute | solution.py:178
  36.9 10.5 %collective-permute-start.9 = (f32[64,64]{1,0:T(8,128)S(1)}, f32[64,64]{1,0:T(8,128)S(1)}, u32[]{:S(2)}, u32[]{:S(2)}) collective-permute-start(f32[64,64]{1,0:T(8,128)S(1)} %fusion.81), channel_id=1, source_target_pairs={{0,6},{2,4},{4,2},{6,0},{1,7},{3,5},{5,3},{7,1},{8,14},{10,12},{12... | collective-permute-start | bytes 49160 | tf_op jit(solution)/shard_map/ppermute | solution.py:178
  44.3 62.2 %collective-permute-start.12 = (f32[64,1024]{1,0:T(8,128)}, f32[64,1024]{1,0:T(8,128)}, u32[]{:S(2)}, u32[]{:S(2)}) collective-permute-start(f32[64,1024]{1,0:T(8,128)} %constant_dynamic-slice_fusion.3), channel_id=1, source_target_pairs={{0,2},{2,0},{4,6},{6,4},{1,3},{3,1},{5,7},{7,5},{8,10},{10,8},{12,... | collective-permute-start | bytes 786440 | tf_op jit(solution)/shard_map/ppermute | solution.py:178
  45.9 64.1 %collective-permute-start.5 = (f32[64,1024]{1,0:T(8,128)S(1)}, f32[64,1024]{1,0:T(8,128)}, u32[]{:S(2)}, u32[]{:S(2)}) collective-permute-start(f32[64,1024]{1,0:T(8,128)S(1)} %constant_dynamic-slice_fusion.5), channel_id=1, source_target_pairs={{0,2},{2,0},{4,6},{6,4},{1,3},{3,1},{5,7},{7,5},{8,10},{10,8},{12,... | collective-permute-start | bytes 786440 | tf_op jit(solution)/shard_map/ppermute | solution.py:178
  107.5 12.1 %collective-permute-start.13 = (f32[64,512]{1,0:T(8,128)S(1)}, f32[64,512]{1,0:T(8,128)S(1)}, u32[]{:S(2)}, u32[]{:S(2)}) collective-permute-start(f32[64,512]{1,0:T(8,128)S(1)} %constant_dynamic-slice_fusion.2), channel_id=1, source_target_pairs={{0,4},{2,6},{4,0},{6,2},{1,5},{3,7},{5,1},{7,3},{8,12},{10,14},{12... | collective-permute-start | bytes 393224 | tf_op jit(solution)/shard_map/ppermute | solution.py:178
  111.1 10.5 %collective-permute-start.6 = (f32[64,512]{1,0:T(8,128)S(1)}, f32[64,512]{1,0:T(8,128)S(1)}, u32[]{:S(2)}, u32[]{:S(2)}) collective-permute-start(f32[64,512]{1,0:T(8,128)S(1)} %constant_dynamic-slice_fusion.4), channel_id=1, source_target_pairs={{0,4},{2,6},{4,0},{6,2},{1,5},{3,7},{5,1},{7,3},{8,12},{10,14},{12... | collective-permute-start | bytes 393224 | tf_op jit(solution)/shard_map/ppermute | solution.py:178
  120.9 6.0 %collective-permute-start.14 = (bf16[64,512]{1,0:T(8,128)(2,1)S(1)}, bf16[64,512]{1,0:T(8,128)(2,1)S(1)}, u32[]{:S(2)}, u32[]{:S(2)}) collective-permute-start(bf16[64,512]{1,0:T(8,128)(2,1)S(1)} %get-tuple-element.45), channel_id=1, source_target_pairs={{0,4},{2,6},{4,0},{6,2},{1,5},{3,7},{5,1},{7,3},{8,12},{10,14},{12... | collective-permute-start | bytes 196616 | tf_op jit(solution)/shard_map/ppermute | solution.py:178
  122.9 6.0 %collective-permute-start.10 = (bf16[64,512]{1,0:T(8,128)(2,1)S(1)}, bf16[64,512]{1,0:T(8,128)(2,1)S(1)}, u32[]{:S(2)}, u32[]{:S(2)}) collective-permute-start(bf16[64,512]{1,0:T(8,128)(2,1)S(1)} %get-tuple-element.41), channel_id=1, source_target_pairs={{0,4},{2,6},{4,0},{6,2},{1,5},{3,7},{5,1},{7,3},{8,12},{10,14},{12... | collective-permute-start | bytes 196616 | tf_op jit(solution)/shard_map/ppermute | solution.py:178
  127.0 5.8 %collective-permute-start.15 = (bf16[64,1024]{1,0:T(8,128)(2,1)S(1)}, bf16[64,1024]{1,0:T(8,128)(2,1)S(1)}, u32[]{:S(2)}, u32[]{:S(2)}) collective-permute-start(bf16[64,1024]{1,0:T(8,128)(2,1)S(1)} %pad_maximum_fusion.11), channel_id=1, source_target_pairs={{0,2},{2,0},{4,6},{6,4},{1,3},{3,1},{5,7},{7,5},{8,10},{10,8},{12,... | collective-permute-start | bytes 393224 | tf_op jit(solution)/shard_map/ppermute | solution.py:178
  129.0 7.6 %collective-permute-start.11 = (bf16[64,1024]{1,0:T(8,128)(2,1)S(1)}, bf16[64,1024]{1,0:T(8,128)(2,1)S(1)}, u32[]{:S(2)}, u32[]{:S(2)}) collective-permute-start(bf16[64,1024]{1,0:T(8,128)(2,1)S(1)} %pad_maximum_fusion.10), channel_id=1, source_target_pairs={{0,2},{2,0},{4,6},{6,4},{1,3},{3,1},{5,7},{7,5},{8,10},{10,8},{12,... | collective-permute-start | bytes 393224 | tf_op jit(solution)/shard_map/ppermute | solution.py:178
  132.8 5.6 %slice-start = ((s8[8388608]{0:T(1024)(128)(4,1)}), s8[4194304]{0:T(1024)(128)(4,1)S(1)}, s32[]{:S(2)}) async-start(s8[8388608]{0:T(1024)(128)(4,1)} %bitcast.43), calls=%async_computation.1 | async-start | bytes 8388608
  136.6 4.2 %copy-start.2 = (bf16[64,1024]{1,0:T(8,128)(2,1)}, bf16[64,1024]{1,0:T(8,128)(2,1)S(1)}, u32[]{:S(2)}) copy-start(bf16[64,1024]{1,0:T(8,128)(2,1)S(1)} %get-tuple-element.36) | copy-start | bytes 393220
  136.9 2.2 %slice-start.1 = ((s8[8388608]{0:T(1024)(128)(4,1)}), s8[4194304]{0:T(1024)(128)(4,1)S(1)}, s32[]{:S(2)}) async-start(s8[8388608]{0:T(1024)(128)(4,1)} %bitcast.43), calls=%async_computation.2 | async-start | bytes 8388608
  141.2 1.3 collective-permute-start.17
  141.3 1.5 collective-permute-start.16
  142.9 8.8 %collective-permute-start.18 = (f32[64,704]{1,0:T(8,128)S(1)}, f32[64,704]{1,0:T(8,128)S(1)}, u32[]{:S(2)}, u32[]{:S(2)}) collective-permute-start(f32[64,704]{1,0:T(8,128)S(1)} %pad_maximum_fusion.8), channel_id=1, source_target_pairs={{0,8},{8,0},{16,24},{24,16},{1,9},{9,1},{17,25},{25,17},{2,10},{10... | collective-permute-start | bytes 540680 | tf_op jit(solution)/shard_map/ppermute | solution.py:178
  144.2 11.1 %collective-permute-start.19 = (f32[64,704]{1,0:T(8,128)S(1)}, f32[64,704]{1,0:T(8,128)S(1)}, u32[]{:S(2)}, u32[]{:S(2)}) collective-permute-start(f32[64,704]{1,0:T(8,128)S(1)} %pad_maximum_fusion.8), channel_id=1, source_target_pairs={{0,16},{8,24},{16,0},{24,8},{1,17},{9,25},{17,1},{25,9},{2,18},{10... | collective-permute-start | bytes 540680 | tf_op jit(solution)/shard_map/ppermute | solution.py:178
  144.4 10.9 %collective-permute-start.20 = (f32[64,704]{1,0:T(8,128)S(1)}, f32[64,704]{1,0:T(8,128)S(1)}, u32[]{:S(2)}, u32[]{:S(2)}) collective-permute-start(f32[64,704]{1,0:T(8,128)S(1)} %pad_maximum_fusion.8), channel_id=1, source_target_pairs={{0,24},{8,16},{16,8},{24,0},{1,25},{9,17},{17,9},{25,1},{2,26},{10... | collective-permute-start | bytes 540680 | tf_op jit(solution)/shard_map/ppermute | solution.py:178
  146.8 1.3 collective-permute-start.24
  148.2 8.4 %collective-permute-start.25 = (f32[128,128]{1,0:T(8,128)S(1)}, f32[128,128]{1,0:T(8,128)S(1)}, u32[]{:S(2)}, u32[]{:S(2)}) collective-permute-start(f32[128,128]{1,0:T(8,128)S(1)} %add.189), channel_id=1, source_target_pairs={{0,2},{2,0},{4,6},{6,4},{1,3},{3,1},{5,7},{7,5},{8,10},{10,8},{12,... | collective-permute-start | bytes 196616 | tf_op jit(solution)/shard_map/ppermute | solution.py:178
  148.9 7.7 %collective-permute-start.26 = (f32[128,128]{1,0:T(8,128)S(1)}, f32[128,128]{1,0:T(8,128)S(1)}, u32[]{:S(2)}, u32[]{:S(2)}) collective-permute-start(f32[128,128]{1,0:T(8,128)S(1)} %add.189), channel_id=1, source_target_pairs={{0,4},{2,6},{4,0},{6,2},{1,5},{3,7},{5,1},{7,3},{8,12},{10,14},{12... | collective-permute-start | bytes 196616 | tf_op jit(solution)/shard_map/ppermute | solution.py:178
  151.7 6.2 %collective-permute-start.27 = (f32[128,128]{1,0:T(8,128)S(1)}, f32[128,128]{1,0:T(8,128)S(1)}, u32[]{:S(2)}, u32[]{:S(2)}) collective-permute-start(f32[128,128]{1,0:T(8,128)S(1)} %add.189), channel_id=1, source_target_pairs={{0,6},{2,4},{4,2},{6,0},{1,7},{3,5},{5,3},{7,1},{8,14},{10,12},{12... | collective-permute-start | bytes 196616 | tf_op jit(solution)/shard_map/ppermute | solution.py:178
  156.5 2.0 %collective-permute-start.21 = (f32[64,192]{1,0:T(8,128)S(1)}, f32[64,192]{1,0:T(8,128)S(1)}, u32[]{:S(2)}, u32[]{:S(2)}) collective-permute-start(f32[64,192]{1,0:T(8,128)S(1)} %pad_maximum_fusion.14), channel_id=1, source_target_pairs={{0,1},{1,0},{2,3},{3,2},{4,5},{5,4},{6,7},{7,6},{8,9},{9,8},{10,11... | collective-permute-start | bytes 147464 | tf_op jit(solution)/shard_map/ppermute | solution.py:178
  158.5 9.9 %collective-permute-start.28 = (f32[64,192]{1,0:T(8,128)S(1)}, f32[64,192]{1,0:T(8,128)S(1)}, u32[]{:S(2)}, u32[]{:S(2)}) collective-permute-start(f32[64,192]{1,0:T(8,128)S(1)} %fusion.73), channel_id=1, source_target_pairs={{0,2},{2,0},{4,6},{6,4},{1,3},{3,1},{5,7},{7,5},{8,10},{10,8},{12,... | collective-permute-start | bytes 147464 | tf_op jit(solution)/shard_map/ppermute | solution.py:178
  159.4 10.1 %collective-permute-start.29 = (f32[64,192]{1,0:T(8,128)S(1)}, f32[64,192]{1,0:T(8,128)S(1)}, u32[]{:S(2)}, u32[]{:S(2)}) collective-permute-start(f32[64,192]{1,0:T(8,128)S(1)} %fusion.73), channel_id=1, source_target_pairs={{0,4},{2,6},{4,0},{6,2},{1,5},{3,7},{5,1},{7,3},{8,12},{10,14},{12... | collective-permute-start | bytes 147464 | tf_op jit(solution)/shard_map/ppermute | solution.py:178
  161.0 8.5 %collective-permute-start.30 = (f32[64,192]{1,0:T(8,128)S(1)}, f32[64,192]{1,0:T(8,128)S(1)}, u32[]{:S(2)}, u32[]{:S(2)}) collective-permute-start(f32[64,192]{1,0:T(8,128)S(1)} %fusion.73), channel_id=1, source_target_pairs={{0,6},{2,4},{4,2},{6,0},{1,7},{3,5},{5,3},{7,1},{8,14},{10,12},{12... | collective-permute-start | bytes 147464 | tf_op jit(solution)/shard_map/ppermute | solution.py:178
  163.6 9.4 %collective-permute-start.22 = (bf16[64,1024]{1,0:T(8,128)(2,1)S(1)}, bf16[64,1024]{1,0:T(8,128)(2,1)S(1)}, u32[]{:S(2)}, u32[]{:S(2)}) collective-permute-start(bf16[64,1024]{1,0:T(8,128)(2,1)S(1)} %pad_maximum_fusion.12), channel_id=1, source_target_pairs={{0,4},{2,6},{4,0},{6,2},{1,5},{3,7},{5,1},{7,3},{8,12},{10,14},{12... | collective-permute-start | bytes 393224 | tf_op jit(solution)/shard_map/ppermute | solution.py:178
  173.1 10.5 %copy-start.3 = (bf16[64,1024]{1,0:T(8,128)(2,1)S(1)}, bf16[64,1024]{1,0:T(8,128)(2,1)}, u32[]{:S(2)}) copy-start(bf16[64,1024]{1,0:T(8,128)(2,1)} %copy-done.2) | copy-start | bytes 393220
  173.1 10.2 %collective-permute-start.23 = (bf16[64,2048]{1,0:T(8,128)(2,1)S(1)}, bf16[64,2048]{1,0:T(8,128)(2,1)S(1)}, u32[]{:S(2)}, u32[]{:S(2)}) collective-permute-start(bf16[64,2048]{1,0:T(8,128)(2,1)S(1)} %pad_maximum_fusion.7), channel_id=1, source_target_pairs={{0,2},{2,0},{4,6},{6,4},{1,3},{3,1},{5,7},{7,5},{8,10},{10,8},{12,... | collective-permute-start | bytes 786440 | tf_op jit(solution)/shard_map/ppermute | solution.py:178
  183.3 0.9 copy-start.5
Sparse Core Ops, SparseCore 0:
  43.7 54.2 all-reduce.1

commit v3 on v2

--- a/solution.py
+++ b/solution.py
@@ -122,10 +122,15 @@
     power_ref[...] = product(power_ref[...], matrix_ref[...])
 
     def sweep(step_ref, count):
-        basis_ref[...] = identity(size, cols)
-
-        def turn(_, good):
-            turned_ref[...] = product(step_ref[...], basis_ref[...])
+        def turn(number, good):
+            @pl.when(number == 0)
+            def _():
+                turned_ref[...] = step_ref[:, :cols]
+
+            @pl.when(number > 0)
+            def _():
+                turned_ref[...] = product(step_ref[...], basis_ref[...])
+
             turned = turned_ref[...]
             inverse, low, high, total = factor_inverse(exact_transposed(turned, turned))
             basis_ref[...] = exact_rows(turned_ref[...], inverse)
@@ -144,10 +149,9 @@
         basis_ref[...] * product(matrix_ref[...], basis_ref[...]), axis=0, keepdims=True
     )
     down = lax.broadcasted_iota(jnp.int32, (size, cols), 0)
-    coeffs_ref[:, :cols] = exact_transposed(whiten_ref[...], basis_ref[...])
-    coeffs_ref[:, cols:] = exact_transposed(
-        whiten_ref[...], jnp.where(down >= cols, basis_ref[...], 0.0)
-    )
+    power_ref[:, :cols] = basis_ref[...]
+    power_ref[:, cols : 2 * cols] = jnp.where(down >= cols, basis_ref[...], 0.0)
+    coeffs_ref[...] = exact_transposed(whiten_ref[...], power_ref[:, : 2 * cols])
 
 
 def ritz_of(given, rest, raw_given, raw_rest):
@@ -174,6 +178,16 @@
     return lax.reduce_precision(value, exponent_bits=8, mantissa_bits=7)
 
 
+def moved(coeffs, rows):
+    return lax.dot_general(
+        coeffs,
+        rows,
+        (((0,), (0,)), ((), ())),
+        precision=lax.Precision.HIGH,
+        preferred_element_type=jnp.float32,
+    )
+
+
 def swap(value, axis, step):
     return lax.ppermute(value, axis, [(i, i ^ step) for i in range(lax.axis_size(axis))])
 
@@ -199,28 +213,37 @@
     return (lax.axis_index(axis) // step) % 2
 
 
+def sent_half(value, axis, step):
+    half = value.shape[1] // 2
+    return lax.dynamic_slice_in_dim(value, (1 - side_of(axis, step)) * half, half, 1)
+
+
+def kept_half(value, axis, step):
+    half = value.shape[1] // 2
+    return lax.dynamic_slice_in_dim(value, side_of(axis, step) * half, half, 1)
+
+
 def reduce_halves(value, axis):
     for step in steps_of(axis):
-        half = value.shape[1] // 2
-        side = side_of(axis, step)
-        kept = lax.dynamic_slice_in_dim(value, side * half, half, 1)
-        sent = lax.dynamic_slice_in_dim(value, (1 - side) * half, half, 1)
-        value = kept + swap(sent, axis, step)
+        value = kept_half(value, axis, step) + swap(sent_half(value, axis, step), axis, step)
     return value
 
 
 def own_part(value, axis):
     for step in steps_of(axis):
-        half = value.shape[1] // 2
-        value = lax.dynamic_slice_in_dim(value, side_of(axis, step) * half, half, 1)
+        value = kept_half(value, axis, step)
     return value
+
+
+def joined_halves(value, axis, step):
+    other = swap(value, axis, step)
+    first = side_of(axis, step) == 0
+    return jnp.concatenate([jnp.where(first, value, other), jnp.where(first, other, value)], axis=1)
 
 
 def gather_halves(value, axis):
     for step in reversed(steps_of(axis)):
-        other = swap(value, axis, step)
-        first = side_of(axis, step) == 0
-        value = jnp.concatenate([jnp.where(first, value, other), jnp.where(first, other, value)], axis=1)
+        value = joined_halves(value, axis, step)
     return value
 
 
@@ -228,16 +251,6 @@
     return lax.dot_general(
         rows_b, slab_part, (((1,), (1,)), ((), ())), preferred_element_type=jnp.float32
     )
-
-
-def probe_of_exact(rows_b, rows):
-    total = None
-    for _ in range(3):
-        part = rounded(rows)
-        rows = rows - part
-        term = probe_of(rows_b, part.astype(jnp.bfloat16))
-        total = term if total is None else total + term
-    return total
 
 
 def reordered(value, chunks):
@@ -266,70 +279,120 @@
     chunk = half_width // CHUNKS
     starts = [chunk * c for c in range(CHUNKS)]
     slabs = [hidden_slab[:, at : at + chunk] for at in starts]
-    given_b = jnp.concatenate([x_rows, d_rows], axis=0).astype(jnp.bfloat16)
-    given_part = probe_of(given_b, hidden_slab)
+    given_rows = jnp.concatenate([x_rows, d_rows], axis=0)
+    given_hi = rounded(given_rows)
+    given_b = given_hi.astype(jnp.bfloat16)
+    given_lo = (given_rows - given_hi).astype(jnp.bfloat16)
+    given_part = probe_of(jnp.concatenate([given_b, given_lo[:cols]], axis=0), hidden_slab)
     x_probe = reduce_all(reduce_halves(given_part[:cols], "fhalf"), "layer")
     x_probe_b = rounded(x_probe)
     block_probe = gather_halves(x_probe_b.astype(jnp.bfloat16), "fhalf")
-    image_parts = [jnp.dot(block_probe, slab, preferred_element_type=jnp.float32) for slab in slabs]
-    late_probe = after(block_probe, image_parts[-1])
-    ritz_block = reduce_all(probe_of(late_probe, late_probe), "token") * ritz_scale
-    images = [reduce_halves(part, "token") for part in image_parts]
+    token_steps = steps_of("token")
+    parts, sents = [], []
+    for slab in slabs:
+        probe = after(block_probe, sents[-1]) if sents else block_probe
+        part = jnp.dot(probe, slab, preferred_element_type=jnp.float32)
+        sent = sent_half(part, "token", token_steps[0])
+        if not parts:
+            ritz_block = probe_of(block_probe, block_probe)
+            sent = jnp.concatenate([sent, ritz_block], axis=1)
+        parts.append(part)
+        sents.append(sent)
+    for number, step in enumerate(token_steps):
+        images = []
+        for c in range(CHUNKS):
+            got = swap(sents[c], "token", step)
+            if c == 0:
+                ritz_block = ritz_block + got[:, got.shape[1] - cols :]
+                got = got[:, : got.shape[1] - cols]
+            images.append(kept_half(parts[c], "token", step) + got)
+        parts = images
+        if number + 1 < len(token_steps):
+            sents = [sent_half(part, "token", token_steps[number + 1]) for part in parts]
+            sents[0] = jnp.concatenate([sents[0], ritz_block], axis=1)
+        if number == 0:
+            d_part, late_rows = lax.optimization_barrier((given_part[cols:], given_rows, sents[0]))[:2]
+            gram_given = exact_rows(late_rows, late_rows)
+            gram_given = jnp.concatenate([gram_given[:cols], gram_given[cols:]], axis=1)
+            near = steps_of("fhalf")[0]
+            joined_sent, joined_kept = (
+                jnp.concatenate([half[:cols], half[cols:], gram_given], axis=1)
+                for half in (sent_half(d_part, "fhalf", near), kept_half(d_part, "fhalf", near))
+            )
+            joined = joined_kept + swap(joined_sent, "fhalf", near)
+            joined = after(joined, *sents)
+    ritz_block = ritz_block * ritz_scale
     residuals = [
         image / token_total
         - exact_transposed(ritz_block, own_part(x_rows[:, at : at + chunk], "token"))
         for image, at in zip(images, starts)
     ]
     highs = [rounded(residual) for residual in residuals]
-    search = [gather_halves(high.astype(jnp.bfloat16), "token") for high in highs]
-    x_late, d_late = lax.optimization_barrier((x_rows, d_rows, image_parts[-1]))[:2]
-    gram_given = exact_rows(
-        jnp.concatenate([x_late, d_late], axis=0), jnp.concatenate([x_late, d_late], axis=0)
-    )
-    joined = jnp.concatenate([given_part[cols:], gram_given[:cols], gram_given[cols:]], axis=1)
-    joined = lax.psum(joined, ("layer", "fhalf"))
-    d_probe = joined[:, :tok_rows]
-    gram_given = jnp.concatenate(
-        [joined[:, tok_rows : tok_rows + 2 * cols], joined[:, tok_rows + 2 * cols :]], axis=0
-    )
-    given_inverse = whiten_given(gram_given / feat_total)
-    d_own = own_part(d_probe, "fhalf")
-    given_probe = jnp.concatenate([x_probe, d_own], axis=0)
-    given_probe_b = jnp.concatenate([x_probe_b, rounded(d_own)], axis=0)
+    high_b = [high.astype(jnp.bfloat16) for high in highs]
+    search = [gather_halves(high, "token") for high in high_b]
+    joined = reduce_all(joined, "layer")
     r_part = sum(probe_of(rows, slab) for rows, slab in zip(search, slabs))
     search_rows = jnp.concatenate(search, axis=1)
     gram_rest = jnp.concatenate(
-        [probe_of_exact(search_rows, x_rows), probe_of_exact(search_rows, d_rows),
-         probe_of(search_rows, search_rows)], axis=1
-    )
-    r_half = reduce_halves(r_part, "fhalf")
-    gram_rest = reduce_all(gram_rest, "fhalf")
-    r_joined = jnp.concatenate([r_half, gram_rest], axis=1)
-    raw_given = exact_rows(*lax.optimization_barrier((given_probe, given_probe_b, r_joined))[:2])
+        [
+            probe_of(search_rows, given_b) + probe_of(search_rows, given_lo),
+            probe_of(search_rows, search_rows),
+        ],
+        axis=1,
+    )
+    step = steps_of("fhalf")[0]
+    r_sent = jnp.concatenate([sent_half(r_part, "fhalf", step), gram_rest], axis=1)
+    r_kept = jnp.concatenate([kept_half(r_part, "fhalf", step), gram_rest], axis=1)
+    r_joined = r_kept + swap(r_sent, "fhalf", step)
+    joined = after(joined, r_joined)
+    half_rows = tok_rows // 2
+    d_probe = joined[:, :half_rows]
+    x_full = x_probe + joined[:, half_rows : 2 * half_rows]
+    gram_given = joined[:, 2 * half_rows :]
+    gram_given = jnp.concatenate([gram_given[:, : 2 * cols], gram_given[:, 2 * cols :]], axis=0)
+    given_inverse = whiten_given(gram_given / feat_total)
+    given_probe = jnp.concatenate([x_full, d_probe], axis=0)
+    given_probe_b = jnp.concatenate([x_probe_b, rounded(d_probe)], axis=0)
+    raw_given = exact_rows(given_probe, given_probe_b)
+    raw_given = jnp.concatenate([raw_given[:cols], raw_given[cols:]], axis=1)
+    residual_lo = jnp.concatenate(
+        [(residual - high).astype(jnp.bfloat16) for residual, high in zip(residuals, highs)], axis=1
+    )
+    residual_lo = after(residual_lo, r_part)
     r_joined = reduce_all(r_joined, "layer")
-    r_probe = r_joined[:, : r_half.shape[1]]
-    gram_rest = r_joined[:, r_half.shape[1] :]
-    raw_given = reduce_all(reduce_all(raw_given, "fhalf"), "token") * ritz_scale
+    r_probe = r_joined[:, :half_rows]
+    gram_rest = r_joined[:, half_rows:]
     r_probe_b = rounded(r_probe)
-    raw_rest = jnp.concatenate(
+    raw = jnp.concatenate(
         [
             0.5 * (exact_rows(r_probe, given_probe_b) + exact_rows(r_probe_b, given_probe)),
             exact_rows(r_probe, r_probe_b),
+            raw_given,
         ],
         axis=1,
     )
-    raw_rest = reduce_all(raw_rest, "fhalf")
-    rest_inverse = whiten_rest(given_inverse, after(gram_rest, raw_rest) / feat_total)
-    residual_lo = jnp.concatenate(
-        [(residual - high).astype(jnp.bfloat16) for residual, high in zip(residuals, highs)], axis=1
-    )
-    residual_lo = gather_halves(after(residual_lo, raw_rest), "token")
-    raw_rest = reduce_all(raw_rest, "token") * ritz_scale
+    near = steps_of("fhalf")[0]
+    side = side_of("fhalf", near)
+    raw = lax.dynamic_slice_in_dim(raw, side * (cols // 2), cols // 2, 0) + swap(
+        lax.dynamic_slice_in_dim(raw, (1 - side) * (cols // 2), cols // 2, 0), "fhalf", near
+    )
+    rest_inverse = whiten_rest(given_inverse, after(gram_rest, raw) / feat_total)
+    raw = reduce_all(raw, "token") * ritz_scale
+    other = swap(raw, "fhalf", near)
+    raw = jnp.concatenate(
+        [jnp.where(side == 0, raw, other), jnp.where(side == 0, other, raw)], axis=0
+    )
+    raw_rest = raw[:, : 3 * cols]
+    raw_given = jnp.concatenate([raw[:, 3 * cols : 5 * cols], raw[:, 5 * cols :]], axis=0)
     all_coeffs, ritz_values = ritz_of(given_inverse, rest_inverse, raw_given, raw_rest)
+    for step in reversed(token_steps):
+        if step == token_steps[0]:
+            residual_lo = after(residual_lo, raw)
+        residual_lo = joined_halves(residual_lo, "token", step)
     residual_rows = search_rows.astype(jnp.float32) + reordered(residual_lo, CHUNKS).astype(jnp.float32)
     search_basis = jnp.concatenate([x_rows, d_rows, residual_rows], axis=0)
-    new_block = exact_transposed(all_coeffs[:, :cols], search_basis)
-    new_direction = exact_transposed(all_coeffs[:, cols:], search_basis)
+    new_block = moved(all_coeffs[:, :cols], search_basis)
+    new_direction = moved(all_coeffs[:, cols:], search_basis)
     return (new_block.T, new_direction.T, ritz_values[0])
 
 

time: 198 us -> 131 us (0.66)
  waiting for transfers between devices: 81.4 us -> 47.4 us
  between operations: 14.7 us -> 1.46 us
  matrix products: 33.1 us -> 25.9 us
  starting transfers between devices: 34.1 us -> 27.3 us
  local copies, waits for them, and re-layouts: 5.96 us -> 1.41 us
    psum x1 -> x0, waiting for transfers between devices: 50.6 us -> none  [local(): joined = lax.psum(joined, ('layer', 'fhalf'))]
    ppermute x31 -> x28, waiting for transfers between devices: 30.9 us -> 47.4 us  [swap(): lax.ppermute(value, axis, [(i, i ^ step) for i in range(lax.axis_size(axi...]
    dot_general x4 -> x2, matrix products: 8.93 us -> 0.77 us  [exact_transposed(): lax.dot_general(left, right, (((0,), (0,)), ((), ())), precision=HIGHEST,...]
    ppermute x31 -> x28, starting transfers between devices: 34.1 us -> 27.3 us  [swap(): lax.ppermute(value, axis, [(i, i ^ step) for i in range(lax.axis_size(axi...]
    dot_general x2 -> x4, matrix products: 7.01 us -> 11.4 us  [the longest x2 6.21 us: local(): part = jnp.dot(probe, slab, preferred_element_type=jnp.float32)]
    dot_general x11 -> x7, matrix products: 14 us -> 10.5 us  [probe_of(): lax.dot_general(rows_b, slab_part, (((1,), (1,)), ((), ())), preferred_el...]
    concatenate x9 -> x12, other arithmetic: 0.94 us -> 3.43 us  [the longest x1 1.95 us: local(): given_rows = jnp.concatenate([x_rows, d_rows], axis=0)]
    add x7, other arithmetic: 2.25 us -> 0.18 us  [the longest x2 0.07 us: local(): images.append(kept_half(parts[c], 'token', step) + got)]
  transfers between devices with their start and end apart: 32 -> 28, of which waited for: 17 -> 16; matrix products, arithmetic and copies ran while one was open for 12% -> 9% of each run, Pallas kernels for 10% -> 8%
where the time goes in v3:
time: 131 us; the launch traced here: 130 us
  waiting for transfers between devices  47.4 us (36%)
  starting transfers between devices  27.3 us (21%)
  matrix products  25.9 us (20%)
  Pallas kernels  19.5 us (15%)
  other arithmetic  7.43 us (6%)
  between operations  1.46 us (1%)
  local copies, waits for them, and re-layouts  1.41 us (1%)
    ppermute x28, waiting for transfers between devices, swap(): lax.ppermute(value, axis, [(i, i ^ step) for i in range(lax.axis_size(axi...  47.4 us
    ppermute x28, starting transfers between devices, swap(): lax.ppermute(value, axis, [(i, i ^ step) for i in range(lax.axis_size(axi...  27.3 us
    dot_general x7, matrix products, probe_of(): lax.dot_general(rows_b, slab_part, (((1,), (1,)), ((), ())), preferred_el...  10.5 us
    pallas_call x1, Pallas kernels, ritz_of(): pl.pallas_call(ritz_kernel, out_shape=(jax.ShapeDtypeStruct((size, 2 * co...  9.29 us
    dot_general x2, matrix products, local(): part = jnp.dot(probe, slab, preferred_element_type=jnp.float32)  6.21 us
    pallas_call x1, Pallas kernels, whiten_given(): pl.pallas_call(whiten_given_kernel, out_shape=jax.ShapeDtypeStruct(gram_m...  6.21 us
    dot_general x2, matrix products, moved(): lax.dot_general(coeffs, rows, (((0,), (0,)), ((), ())), precision=lax.Pre...  5.2 us
    pallas_call x1, Pallas kernels, whiten_rest(): pl.pallas_call(whiten_rest_kernel, out_shape=jax.ShapeDtypeStruct(gram_ro...  3.99 us
  transfers between devices with their start and end apart: 28, of which 16 were waited for; matrix products, arithmetic and copies ran while one was open for 9% of the time, Pallas kernels for 8%

profile of v3, /device:TPU:0, one launch (start us, length us, event | category | flops | bytes accessed | tf_op | source)
XLA Modules:
  0.0 130.3 jit_solution(4673376683657896157)
XLA Ops:
  0.6 1.9 %pad_maximum_fusion.3 = (f32[128,4096]{1,0:T(8,128)S(1)}, bf16[128,4096]{1,0:T(8,128)(2,1)S(1)}, bf16[128,4096]{1,0:T(8,128)(2,1)S(1)}) fusion(f32[64,4096]{1,0:T(8,128)} %bitcast.13, f32[64,4096]{1,0:T(8,128)} %bitcast.9), kind=kLoop, calls=%fused_computation.14 | loop fusion | flops 2621440 | bytes 6291456 | tf_op jit(solution)/shard_map/concatenate | solution.py:282
  2.6 0.9 copy-done.2
  3.6 6.3 %fusion.11 = f32[192,1024]{1,0:T(8,128)S(1)} fusion(bf16[1024,4096]{1,0:T(8,128)(2,1)} %param.3, bf16[64,4096]{1,0:T(8,128)(2,1)S(1)} %slice.155, bf16[128,4096]{1,0:T(8,128)(2,1)S(1)} %get-tuple-element.26), kind=kOutput, calls=%fused_computation.15 | convolution fusion | flops 1613758464 | bytes 10747904 | tf_op jit(solution)/shard_map/dot_general | solution.py:251
  10.0 0.5 collective-permute-start
  10.5 1.0 collective-permute-done
  11.5 3.9 %collective-permute-start.3 = (f32[64,512]{1,0:T(8,128)S(1)}, f32[64,512]{1,0:T(8,128)S(1)}, u32[]{:S(2)}, u32[]{:S(2)}) collective-permute-start(f32[64,512]{1,0:T(8,128)S(1)} %dynamic-slice_add_fusion.1), channel_id=1, source_target_pairs={{0,24},{8,16},{16,8},{24,0},{1,25},{9,17},{17,9},{25,1},{2,26},{10... | collective-permute-start | bytes 393224 | tf_op jit(solution)/shard_map/ppermute | solution.py:192
  15.4 0.5 collective-permute-start.2
  15.9 0.1 collective-permute-start.1
  16.0 3.3 %collective-permute-done.3 = f32[64,512]{1,0:T(8,128)S(1)} collective-permute-done((f32[64,512]{1,0:T(8,128)S(1)}, f32[64,512]{1,0:T(8,128)S(1)}, u32[]{:S(2)}, u32[]{:S(2)}) %collective-permute-start.3) | collective-permute-done | bytes 131104 | tf_op jit(solution)/shard_map/ppermute | solution.py:192
  19.3 2.7 %collective-permute-done.2 = f32[64,512]{1,0:T(8,128)S(1)} collective-permute-done((f32[64,512]{1,0:T(8,128)S(1)}, f32[64,512]{1,0:T(8,128)S(1)}, u32[]{:S(2)}, u32[]{:S(2)}) %collective-permute-start.2) | collective-permute-done | bytes 131104 | tf_op jit(solution)/shard_map/ppermute | solution.py:192
  22.0 0.3 collective-permute-done.1
  22.5 1.2 collective-permute-done.4
  23.7 0.2 fusion.69
  23.9 3.0 %fusion.6 = f32[64,2048]{1,0:T(8,128)S(1)} fusion(bf16[1024,4096]{1,0:T(8,128)(2,1)} %param.3, bf16[64,512]{1,0:T(8,128)(2,1)S(1)} %get-tuple-element.62, bf16[64,512]{1,0:T(8,128)(2,1)S(1)} %get-tuple-element.61), kind=kOutput, calls=%fused_computation.6 | convolution fusion | flops 268697600 | bytes 4849664 | tf_op jit(solution)/shard_map/dot_general | solution.py:294
  27.0 3.2 %fusion.2 = f32[64,2048]{1,0:T(8,128)S(1)} fusion(bf16[64,1024]{1,0:T(8,128)(2,1)S(1)} %pad_maximum_fusion.23, bf16[1024,4096]{1,0:T(8,128)(2,1)} %param.3), kind=kOutput, calls=%fused_computation.2 | convolution fusion | flops 268435456 | bytes 4849664 | tf_op jit(solution)/shard_map/dot_general | solution.py:294
  30.2 1.6 %collective-permute-start.9 = (f32[64,1024]{1,0:T(8,128)S(1)}, f32[64,1024]{1,0:T(8,128)S(1)}, u32[]{:S(2)}, u32[]{:S(2)}) collective-permute-start(f32[64,1024]{1,0:T(8,128)S(1)} %constant_dynamic-slice_fusion.5), channel_id=1, source_target_pairs={{0,2},{2,0},{4,6},{6,4},{1,3},{3,1},{5,7},{7,5},{8,10},{10,8},{12,... | collective-permute-start | bytes 786440 | tf_op jit(solution)/shard_map/ppermute | solution.py:192
  32.0 0.5 collective-permute-start.5
  32.5 7.0 %collective-permute-done.9 = f32[64,1024]{1,0:T(8,128)S(1)} collective-permute-done((f32[64,1024]{1,0:T(8,128)S(1)}, f32[64,1024]{1,0:T(8,128)S(1)}, u32[]{:S(2)}, u32[]{:S(2)}) %collective-permute-start.9) | collective-permute-done | bytes 262176 | tf_op jit(solution)/shard_map/ppermute | solution.py:192
  39.5 2.7 %collective-permute-start.10 = (f32[64,512]{1,0:T(8,128)S(1)}, f32[64,512]{1,0:T(8,128)S(1)}, u32[]{:S(2)}, u32[]{:S(2)}) collective-permute-start(f32[64,512]{1,0:T(8,128)S(1)} %constant_dynamic-slice_fusion.4), channel_id=1, source_target_pairs={{0,4},{2,6},{4,0},{6,2},{1,5},{3,7},{5,1},{7,3},{8,12},{10,14},{12... | collective-permute-start | bytes 393224 | tf_op jit(solution)/shard_map/ppermute | solution.py:192
  42.2 5.6 %collective-permute-done.5 = f32[64,1088]{1,0:T(8,128)S(1)} collective-permute-done((f32[64,1088]{1,0:T(8,128)S(1)}, f32[64,1088]{1,0:T(8,128)S(1)}, u32[]{:S(2)}, u32[]{:S(2)}) %collective-permute-start.5) | collective-permute-done | bytes 278560 | tf_op jit(solution)/shard_map/ppermute | solution.py:192
  47.9 1.2 collective-permute-start.6
  49.1 1.8 %fusion.77 = f32[128,128]{1,0:T(8,128)S(1)} fusion(f32[128,4096]{1,0:T(8,128)S(1)} %get-tuple-element.16), kind=kOutput, calls=%fused_computation.156 | convolution fusion | flops 805306368 | bytes 2162688 | tf_op jit(solution)/shard_map/dot_general | solution.py:22
  51.1 6.7 %collective-permute-done.6 = f32[64,576]{1,0:T(8,128)S(1)} collective-permute-done((f32[64,576]{1,0:T(8,128)S(1)}, f32[64,576]{1,0:T(8,128)S(1)}, u32[]{:S(2)}, u32[]{:S(2)}) %collective-permute-start.6) | collective-permute-done | bytes 147488 | tf_op jit(solution)/shard_map/ppermute | solution.py:192
  57.8 0.4 reduce-precision_convert_fusion.2
  58.3 0.4 reduce-precision_convert_fusion.1
  58.7 3.0 %collective-permute-start.11 = (bf16[64,512]{1,0:T(8,128)(2,1)S(1)}, bf16[64,512]{1,0:T(8,128)(2,1)S(1)}, u32[]{:S(2)}, u32[]{:S(2)}) collective-permute-start(bf16[64,512]{1,0:T(8,128)(2,1)S(1)} %get-tuple-element.59), channel_id=1, source_target_pairs={{0,4},{2,6},{4,0},{6,2},{1,5},{3,7},{5,1},{7,3},{8,12},{10,14},{12... | collective-permute-start | bytes 196616 | tf_op jit(solution)/shard_map/ppermute | solution.py:192
  61.7 3.2 %collective-permute-done.7 = bf16[64,512]{1,0:T(8,128)(2,1)S(1)} collective-permute-done((bf16[64,512]{1,0:T(8,128)(2,1)S(1)}, bf16[64,512]{1,0:T(8,128)(2,1)S(1)}, u32[]{:S(2)}, u32[]{:S(2)}) %collective-permute-start.7) | collective-permute-done | bytes 65568 | tf_op jit(solution)/shard_map/ppermute | solution.py:192
  65.0 1.7 %collective-permute-done.11 = bf16[64,512]{1,0:T(8,128)(2,1)S(1)} collective-permute-done((bf16[64,512]{1,0:T(8,128)(2,1)S(1)}, bf16[64,512]{1,0:T(8,128)(2,1)S(1)}, u32[]{:S(2)}, u32[]{:S(2)}) %collective-permute-start.11) | collective-permute-done | bytes 65568 | tf_op jit(solution)/shard_map/ppermute | solution.py:192
  66.7 0.4 collective-permute-start.12
  67.1 1.6 %collective-permute-start.21 = (f32[64,1280]{1,0:T(8,128)S(1)}, f32[64,1280]{1,0:T(8,128)S(1)}, u32[]{:S(2)}, u32[]{:S(2)}) collective-permute-start(f32[64,1280]{1,0:T(8,128)S(1)} %fusion.19), channel_id=1, source_target_pairs={{0,24},{8,16},{16,8},{24,0},{1,25},{9,17},{17,9},{25,1},{2,26},{10... | collective-permute-start | bytes 983048 | tf_op jit(solution)/shard_map/ppermute | solution.py:192
  68.7 1.4 %collective-permute-start.20 = (f32[64,1280]{1,0:T(8,128)S(1)}, f32[64,1280]{1,0:T(8,128)S(1)}, u32[]{:S(2)}, u32[]{:S(2)}) collective-permute-start(f32[64,1280]{1,0:T(8,128)S(1)} %fusion.19), channel_id=1, source_target_pairs={{0,16},{8,24},{16,0},{24,8},{1,17},{9,25},{17,1},{25,9},{2,18},{10... | collective-permute-start | bytes 983048 | tf_op jit(solution)/shard_map/ppermute | solution.py:192
  70.2 0.5 collective-permute-start.19
  70.7 2.0 %collective-permute-done.12 = bf16[64,1024]{1,0:T(8,128)(2,1)S(1)} collective-permute-done((bf16[64,1024]{1,0:T(8,128)(2,1)S(1)}, bf16[64,1024]{1,0:T(8,128)(2,1)S(1)}, u32[]{:S(2)}, u32[]{:S(2)}) %collective-permute-start.12) | collective-permute-done | bytes 131104 | tf_op jit(solution)/shard_map/ppermute | solution.py:192
  72.8 1.4 %fusion = f32[64,1024]{1,0:T(8,128)S(1)} fusion(bf16[1024,4096]{1,0:T(8,128)(2,1)S(1)} %bitcast.17, bf16[64,1024]{1,0:T(8,128)(2,1)S(1)} %get-tuple-element.48, bf16[64,1024]{1,0:T(8,128)(2,1)S(1)} %get-tuple-element.47), kind=kOutput, calls=%fused_computation | convolution fusion | flops 268959744 | bytes 4718592 | tf_op jit(solution)/shard_map/dot_general | solution.py:251
  74.3 0.5 fusion.71
  74.8 0.5 convolution_add_fusion
  75.3 1.4 %fusion.15 = f32[64,1024]{1,0:T(8,128)S(1)} fusion(f32[64,1024]{1,0:T(8,128)S(1)} %fusion, bf16[1024,4096]{1,0:T(8,128)(2,1)S(1)} %bitcast.17, bf16[64,1024]{1,0:T(8,128)(2,1)S(1)} %get-tuple-element.46, bf16[64,1024]{1,0:T(8,128)(2,1)S(1)} %get-tuple-element.45), kind=kOutput, calls=%fused_computation.19 | convolution fusion | flops 269025280 | bytes 4980736 | tf_op jit(solution)/shard_map/dot_general | solution.py:251
  76.7 0.8 collective-permute-start.13
  77.5 0.3 fusion.70
  77.9 6.8 %collective-permute-done.13 = bf16[64,1024]{1,0:T(8,128)(2,1)S(1)} collective-permute-done((bf16[64,1024]{1,0:T(8,128)(2,1)S(1)}, bf16[64,1024]{1,0:T(8,128)(2,1)S(1)}, u32[]{:S(2)}, u32[]{:S(2)}) %collective-permute-start.13) | collective-permute-done | bytes 131104 | tf_op jit(solution)/shard_map/ppermute | solution.py:192
  84.9 1.6 %collective-permute-start.17 = (f32[64,704]{1,0:T(8,128)S(1)}, f32[64,704]{1,0:T(8,128)S(1)}, u32[]{:S(2)}, u32[]{:S(2)}) collective-permute-start(f32[64,704]{1,0:T(8,128)S(1)} %fusion.28), channel_id=1, source_target_pairs={{0,24},{8,16},{16,8},{24,0},{1,25},{9,17},{17,9},{25,1},{2,26},{10... | collective-permute-start | bytes 540680 | tf_op jit(solution)/shard_map/ppermute | solution.py:192
  86.5 1.4 %collective-permute-start.16 = (f32[64,704]{1,0:T(8,128)S(1)}, f32[64,704]{1,0:T(8,128)S(1)}, u32[]{:S(2)}, u32[]{:S(2)}) collective-permute-start(f32[64,704]{1,0:T(8,128)S(1)} %fusion.28), channel_id=1, source_target_pairs={{0,16},{8,24},{16,0},{24,8},{1,17},{9,25},{17,1},{25,9},{2,18},{10... | collective-permute-start | bytes 540680 | tf_op jit(solution)/shard_map/ppermute | solution.py:192
  87.9 0.5 collective-permute-start.15
  88.6 0.6 maximum_multiply_fusion.gram_ref
  89.2 6.2 %whiten_given.1.given_ref = f32[128,128]{1,0:T(8,128)} custom-call(f32[128,128]{1,0:T(8,128)} %maximum_multiply_fusion.gram_ref), custom_call_target="tpu_custom_call" | custom-call | flops 4000000000 | bytes 131072 | tf_op jit(solution)/shard_map/whiten_given/pallas_call | solution.py:81
  95.4 0.4 fusion.26
  95.8 0.9 collective-permute-done.16
  96.9 1.0 add_add_fusion.1
  97.8 0.3 fusion.29
  98.1 0.4 fusion.27
  98.5 0.4 fusion.18
  99.1 1.0 broadcast_select_fusion
  100.4 2.3 %collective-permute-start.25 = (f32[32,448]{1,0:T(8,128)S(1)}, f32[32,448]{1,0:T(8,128)S(1)}, u32[]{:S(2)}, u32[]{:S(2)}) collective-permute-start(f32[32,448]{1,0:T(8,128)S(1)} %dynamic-slice_add_fusion.2), channel_id=1, source_target_pairs={{0,6},{2,4},{4,2},{6,0},{1,7},{3,5},{5,3},{7,1},{8,14},{10,12},{12... | collective-permute-start | bytes 172040 | tf_op jit(solution)/shard_map/ppermute | solution.py:192
  102.7 1.0 collective-permute-start.24
  103.6 1.2 collective-permute-start.23
  104.8 0.6 broadcast_multiply_fusion.gram_ref
  105.5 1.5 %collective-permute-done.25 = f32[32,448]{1,0:T(8,128)S(1)} collective-permute-done((f32[32,448]{1,0:T(8,128)S(1)}, f32[32,448]{1,0:T(8,128)S(1)}, u32[]{:S(2)}, u32[]{:S(2)}) %collective-permute-start.25) | collective-permute-done | bytes 57376 | tf_op jit(solution)/shard_map/ppermute | solution.py:192
  107.0 3.3 %collective-permute-done.24 = f32[32,448]{1,0:T(8,128)S(1)} collective-permute-done((f32[32,448]{1,0:T(8,128)S(1)}, f32[32,448]{1,0:T(8,128)S(1)}, u32[]{:S(2)}, u32[]{:S(2)}) %collective-permute-start.24) | collective-permute-done | bytes 57376 | tf_op jit(solution)/shard_map/ppermute | solution.py:192
  110.4 4.0 %whiten_rest.1.rest_ref = f32[64,192]{1,0:T(8,128)} custom-call(f32[128,128]{1,0:T(8,128)} %whiten_given.1.given_ref, f32[64,192]{1,0:T(8,128)} %broadcast_multiply_fusion.gram_ref), custom_call_target="tpu_custom_call" | custom-call | flops 3000000000 | bytes 131072 | tf_op jit(solution)/shard_map/whiten_rest/pallas_call | solution.py:98
  114.4 0.6 fusion.47.raw_rest_ref
  115.1 0.6 pad_maximum_fusion.28.raw_given_ref
  115.8 9.3 %ritz.1 = (f32[192,128]{1,0:T(8,128)}, f32[1,64]{1,0:T(1,128)}) custom-call(f32[128,128]{1,0:T(8,128)} %whiten_given.1.given_ref, f32[64,192]{1,0:T(8,128)} %whiten_rest.1.rest_ref, f32[128,128]{1,0:T(8,128)} %pad_maximum_fusion.28.raw_given_ref, f32[64,192]{1,0:T(8,128)} %fusion.47.raw_rest_ref), custom_call_target="tpu_custom_call" | custom-call | flops 10000000000 | bytes 524288 | tf_op jit(solution)/shard_map/ritz/pallas_call | solution.py:159
  125.1 3.1 %fusion.8 = f32[4096,64]{0,1:T(8,128)} fusion(f32[64,4096]{1,0:T(8,128)S(1)} %convert_add_fusion, f32[64,4096]{1,0:T(8,128)S(1)} %bitcast.14, f32[64,4096]{1,0:T(8,128)S(1)} %bitcast.11, f32[192,128]{1,0:T(8,128)} %get-tuple-element.21), kind=kOutput, calls=%fused_computation.11 | convolution fusion | flops 303562752 | bytes 4292608 | tf_op jit(solution)/shard_map/dot_general | solution.py:182
  128.2 2.1 %fusion.9 = f32[4096,64]{0,1:T(8,128)} fusion(f32[64,4096]{1,0:T(8,128)S(1)} %convert_add_fusion, f32[64,4096]{1,0:T(8,128)S(1)} %bitcast.15, f32[64,4096]{1,0:T(8,128)S(1)} %bitcast.12, f32[192,128]{1,0:T(8,128)S(1)} %copy-done.7), kind=kOutput, calls=%fused_computation.12 | convolution fusion | flops 303562752 | bytes 4292608 | tf_op jit(solution)/shard_map/dot_general | solution.py:182
  (97 shorter events, 2.2 us)
Async XLA Ops:
  2.6 1.0 copy-start.2
  2.6 7.3 %copy-start.5 = (bf16[128,4096]{1,0:T(8,128)(2,1)}, bf16[128,4096]{1,0:T(8,128)(2,1)S(1)}, u32[]{:S(2)}) copy-start(bf16[128,4096]{1,0:T(8,128)(2,1)S(1)} %get-tuple-element.26) | copy-start | bytes 3145732
  9.9 17.0 %copy-start.4 = (f32[192,1024]{1,0:T(8,128)}, f32[192,1024]{1,0:T(8,128)S(1)}, u32[]{:S(2)}) copy-start(f32[192,1024]{1,0:T(8,128)S(1)} %fusion.11) | copy-start | bytes 2359300
  10.0 1.5 %collective-permute-start = (f32[64,512]{1,0:T(8,128)S(1)}, f32[64,512]{1,0:T(8,128)S(1)}, u32[]{:S(2)}, u32[]{:S(2)}) collective-permute-start(f32[64,512]{1,0:T(8,128)S(1)} %constant_dynamic-slice_fusion.9), channel_id=1, source_target_pairs={{0,1},{1,0},{2,3},{3,2},{4,5},{5,4},{6,7},{7,6},{8,9},{9,8},{10,11... | collective-permute-start | bytes 393224 | tf_op jit(solution)/shard_map/ppermute | solution.py:192
  11.5 7.8 %collective-permute-start.3 = (f32[64,512]{1,0:T(8,128)S(1)}, f32[64,512]{1,0:T(8,128)S(1)}, u32[]{:S(2)}, u32[]{:S(2)}) collective-permute-start(f32[64,512]{1,0:T(8,128)S(1)} %dynamic-slice_add_fusion.1), channel_id=1, source_target_pairs={{0,24},{8,16},{16,8},{24,0},{1,25},{9,17},{17,9},{25,1},{2,26},{10... | collective-permute-start | bytes 393224 | tf_op jit(solution)/shard_map/ppermute | solution.py:192
  15.4 6.6 %collective-permute-start.2 = (f32[64,512]{1,0:T(8,128)S(1)}, f32[64,512]{1,0:T(8,128)S(1)}, u32[]{:S(2)}, u32[]{:S(2)}) collective-permute-start(f32[64,512]{1,0:T(8,128)S(1)} %dynamic-slice_add_fusion.1), channel_id=1, source_target_pairs={{0,16},{8,24},{16,0},{24,8},{1,17},{9,25},{17,1},{25,9},{2,18},{10... | collective-permute-start | bytes 393224 | tf_op jit(solution)/shard_map/ppermute | solution.py:192
  15.9 6.4 %collective-permute-start.1 = (f32[64,512]{1,0:T(8,128)S(1)}, f32[64,512]{1,0:T(8,128)S(1)}, u32[]{:S(2)}, u32[]{:S(2)}) collective-permute-start(f32[64,512]{1,0:T(8,128)S(1)} %dynamic-slice_add_fusion.1), channel_id=1, source_target_pairs={{0,8},{8,0},{16,24},{24,16},{1,9},{9,1},{17,25},{25,17},{2,10},{10... | collective-permute-start | bytes 393224 | tf_op jit(solution)/shard_map/ppermute | solution.py:192
  22.3 1.3 %collective-permute-start.4 = (bf16[64,512]{1,0:T(8,128)(2,1)S(1)}, bf16[64,512]{1,0:T(8,128)(2,1)S(1)}, u32[]{:S(2)}, u32[]{:S(2)}) collective-permute-start(bf16[64,512]{1,0:T(8,128)(2,1)S(1)} %reduce-precision_convert_fusion.3), channel_id=1, source_target_pairs={{0,1},{1,0},{2,3},{3,2},{4,5},{5,4},{6,7},{7,6},{8,9},{9,8},{10,11... | collective-permute-start | bytes 196616 | tf_op jit(solution)/shard_map/ppermute | solution.py:192
  27.0 4.9 %copy-start = (f32[4096,64]{0,1:T(8,128)S(1)}, f32[4096,64]{0,1:T(8,128)}, u32[]{:S(2)}) copy-start(f32[4096,64]{0,1:T(8,128)} %param.4) | copy-start | bytes 3145732
  27.0 45.8 %slice-start.1 = ((s8[8388608]{0:T(1024)(128)(4,1)}), s8[4194304]{0:T(1024)(128)(4,1)S(1)}, s32[]{:S(2)}) async-start(s8[8388608]{0:T(1024)(128)(4,1)} %bitcast.16), calls=%async_computation.1 | async-start | bytes 8388608
  30.2 9.2 %collective-permute-start.9 = (f32[64,1024]{1,0:T(8,128)S(1)}, f32[64,1024]{1,0:T(8,128)S(1)}, u32[]{:S(2)}, u32[]{:S(2)}) collective-permute-start(f32[64,1024]{1,0:T(8,128)S(1)} %constant_dynamic-slice_fusion.5), channel_id=1, source_target_pairs={{0,2},{2,0},{4,6},{6,4},{1,3},{3,1},{5,7},{7,5},{8,10},{10,8},{12,... | collective-permute-start | bytes 786440 | tf_op jit(solution)/shard_map/ppermute | solution.py:192
  32.0 15.8 %collective-permute-start.5 = (f32[64,1088]{1,0:T(8,128)S(1)}, f32[64,1088]{1,0:T(8,128)S(1)}, u32[]{:S(2)}, u32[]{:S(2)}) collective-permute-start(f32[64,1088]{1,0:T(8,128)S(1)} %pad_maximum_fusion.9), channel_id=1, source_target_pairs={{0,2},{2,0},{4,6},{6,4},{1,3},{3,1},{5,7},{7,5},{8,10},{10,8},{12,... | collective-permute-start | bytes 835592 | tf_op jit(solution)/shard_map/ppermute | solution.py:192
  39.5 11.4 %slice-start = ((f32[192,1024]{1,0:T(8,128)}), f32[128,1024]{1,0:T(8,128)S(1)}, s32[]{:S(2)}) async-start(f32[192,1024]{1,0:T(8,128)} %copy-done.4), calls=%async_computation | async-start | bytes 1048576 | tf_op jit(solution)/shard_map/slice | solution.py:314
  39.5 18.8 %collective-permute-start.10 = (f32[64,512]{1,0:T(8,128)S(1)}, f32[64,512]{1,0:T(8,128)S(1)}, u32[]{:S(2)}, u32[]{:S(2)}) collective-permute-start(f32[64,512]{1,0:T(8,128)S(1)} %constant_dynamic-slice_fusion.4), channel_id=1, source_target_pairs={{0,4},{2,6},{4,0},{6,2},{1,5},{3,7},{5,1},{7,3},{8,12},{10,14},{12... | collective-permute-start | bytes 393224 | tf_op jit(solution)/shard_map/ppermute | solution.py:192
  47.9 24.9 %slice-start.2 = ((s8[8388608]{0:T(1024)(128)(4,1)}), s8[4194304]{0:T(1024)(128)(4,1)S(1)}, s32[]{:S(2)}) async-start(s8[8388608]{0:T(1024)(128)(4,1)} %bitcast.16), calls=%async_computation.2 | async-start | bytes 8388608
  47.9 9.9 %collective-permute-start.6 = (f32[64,576]{1,0:T(8,128)S(1)}, f32[64,576]{1,0:T(8,128)S(1)}, u32[]{:S(2)}, u32[]{:S(2)}) collective-permute-start(f32[64,576]{1,0:T(8,128)S(1)} %pad_maximum_fusion.22), channel_id=1, source_target_pairs={{0,4},{2,6},{4,0},{6,2},{1,5},{3,7},{5,1},{7,3},{8,12},{10,14},{12... | collective-permute-start | bytes 442376 | tf_op jit(solution)/shard_map/ppermute | solution.py:192
  51.0 16.1 %collective-permute-start.18 = (f32[64,1280]{1,0:T(8,128)S(1)}, f32[64,1280]{1,0:T(8,128)S(1)}, u32[]{:S(2)}, u32[]{:S(2)}) collective-permute-start(f32[64,1280]{1,0:T(8,128)S(1)} %pad_maximum_fusion.5), channel_id=1, source_target_pairs={{0,1},{1,0},{2,3},{3,2},{4,5},{5,4},{6,7},{7,6},{8,9},{9,8},{10,11... | collective-permute-start | bytes 983048 | tf_op jit(solution)/shard_map/ppermute | solution.py:192
  58.2 6.6 %collective-permute-start.7 = (bf16[64,512]{1,0:T(8,128)(2,1)S(1)}, bf16[64,512]{1,0:T(8,128)(2,1)S(1)}, u32[]{:S(2)}, u32[]{:S(2)}) collective-permute-start(bf16[64,512]{1,0:T(8,128)(2,1)S(1)} %get-tuple-element.55), channel_id=1, source_target_pairs={{0,4},{2,6},{4,0},{6,2},{1,5},{3,7},{5,1},{7,3},{8,12},{10,14},{12... | collective-permute-start | bytes 196616 | tf_op jit(solution)/shard_map/ppermute | solution.py:192
  58.7 8.0 %collective-permute-start.11 = (bf16[64,512]{1,0:T(8,128)(2,1)S(1)}, bf16[64,512]{1,0:T(8,128)(2,1)S(1)}, u32[]{:S(2)}, u32[]{:S(2)}) collective-permute-start(bf16[64,512]{1,0:T(8,128)(2,1)S(1)} %get-tuple-element.59), channel_id=1, source_target_pairs={{0,4},{2,6},{4,0},{6,2},{1,5},{3,7},{5,1},{7,3},{8,12},{10,14},{12... | collective-permute-start | bytes 196616 | tf_op jit(solution)/shard_map/ppermute | solution.py:192
  64.9 9.3 %collective-permute-start.8 = (bf16[64,1024]{1,0:T(8,128)(2,1)S(1)}, bf16[64,1024]{1,0:T(8,128)(2,1)S(1)}, u32[]{:S(2)}, u32[]{:S(2)}) collective-permute-start(bf16[64,1024]{1,0:T(8,128)(2,1)S(1)} %pad_maximum_fusion.24), channel_id=1, source_target_pairs={{0,2},{2,0},{4,6},{6,4},{1,3},{3,1},{5,7},{7,5},{8,10},{10,8},{12,... | collective-permute-start | bytes 393224 | tf_op jit(solution)/shard_map/ppermute | solution.py:192
  66.7 6.0 %collective-permute-start.12 = (bf16[64,1024]{1,0:T(8,128)(2,1)S(1)}, bf16[64,1024]{1,0:T(8,128)(2,1)S(1)}, u32[]{:S(2)}, u32[]{:S(2)}) collective-permute-start(bf16[64,1024]{1,0:T(8,128)(2,1)S(1)} %pad_maximum_fusion.25), channel_id=1, source_target_pairs={{0,2},{2,0},{4,6},{6,4},{1,3},{3,1},{5,7},{7,5},{8,10},{10,8},{12,... | collective-permute-start | bytes 393224 | tf_op jit(solution)/shard_map/ppermute | solution.py:192
  67.1 7.2 %copy-start.3 = (bf16[128,4096]{1,0:T(8,128)(2,1)S(1)}, bf16[128,4096]{1,0:T(8,128)(2,1)}, u32[]{:S(2)}) copy-start(bf16[128,4096]{1,0:T(8,128)(2,1)} %copy-done.2) | copy-start | bytes 3145732
  67.1 19.4 %collective-permute-start.21 = (f32[64,1280]{1,0:T(8,128)S(1)}, f32[64,1280]{1,0:T(8,128)S(1)}, u32[]{:S(2)}, u32[]{:S(2)}) collective-permute-start(f32[64,1280]{1,0:T(8,128)S(1)} %fusion.19), channel_id=1, source_target_pairs={{0,24},{8,16},{16,8},{24,0},{1,25},{9,17},{17,9},{25,1},{2,26},{10... | collective-permute-start | bytes 983048 | tf_op jit(solution)/shard_map/ppermute | solution.py:192
  68.7 19.2 %collective-permute-start.20 = (f32[64,1280]{1,0:T(8,128)S(1)}, f32[64,1280]{1,0:T(8,128)S(1)}, u32[]{:S(2)}, u32[]{:S(2)}) collective-permute-start(f32[64,1280]{1,0:T(8,128)S(1)} %fusion.19), channel_id=1, source_target_pairs={{0,16},{8,24},{16,0},{24,8},{1,17},{9,25},{17,1},{25,9},{2,18},{10... | collective-permute-start | bytes 983048 | tf_op jit(solution)/shard_map/ppermute | solution.py:192
  70.2 18.2 %collective-permute-start.19 = (f32[64,1280]{1,0:T(8,128)S(1)}, f32[64,1280]{1,0:T(8,128)S(1)}, u32[]{:S(2)}, u32[]{:S(2)}) collective-permute-start(f32[64,1280]{1,0:T(8,128)S(1)} %fusion.19), channel_id=1, source_target_pairs={{0,8},{8,0},{16,24},{24,16},{1,9},{9,1},{17,25},{25,17},{2,10},{10... | collective-permute-start | bytes 983048 | tf_op jit(solution)/shard_map/ppermute | solution.py:192
  72.8 2.0 %copy-start.6 = (bf16[128,4096]{1,0:T(8,128)(2,1)S(1)}, bf16[128,4096]{1,0:T(8,128)(2,1)}, u32[]{:S(2)}) copy-start(bf16[128,4096]{1,0:T(8,128)(2,1)} %copy-done.5) | copy-start | bytes 3145732
  76.7 8.0 %collective-permute-start.13 = (bf16[64,1024]{1,0:T(8,128)(2,1)S(1)}, bf16[64,1024]{1,0:T(8,128)(2,1)S(1)}, u32[]{:S(2)}, u32[]{:S(2)}) collective-permute-start(bf16[64,1024]{1,0:T(8,128)(2,1)S(1)} %pad_maximum_fusion.26), channel_id=1, source_target_pairs={{0,4},{2,6},{4,0},{6,2},{1,5},{3,7},{5,1},{7,3},{8,12},{10,14},{12... | collective-permute-start | bytes 393224 | tf_op jit(solution)/shard_map/ppermute | solution.py:192
  77.8 7.0 %collective-permute-start.14 = (f32[64,704]{1,0:T(8,128)S(1)}, f32[64,704]{1,0:T(8,128)S(1)}, u32[]{:S(2)}, u32[]{:S(2)}) collective-permute-start(f32[64,704]{1,0:T(8,128)S(1)} %pad_maximum_fusion.10), channel_id=1, source_target_pairs={{0,1},{1,0},{2,3},{3,2},{4,5},{5,4},{6,7},{7,6},{8,9},{9,8},{10,11... | collective-permute-start | bytes 540680 | tf_op jit(solution)/shard_map/ppermute | solution.py:192
  84.7 14.4 %collective-permute-start.27 = (bf16[64,2048]{1,0:T(8,128)(2,1)S(1)}, bf16[64,2048]{1,0:T(8,128)(2,1)}, u32[]{:S(2)}, u32[]{:S(2)}) collective-permute-start(bf16[64,2048]{1,0:T(8,128)(2,1)S(1)} %pad_maximum_fusion.14), channel_id=1, source_target_pairs={{0,2},{2,0},{4,6},{6,4},{1,3},{3,1},{5,7},{7,5},{8,10},{10,8},{12,... | collective-permute-start | bytes 786440 | tf_op jit(solution)/shard_map/ppermute | solution.py:192
  84.9 11.0 %collective-permute-start.17 = (f32[64,704]{1,0:T(8,128)S(1)}, f32[64,704]{1,0:T(8,128)S(1)}, u32[]{:S(2)}, u32[]{:S(2)}) collective-permute-start(f32[64,704]{1,0:T(8,128)S(1)} %fusion.28), channel_id=1, source_target_pairs={{0,24},{8,16},{16,8},{24,0},{1,25},{9,17},{17,9},{25,1},{2,26},{10... | collective-permute-start | bytes 540680 | tf_op jit(solution)/shard_map/ppermute | solution.py:192
  86.5 10.2 %collective-permute-start.16 = (f32[64,704]{1,0:T(8,128)S(1)}, f32[64,704]{1,0:T(8,128)S(1)}, u32[]{:S(2)}, u32[]{:S(2)}) collective-permute-start(f32[64,704]{1,0:T(8,128)S(1)} %fusion.28), channel_id=1, source_target_pairs={{0,16},{8,24},{16,0},{24,8},{1,17},{9,25},{17,1},{25,9},{2,18},{10... | collective-permute-start | bytes 540680 | tf_op jit(solution)/shard_map/ppermute | solution.py:192
  87.9 9.0 %collective-permute-start.15 = (f32[64,704]{1,0:T(8,128)S(1)}, f32[64,704]{1,0:T(8,128)}, u32[]{:S(2)}, u32[]{:S(2)}) collective-permute-start(f32[64,704]{1,0:T(8,128)S(1)} %fusion.28), channel_id=1, source_target_pairs={{0,8},{8,0},{16,24},{24,16},{1,9},{9,1},{17,25},{25,17},{2,10},{10... | collective-permute-start | bytes 540680 | tf_op jit(solution)/shard_map/ppermute | solution.py:192
  99.0 1.3 %collective-permute-start.22 = (f32[32,448]{1,0:T(8,128)S(1)}, f32[32,448]{1,0:T(8,128)S(1)}, u32[]{:S(2)}, u32[]{:S(2)}) collective-permute-start(f32[32,448]{1,0:T(8,128)S(1)} %constant_dynamic-slice_fusion.3), channel_id=1, source_target_pairs={{0,1},{1,0},{2,3},{3,2},{4,5},{5,4},{6,7},{7,6},{8,9},{9,8},{10,11... | collective-permute-start | bytes 172040 | tf_op jit(solution)/shard_map/ppermute | solution.py:192
  100.4 6.6 %collective-permute-start.25 = (f32[32,448]{1,0:T(8,128)S(1)}, f32[32,448]{1,0:T(8,128)S(1)}, u32[]{:S(2)}, u32[]{:S(2)}) collective-permute-start(f32[32,448]{1,0:T(8,128)S(1)} %dynamic-slice_add_fusion.2), channel_id=1, source_target_pairs={{0,6},{2,4},{4,2},{6,0},{1,7},{3,5},{5,3},{7,1},{8,14},{10,12},{12... | collective-permute-start | bytes 172040 | tf_op jit(solution)/shard_map/ppermute | solution.py:192
  102.7 7.6 %collective-permute-start.24 = (f32[32,448]{1,0:T(8,128)S(1)}, f32[32,448]{1,0:T(8,128)S(1)}, u32[]{:S(2)}, u32[]{:S(2)}) collective-permute-start(f32[32,448]{1,0:T(8,128)S(1)} %dynamic-slice_add_fusion.2), channel_id=1, source_target_pairs={{0,4},{2,6},{4,0},{6,2},{1,5},{3,7},{5,1},{7,3},{8,12},{10,14},{12... | collective-permute-start | bytes 172040 | tf_op jit(solution)/shard_map/ppermute | solution.py:192
  103.6 6.7 %collective-permute-start.23 = (f32[32,448]{1,0:T(8,128)S(1)}, f32[32,448]{1,0:T(8,128)S(1)}, u32[]{:S(2)}, u32[]{:S(2)}) collective-permute-start(f32[32,448]{1,0:T(8,128)S(1)} %dynamic-slice_add_fusion.2), channel_id=1, source_target_pairs={{0,2},{2,0},{4,6},{6,4},{1,3},{3,1},{5,7},{7,5},{8,10},{10,8},{12,... | collective-permute-start | bytes 172040 | tf_op jit(solution)/shard_map/ppermute | solution.py:192
  110.3 4.1 %collective-permute-start.26 = (f32[32,448]{1,0:T(8,128)S(1)}, f32[32,448]{1,0:T(8,128)S(1)}, u32[]{:S(2)}, u32[]{:S(2)}) collective-permute-start(f32[32,448]{1,0:T(8,128)S(1)} %add_multiply_fusion), channel_id=1, source_target_pairs={{0,1},{1,0},{2,3},{3,2},{4,5},{5,4},{6,7},{7,6},{8,9},{9,8},{10,11... | collective-permute-start | bytes 172040 | tf_op jit(solution)/shard_map/ppermute | solution.py:192
  115.8 9.3 %copy-start.1 = (f32[4096,64]{0,1:T(8,128)S(1)}, f32[4096,64]{0,1:T(8,128)}, u32[]{:S(2)}) copy-start(f32[4096,64]{0,1:T(8,128)} %param.5) | copy-start | bytes 3145732
  125.1 3.1 %copy-start.7 = (f32[192,128]{1,0:T(8,128)S(1)}, f32[192,128]{1,0:T(8,128)}, u32[]{:S(2)}) copy-start(f32[192,128]{1,0:T(8,128)} %get-tuple-element.21) | copy-start | bytes 294916

commit v4 on v3

--- a/solution.py
+++ b/solution.py
@@ -358,7 +358,6 @@
     residual_lo = jnp.concatenate(
         [(residual - high).astype(jnp.bfloat16) for residual, high in zip(residuals, highs)], axis=1
     )
-    residual_lo = after(residual_lo, r_part)
     r_joined = reduce_all(r_joined, "layer")
     r_probe = r_joined[:, :half_rows]
     gram_rest = r_joined[:, half_rows:]
@@ -377,6 +376,7 @@
         lax.dynamic_slice_in_dim(raw, (1 - side) * (cols // 2), cols // 2, 0), "fhalf", near
     )
     rest_inverse = whiten_rest(given_inverse, after(gram_rest, raw) / feat_total)
+    residual_lo = after(residual_lo, raw)
     raw = reduce_all(raw, "token") * ritz_scale
     other = swap(raw, "fhalf", near)
     raw = jnp.concatenate(

time: 131 us -> 142 us (1.084)
  waiting for transfers between devices: 47.4 us -> 59.6 us
  other arithmetic: 7.43 us -> 5.53 us
    ppermute x28, waiting for transfers between devices: 47.4 us -> 59.6 us  [swap(): lax.ppermute(value, axis, [(i, i ^ step) for i in range(lax.axis_size(axi...]
  transfers between devices with their start and end apart: 28 -> 28, of which waited for: 16 -> 19; matrix products, arithmetic and copies ran while one was open for 9% -> 7% of each run, Pallas kernels for 8% -> 14%
where the time goes in v4:
time: 142 us; the launch traced here: 141 us
  waiting for transfers between devices  59.6 us (42%)
  starting transfers between devices  27.9 us (20%)
  matrix products  25 us (18%)
  Pallas kernels  19.4 us (14%)
  other arithmetic  5.53 us (4%)
  local copies, waits for them, and re-layouts  2.34 us (2%)
  between operations  1.43 us (1%)
    ppermute x28, waiting for transfers between devices, swap(): lax.ppermute(value, axis, [(i, i ^ step) for i in range(lax.axis_size(axi...  59.6 us
    ppermute x28, starting transfers between devices, swap(): lax.ppermute(value, axis, [(i, i ^ step) for i in range(lax.axis_size(axi...  27.9 us
    dot_general x7, matrix products, probe_of(): lax.dot_general(rows_b, slab_part, (((1,), (1,)), ((), ())), preferred_el...  10.5 us
    pallas_call x1, Pallas kernels, ritz_of(): pl.pallas_call(ritz_kernel, out_shape=(jax.ShapeDtypeStruct((size, 2 * co...  9.42 us
    dot_general x2, matrix products, local(): part = jnp.dot(probe, slab, preferred_element_type=jnp.float32)  6.14 us
    pallas_call x1, Pallas kernels, whiten_given(): pl.pallas_call(whiten_given_kernel, out_shape=jax.ShapeDtypeStruct(gram_m...  6.04 us
    dot_general x2, matrix products, moved(): lax.dot_general(coeffs, rows, (((0,), (0,)), ((), ())), precision=lax.Pre...  4.26 us
    pallas_call x1, Pallas kernels, whiten_rest(): pl.pallas_call(whiten_rest_kernel, out_shape=jax.ShapeDtypeStruct(gram_ro...  3.99 us
  transfers between devices with their start and end apart: 28, of which 19 were waited for; matrix products, arithmetic and copies ran while one was open for 7% of the time, Pallas kernels for 14%

profile of v4, /device:TPU:0, one launch (start us, length us, event | category | flops | bytes accessed | tf_op | source)
XLA Modules:
  0.0 141.3 jit_solution(11015212318864798116)
XLA Ops:
  0.6 1.9 %pad_maximum_fusion.3 = (f32[128,4096]{1,0:T(8,128)S(1)}, bf16[128,4096]{1,0:T(8,128)(2,1)S(1)}, bf16[128,4096]{1,0:T(8,128)(2,1)S(1)}) fusion(f32[64,4096]{1,0:T(8,128)} %bitcast.13, f32[64,4096]{1,0:T(8,128)} %bitcast.9), kind=kLoop, calls=%fused_computation.14 | loop fusion | flops 2621440 | bytes 6291456 | tf_op jit(solution)/shard_map/concatenate | solution.py:282
  2.6 0.9 copy-done.2
  3.6 6.3 %fusion.11 = f32[192,1024]{1,0:T(8,128)S(1)} fusion(bf16[1024,4096]{1,0:T(8,128)(2,1)} %param.3, bf16[64,4096]{1,0:T(8,128)(2,1)S(1)} %slice.155, bf16[128,4096]{1,0:T(8,128)(2,1)S(1)} %get-tuple-element.26), kind=kOutput, calls=%fused_computation.15 | convolution fusion | flops 1613758464 | bytes 10747904 | tf_op jit(solution)/shard_map/dot_general | solution.py:251
  10.0 0.5 collective-permute-start
  10.5 1.0 collective-permute-done
  11.5 3.9 %collective-permute-start.3 = (f32[64,512]{1,0:T(8,128)S(1)}, f32[64,512]{1,0:T(8,128)S(1)}, u32[]{:S(2)}, u32[]{:S(2)}) collective-permute-start(f32[64,512]{1,0:T(8,128)S(1)} %dynamic-slice_add_fusion.1), channel_id=1, source_target_pairs={{0,24},{8,16},{16,8},{24,0},{1,25},{9,17},{17,9},{25,1},{2,26},{10... | collective-permute-start | bytes 393224 | tf_op jit(solution)/shard_map/ppermute | solution.py:192
  15.4 0.5 collective-permute-start.2
  16.0 3.3 %collective-permute-done.3 = f32[64,512]{1,0:T(8,128)S(1)} collective-permute-done((f32[64,512]{1,0:T(8,128)S(1)}, f32[64,512]{1,0:T(8,128)S(1)}, u32[]{:S(2)}, u32[]{:S(2)}) %collective-permute-start.3) | collective-permute-done | bytes 131104 | tf_op jit(solution)/shard_map/ppermute | solution.py:192
  19.3 2.7 %collective-permute-done.2 = f32[64,512]{1,0:T(8,128)S(1)} collective-permute-done((f32[64,512]{1,0:T(8,128)S(1)}, f32[64,512]{1,0:T(8,128)S(1)}, u32[]{:S(2)}, u32[]{:S(2)}) %collective-permute-start.2) | collective-permute-done | bytes 131104 | tf_op jit(solution)/shard_map/ppermute | solution.py:192
  22.0 0.3 collective-permute-done.1
  22.5 1.2 collective-permute-done.4
  23.7 0.2 fusion.69
  23.9 3.0 %fusion.6 = f32[64,2048]{1,0:T(8,128)S(1)} fusion(bf16[1024,4096]{1,0:T(8,128)(2,1)} %param.3, bf16[64,512]{1,0:T(8,128)(2,1)S(1)} %get-tuple-element.62, bf16[64,512]{1,0:T(8,128)(2,1)S(1)} %get-tuple-element.61), kind=kOutput, calls=%fused_computation.6 | convolution fusion | flops 268697600 | bytes 4849664 | tf_op jit(solution)/shard_map/dot_general | solution.py:294
  27.0 3.1 %fusion.2 = f32[64,2048]{1,0:T(8,128)S(1)} fusion(bf16[64,1024]{1,0:T(8,128)(2,1)S(1)} %pad_maximum_fusion.23, bf16[1024,4096]{1,0:T(8,128)(2,1)} %param.3), kind=kOutput, calls=%fused_computation.2 | convolution fusion | flops 268435456 | bytes 4849664 | tf_op jit(solution)/shard_map/dot_general | solution.py:294
  30.2 1.6 %collective-permute-start.9 = (f32[64,1024]{1,0:T(8,128)S(1)}, f32[64,1024]{1,0:T(8,128)S(1)}, u32[]{:S(2)}, u32[]{:S(2)}) collective-permute-start(f32[64,1024]{1,0:T(8,128)S(1)} %constant_dynamic-slice_fusion.5), channel_id=1, source_target_pairs={{0,2},{2,0},{4,6},{6,4},{1,3},{3,1},{5,7},{7,5},{8,10},{10,8},{12,... | collective-permute-start | bytes 786440 | tf_op jit(solution)/shard_map/ppermute | solution.py:192
  31.9 0.5 collective-permute-start.5
  32.4 7.0 %collective-permute-done.9 = f32[64,1024]{1,0:T(8,128)S(1)} collective-permute-done((f32[64,1024]{1,0:T(8,128)S(1)}, f32[64,1024]{1,0:T(8,128)S(1)}, u32[]{:S(2)}, u32[]{:S(2)}) %collective-permute-start.9) | collective-permute-done | bytes 262176 | tf_op jit(solution)/shard_map/ppermute | solution.py:192
  39.4 2.7 %collective-permute-start.10 = (f32[64,512]{1,0:T(8,128)S(1)}, f32[64,512]{1,0:T(8,128)S(1)}, u32[]{:S(2)}, u32[]{:S(2)}) collective-permute-start(f32[64,512]{1,0:T(8,128)S(1)} %constant_dynamic-slice_fusion.4), channel_id=1, source_target_pairs={{0,4},{2,6},{4,0},{6,2},{1,5},{3,7},{5,1},{7,3},{8,12},{10,14},{12... | collective-permute-start | bytes 393224 | tf_op jit(solution)/shard_map/ppermute | solution.py:192
  42.1 5.6 %collective-permute-done.5 = f32[64,1088]{1,0:T(8,128)S(1)} collective-permute-done((f32[64,1088]{1,0:T(8,128)S(1)}, f32[64,1088]{1,0:T(8,128)S(1)}, u32[]{:S(2)}, u32[]{:S(2)}) %collective-permute-start.5) | collective-permute-done | bytes 278560 | tf_op jit(solution)/shard_map/ppermute | solution.py:192
  47.8 1.2 collective-permute-start.6
  49.0 1.8 %fusion.77 = f32[128,128]{1,0:T(8,128)S(1)} fusion(f32[128,4096]{1,0:T(8,128)S(1)} %get-tuple-element.15), kind=kOutput, calls=%fused_computation.156 | convolution fusion | flops 805306368 | bytes 2162688 | tf_op jit(solution)/shard_map/dot_general | solution.py:22
  51.0 6.7 %collective-permute-done.6 = f32[64,576]{1,0:T(8,128)S(1)} collective-permute-done((f32[64,576]{1,0:T(8,128)S(1)}, f32[64,576]{1,0:T(8,128)S(1)}, u32[]{:S(2)}, u32[]{:S(2)}) %collective-permute-start.6) | collective-permute-done | bytes 147488 | tf_op jit(solution)/shard_map/ppermute | solution.py:192
  57.7 0.4 reduce-precision_convert_fusion.2
  58.2 0.4 reduce-precision_convert_fusion.1
  58.6 3.0 %collective-permute-start.11 = (bf16[64,512]{1,0:T(8,128)(2,1)S(1)}, bf16[64,512]{1,0:T(8,128)(2,1)S(1)}, u32[]{:S(2)}, u32[]{:S(2)}) collective-permute-start(bf16[64,512]{1,0:T(8,128)(2,1)S(1)} %get-tuple-element.59), channel_id=1, source_target_pairs={{0,4},{2,6},{4,0},{6,2},{1,5},{3,7},{5,1},{7,3},{8,12},{10,14},{12... | collective-permute-start | bytes 196616 | tf_op jit(solution)/shard_map/ppermute | solution.py:192
  61.6 3.2 %collective-permute-done.7 = bf16[64,512]{1,0:T(8,128)(2,1)S(1)} collective-permute-done((bf16[64,512]{1,0:T(8,128)(2,1)S(1)}, bf16[64,512]{1,0:T(8,128)(2,1)S(1)}, u32[]{:S(2)}, u32[]{:S(2)}) %collective-permute-start.7) | collective-permute-done | bytes 65568 | tf_op jit(solution)/shard_map/ppermute | solution.py:192
  64.9 1.7 %collective-permute-done.11 = bf16[64,512]{1,0:T(8,128)(2,1)S(1)} collective-permute-done((bf16[64,512]{1,0:T(8,128)(2,1)S(1)}, bf16[64,512]{1,0:T(8,128)(2,1)S(1)}, u32[]{:S(2)}, u32[]{:S(2)}) %collective-permute-start.11) | collective-permute-done | bytes 65568 | tf_op jit(solution)/shard_map/ppermute | solution.py:192
  66.6 0.4 collective-permute-start.12
  67.0 3.7 %collective-permute-done.8 = bf16[64,1024]{1,0:T(8,128)(2,1)S(1)} collective-permute-done((bf16[64,1024]{1,0:T(8,128)(2,1)S(1)}, bf16[64,1024]{1,0:T(8,128)(2,1)S(1)}, u32[]{:S(2)}, u32[]{:S(2)}) %collective-permute-start.8) | collective-permute-done | bytes 131104 | tf_op jit(solution)/shard_map/ppermute | solution.py:192
  70.7 1.9 %collective-permute-done.12 = bf16[64,1024]{1,0:T(8,128)(2,1)S(1)} collective-permute-done((bf16[64,1024]{1,0:T(8,128)(2,1)S(1)}, bf16[64,1024]{1,0:T(8,128)(2,1)S(1)}, u32[]{:S(2)}, u32[]{:S(2)}) %collective-permute-start.12) | collective-permute-done | bytes 131104 | tf_op jit(solution)/shard_map/ppermute | solution.py:192
  72.7 0.5 fusion.71
  73.2 0.3 fusion.70
  73.5 1.4 fusion
  74.9 1.4 fusion.15
  76.3 0.5 convolution_add_fusion
  77.0 1.6 %collective-permute-start.20 = (f32[64,1280]{1,0:T(8,128)S(1)}, f32[64,1280]{1,0:T(8,128)S(1)}, u32[]{:S(2)}, u32[]{:S(2)}) collective-permute-start(f32[64,1280]{1,0:T(8,128)S(1)} %fusion.19), channel_id=1, source_target_pairs={{0,24},{8,16},{16,8},{24,0},{1,25},{9,17},{17,9},{25,1},{2,26},{10... | collective-permute-start | bytes 983048 | tf_op jit(solution)/shard_map/ppermute | solution.py:192
  78.6 1.4 %collective-permute-start.19 = (f32[64,1280]{1,0:T(8,128)S(1)}, f32[64,1280]{1,0:T(8,128)S(1)}, u32[]{:S(2)}, u32[]{:S(2)}) collective-permute-start(f32[64,1280]{1,0:T(8,128)S(1)} %fusion.19), channel_id=1, source_target_pairs={{0,16},{8,24},{16,0},{24,8},{1,17},{9,25},{17,1},{25,9},{2,18},{10... | collective-permute-start | bytes 983048 | tf_op jit(solution)/shard_map/ppermute | solution.py:192
  80.0 0.5 collective-permute-start.18
  80.6 1.6 %collective-permute-start.16 = (f32[64,704]{1,0:T(8,128)S(1)}, f32[64,704]{1,0:T(8,128)S(1)}, u32[]{:S(2)}, u32[]{:S(2)}) collective-permute-start(f32[64,704]{1,0:T(8,128)S(1)} %fusion.28), channel_id=1, source_target_pairs={{0,24},{8,16},{16,8},{24,0},{1,25},{9,17},{17,9},{25,1},{2,26},{10... | collective-permute-start | bytes 540680 | tf_op jit(solution)/shard_map/ppermute | solution.py:192
  82.2 1.4 %collective-permute-start.15 = (f32[64,704]{1,0:T(8,128)S(1)}, f32[64,704]{1,0:T(8,128)S(1)}, u32[]{:S(2)}, u32[]{:S(2)}) collective-permute-start(f32[64,704]{1,0:T(8,128)S(1)} %fusion.28), channel_id=1, source_target_pairs={{0,16},{8,24},{16,0},{24,8},{1,17},{9,25},{17,1},{25,9},{2,18},{10... | collective-permute-start | bytes 540680 | tf_op jit(solution)/shard_map/ppermute | solution.py:192
  83.6 4.9 %collective-permute-done.20 = f32[64,1280]{1,0:T(8,128)S(1)} collective-permute-done((f32[64,1280]{1,0:T(8,128)S(1)}, f32[64,1280]{1,0:T(8,128)S(1)}, u32[]{:S(2)}, u32[]{:S(2)}) %collective-permute-start.20) | collective-permute-done | bytes 327712 | tf_op jit(solution)/shard_map/ppermute | solution.py:192
  88.5 1.5 %collective-permute-start.14 = (f32[64,704]{1,0:T(8,128)S(1)}, f32[64,704]{1,0:T(8,128)S(1)}, u32[]{:S(2)}, u32[]{:S(2)}) collective-permute-start(f32[64,704]{1,0:T(8,128)S(1)} %fusion.28), channel_id=1, source_target_pairs={{0,8},{8,0},{16,24},{24,16},{1,9},{9,1},{17,25},{25,17},{2,10},{10... | collective-permute-start | bytes 540680 | tf_op jit(solution)/shard_map/ppermute | solution.py:192
  90.0 5.5 %collective-permute-done.19 = f32[64,1280]{1,0:T(8,128)S(1)} collective-permute-done((f32[64,1280]{1,0:T(8,128)S(1)}, f32[64,1280]{1,0:T(8,128)S(1)}, u32[]{:S(2)}, u32[]{:S(2)}) %collective-permute-start.19) | collective-permute-done | bytes 327712 | tf_op jit(solution)/shard_map/ppermute | solution.py:192
  95.7 0.6 maximum_multiply_fusion.gram_ref
  96.3 0.4 fusion.26
  96.7 3.1 %collective-permute-done.16 = f32[64,704]{1,0:T(8,128)S(1)} collective-permute-done((f32[64,704]{1,0:T(8,128)S(1)}, f32[64,704]{1,0:T(8,128)S(1)}, u32[]{:S(2)}, u32[]{:S(2)}) %collective-permute-start.16) | collective-permute-done | bytes 180256 | tf_op jit(solution)/shard_map/ppermute | solution.py:192
  99.8 3.7 %collective-permute-done.15 = f32[64,704]{1,0:T(8,128)S(1)} collective-permute-done((f32[64,704]{1,0:T(8,128)S(1)}, f32[64,704]{1,0:T(8,128)S(1)}, u32[]{:S(2)}, u32[]{:S(2)}) %collective-permute-start.15) | collective-permute-done | bytes 180256 | tf_op jit(solution)/shard_map/ppermute | solution.py:192
  103.6 0.3 fusion.29
  103.9 0.6 fusion.27
  104.4 0.4 fusion.18
  105.0 6.0 %whiten_given.1.given_ref = f32[128,128]{1,0:T(8,128)} custom-call(f32[128,128]{1,0:T(8,128)} %maximum_multiply_fusion.gram_ref), custom_call_target="tpu_custom_call" | custom-call | flops 4000000000 | bytes 131072 | tf_op jit(solution)/shard_map/whiten_given/pallas_call | solution.py:81
  111.1 1.9 %collective-permute-start.25 = (f32[32,448]{1,0:T(8,128)S(1)}, f32[32,448]{1,0:T(8,128)S(1)}, u32[]{:S(2)}, u32[]{:S(2)}) collective-permute-start(f32[32,448]{1,0:T(8,128)S(1)} %dynamic-slice_add_fusion.2), channel_id=1, source_target_pairs={{0,6},{2,4},{4,2},{6,0},{1,7},{3,5},{5,3},{7,1},{8,14},{10,12},{12... | collective-permute-start | bytes 172040 | tf_op jit(solution)/shard_map/ppermute | solution.py:192
  113.1 2.5 %collective-permute-start.23 = (f32[32,448]{1,0:T(8,128)S(1)}, f32[32,448]{1,0:T(8,128)S(1)}, u32[]{:S(2)}, u32[]{:S(2)}) collective-permute-start(f32[32,448]{1,0:T(8,128)S(1)} %dynamic-slice_add_fusion.2), channel_id=1, source_target_pairs={{0,2},{2,0},{4,6},{6,4},{1,3},{3,1},{5,7},{7,5},{8,10},{10,8},{12,... | collective-permute-start | bytes 172040 | tf_op jit(solution)/shard_map/ppermute | solution.py:192
  115.6 0.6 broadcast_multiply_fusion.gram_ref
  116.2 0.4 collective-permute-start.22
  116.6 1.3 collective-permute-done.25
  118.0 2.8 %collective-permute-done.24 = f32[32,448]{1,0:T(8,128)S(1)} collective-permute-done((f32[32,448]{1,0:T(8,128)S(1)}, f32[32,448]{1,0:T(8,128)S(1)}, u32[]{:S(2)}, u32[]{:S(2)}) %collective-permute-start.24) | collective-permute-done | bytes 57376 | tf_op jit(solution)/shard_map/ppermute | solution.py:192
  120.9 4.0 %whiten_rest.1.rest_ref = f32[64,192]{1,0:T(8,128)} custom-call(f32[128,128]{1,0:T(8,128)} %whiten_given.1.given_ref, f32[64,192]{1,0:T(8,128)} %broadcast_multiply_fusion.gram_ref), custom_call_target="tpu_custom_call" | custom-call | flops 3000000000 | bytes 131072 | tf_op jit(solution)/shard_map/whiten_rest/pallas_call | solution.py:98
  124.9 0.6 fusion.47.raw_rest_ref
  125.6 0.6 pad_maximum_fusion.28.raw_given_ref
  126.4 9.4 %ritz.1 = (f32[192,128]{1,0:T(8,128)}, f32[1,64]{1,0:T(1,128)}) custom-call(f32[128,128]{1,0:T(8,128)} %whiten_given.1.given_ref, f32[64,192]{1,0:T(8,128)} %whiten_rest.1.rest_ref, f32[128,128]{1,0:T(8,128)} %pad_maximum_fusion.28.raw_given_ref, f32[64,192]{1,0:T(8,128)} %fusion.47.raw_rest_ref), custom_call_target="tpu_custom_call" | custom-call | flops 10000000000 | bytes 524288 | tf_op jit(solution)/shard_map/ritz/pallas_call | solution.py:159
  136.1 0.9 copy-done.1
  137.0 2.2 %fusion.8 = f32[4096,64]{0,1:T(8,128)} fusion(f32[64,4096]{1,0:T(8,128)S(1)} %convert_add_fusion, f32[64,4096]{1,0:T(8,128)S(1)} %bitcast.14, f32[64,4096]{1,0:T(8,128)S(1)} %bitcast.11, f32[192,128]{1,0:T(8,128)S(1)} %copy-done.7), kind=kOutput, calls=%fused_computation.11 | convolution fusion | flops 303562752 | bytes 4292608 | tf_op jit(solution)/shard_map/dot_general | solution.py:182
  139.2 2.1 %fusion.9 = f32[4096,64]{0,1:T(8,128)} fusion(f32[64,4096]{1,0:T(8,128)S(1)} %convert_add_fusion, f32[64,4096]{1,0:T(8,128)S(1)} %bitcast.15, f32[64,4096]{1,0:T(8,128)S(1)} %bitcast.12, f32[192,128]{1,0:T(8,128)S(1)} %copy-done.7), kind=kOutput, calls=%fused_computation.12 | convolution fusion | flops 303562752 | bytes 4292608 | tf_op jit(solution)/shard_map/dot_general | solution.py:182
  (97 shorter events, 2.3 us)
Async XLA Ops:
  2.6 1.0 copy-start.2
  2.6 7.3 %copy-start.5 = (bf16[128,4096]{1,0:T(8,128)(2,1)}, bf16[128,4096]{1,0:T(8,128)(2,1)S(1)}, u32[]{:S(2)}) copy-start(bf16[128,4096]{1,0:T(8,128)(2,1)S(1)} %get-tuple-element.26) | copy-start | bytes 3145732
  9.9 17.0 %copy-start.4 = (f32[192,1024]{1,0:T(8,128)}, f32[192,1024]{1,0:T(8,128)S(1)}, u32[]{:S(2)}) copy-start(f32[192,1024]{1,0:T(8,128)S(1)} %fusion.11) | copy-start | bytes 2359300
  10.0 1.5 %collective-permute-start = (f32[64,512]{1,0:T(8,128)S(1)}, f32[64,512]{1,0:T(8,128)S(1)}, u32[]{:S(2)}, u32[]{:S(2)}) collective-permute-start(f32[64,512]{1,0:T(8,128)S(1)} %constant_dynamic-slice_fusion.9), channel_id=1, source_target_pairs={{0,1},{1,0},{2,3},{3,2},{4,5},{5,4},{6,7},{7,6},{8,9},{9,8},{10,11... | collective-permute-start | bytes 393224 | tf_op jit(solution)/shard_map/ppermute | solution.py:192
  11.5 7.8 %collective-permute-start.3 = (f32[64,512]{1,0:T(8,128)S(1)}, f32[64,512]{1,0:T(8,128)S(1)}, u32[]{:S(2)}, u32[]{:S(2)}) collective-permute-start(f32[64,512]{1,0:T(8,128)S(1)} %dynamic-slice_add_fusion.1), channel_id=1, source_target_pairs={{0,24},{8,16},{16,8},{24,0},{1,25},{9,17},{17,9},{25,1},{2,26},{10... | collective-permute-start | bytes 393224 | tf_op jit(solution)/shard_map/ppermute | solution.py:192
  15.4 6.6 %collective-permute-start.2 = (f32[64,512]{1,0:T(8,128)S(1)}, f32[64,512]{1,0:T(8,128)S(1)}, u32[]{:S(2)}, u32[]{:S(2)}) collective-permute-start(f32[64,512]{1,0:T(8,128)S(1)} %dynamic-slice_add_fusion.1), channel_id=1, source_target_pairs={{0,16},{8,24},{16,0},{24,8},{1,17},{9,25},{17,1},{25,9},{2,18},{10... | collective-permute-start | bytes 393224 | tf_op jit(solution)/shard_map/ppermute | solution.py:192
  15.9 6.4 %collective-permute-start.1 = (f32[64,512]{1,0:T(8,128)S(1)}, f32[64,512]{1,0:T(8,128)S(1)}, u32[]{:S(2)}, u32[]{:S(2)}) collective-permute-start(f32[64,512]{1,0:T(8,128)S(1)} %dynamic-slice_add_fusion.1), channel_id=1, source_target_pairs={{0,8},{8,0},{16,24},{24,16},{1,9},{9,1},{17,25},{25,17},{2,10},{10... | collective-permute-start | bytes 393224 | tf_op jit(solution)/shard_map/ppermute | solution.py:192
  22.3 1.3 collective-permute-start.4
  27.0 4.8 %copy-start = (f32[4096,64]{0,1:T(8,128)S(1)}, f32[4096,64]{0,1:T(8,128)}, u32[]{:S(2)}) copy-start(f32[4096,64]{0,1:T(8,128)} %param.4) | copy-start | bytes 3145732
  30.2 9.2 %collective-permute-start.9 = (f32[64,1024]{1,0:T(8,128)S(1)}, f32[64,1024]{1,0:T(8,128)S(1)}, u32[]{:S(2)}, u32[]{:S(2)}) collective-permute-start(f32[64,1024]{1,0:T(8,128)S(1)} %constant_dynamic-slice_fusion.5), channel_id=1, source_target_pairs={{0,2},{2,0},{4,6},{6,4},{1,3},{3,1},{5,7},{7,5},{8,10},{10,8},{12,... | collective-permute-start | bytes 786440 | tf_op jit(solution)/shard_map/ppermute | solution.py:192
  31.8 41.7 %slice-start.1 = ((s8[8388608]{0:T(1024)(128)(4,1)}), s8[4194304]{0:T(1024)(128)(4,1)S(1)}, s32[]{:S(2)}) async-start(s8[8388608]{0:T(1024)(128)(4,1)} %bitcast.16), calls=%async_computation.1 | async-start | bytes 8388608
  31.9 15.8 %collective-permute-start.5 = (f32[64,1088]{1,0:T(8,128)S(1)}, f32[64,1088]{1,0:T(8,128)S(1)}, u32[]{:S(2)}, u32[]{:S(2)}) collective-permute-start(f32[64,1088]{1,0:T(8,128)S(1)} %pad_maximum_fusion.9), channel_id=1, source_target_pairs={{0,2},{2,0},{4,6},{6,4},{1,3},{3,1},{5,7},{7,5},{8,10},{10,8},{12,... | collective-permute-start | bytes 835592 | tf_op jit(solution)/shard_map/ppermute | solution.py:192
  39.4 11.4 %slice-start = ((f32[192,1024]{1,0:T(8,128)}), f32[128,1024]{1,0:T(8,128)S(1)}, s32[]{:S(2)}) async-start(f32[192,1024]{1,0:T(8,128)} %copy-done.4), calls=%async_computation | async-start | bytes 1048576 | tf_op jit(solution)/shard_map/slice | solution.py:314
  39.4 18.7 %collective-permute-start.10 = (f32[64,512]{1,0:T(8,128)S(1)}, f32[64,512]{1,0:T(8,128)S(1)}, u32[]{:S(2)}, u32[]{:S(2)}) collective-permute-start(f32[64,512]{1,0:T(8,128)S(1)} %constant_dynamic-slice_fusion.4), channel_id=1, source_target_pairs={{0,4},{2,6},{4,0},{6,2},{1,5},{3,7},{5,1},{7,3},{8,12},{10,14},{12... | collective-permute-start | bytes 393224 | tf_op jit(solution)/shard_map/ppermute | solution.py:192
  47.8 9.9 %collective-permute-start.6 = (f32[64,576]{1,0:T(8,128)S(1)}, f32[64,576]{1,0:T(8,128)S(1)}, u32[]{:S(2)}, u32[]{:S(2)}) collective-permute-start(f32[64,576]{1,0:T(8,128)S(1)} %pad_maximum_fusion.22), channel_id=1, source_target_pairs={{0,4},{2,6},{4,0},{6,2},{1,5},{3,7},{5,1},{7,3},{8,12},{10,14},{12... | collective-permute-start | bytes 442376 | tf_op jit(solution)/shard_map/ppermute | solution.py:192
  50.8 21.9 %copy-start.3 = (bf16[128,4096]{1,0:T(8,128)(2,1)S(1)}, bf16[128,4096]{1,0:T(8,128)(2,1)}, u32[]{:S(2)}) copy-start(bf16[128,4096]{1,0:T(8,128)(2,1)} %copy-done.2) | copy-start | bytes 3145732
  50.8 22.6 %slice-start.2 = ((s8[8388608]{0:T(1024)(128)(4,1)}), s8[4194304]{0:T(1024)(128)(4,1)S(1)}, s32[]{:S(2)}) async-start(s8[8388608]{0:T(1024)(128)(4,1)} %bitcast.16), calls=%async_computation.2 | async-start | bytes 8388608
  50.9 26.0 %collective-permute-start.17 = (f32[64,1280]{1,0:T(8,128)S(1)}, f32[64,1280]{1,0:T(8,128)S(1)}, u32[]{:S(2)}, u32[]{:S(2)}) collective-permute-start(f32[64,1280]{1,0:T(8,128)S(1)} %pad_maximum_fusion.5), channel_id=1, source_target_pairs={{0,1},{1,0},{2,3},{3,2},{4,5},{5,4},{6,7},{7,6},{8,9},{9,8},{10,11... | collective-permute-start | bytes 983048 | tf_op jit(solution)/shard_map/ppermute | solution.py:192
  58.1 6.6 %collective-permute-start.7 = (bf16[64,512]{1,0:T(8,128)(2,1)S(1)}, bf16[64,512]{1,0:T(8,128)(2,1)S(1)}, u32[]{:S(2)}, u32[]{:S(2)}) collective-permute-start(bf16[64,512]{1,0:T(8,128)(2,1)S(1)} %get-tuple-element.55), channel_id=1, source_target_pairs={{0,4},{2,6},{4,0},{6,2},{1,5},{3,7},{5,1},{7,3},{8,12},{10,14},{12... | collective-permute-start | bytes 196616 | tf_op jit(solution)/shard_map/ppermute | solution.py:192
  58.6 8.0 %collective-permute-start.11 = (bf16[64,512]{1,0:T(8,128)(2,1)S(1)}, bf16[64,512]{1,0:T(8,128)(2,1)S(1)}, u32[]{:S(2)}, u32[]{:S(2)}) collective-permute-start(bf16[64,512]{1,0:T(8,128)(2,1)S(1)} %get-tuple-element.59), channel_id=1, source_target_pairs={{0,4},{2,6},{4,0},{6,2},{1,5},{3,7},{5,1},{7,3},{8,12},{10,14},{12... | collective-permute-start | bytes 196616 | tf_op jit(solution)/shard_map/ppermute | solution.py:192
  64.8 5.9 %collective-permute-start.8 = (bf16[64,1024]{1,0:T(8,128)(2,1)S(1)}, bf16[64,1024]{1,0:T(8,128)(2,1)S(1)}, u32[]{:S(2)}, u32[]{:S(2)}) collective-permute-start(bf16[64,1024]{1,0:T(8,128)(2,1)S(1)} %pad_maximum_fusion.24), channel_id=1, source_target_pairs={{0,2},{2,0},{4,6},{6,4},{1,3},{3,1},{5,7},{7,5},{8,10},{10,8},{12,... | collective-permute-start | bytes 393224 | tf_op jit(solution)/shard_map/ppermute | solution.py:192
  66.6 6.0 %collective-permute-start.12 = (bf16[64,1024]{1,0:T(8,128)(2,1)S(1)}, bf16[64,1024]{1,0:T(8,128)(2,1)S(1)}, u32[]{:S(2)}, u32[]{:S(2)}) collective-permute-start(bf16[64,1024]{1,0:T(8,128)(2,1)S(1)} %pad_maximum_fusion.25), channel_id=1, source_target_pairs={{0,2},{2,0},{4,6},{6,4},{1,3},{3,1},{5,7},{7,5},{8,10},{10,8},{12,... | collective-permute-start | bytes 393224 | tf_op jit(solution)/shard_map/ppermute | solution.py:192
  74.9 1.4 %copy-start.6 = (bf16[128,4096]{1,0:T(8,128)(2,1)S(1)}, bf16[128,4096]{1,0:T(8,128)(2,1)}, u32[]{:S(2)}) copy-start(bf16[128,4096]{1,0:T(8,128)(2,1)} %copy-done.5) | copy-start | bytes 3145732
  76.9 3.7 %collective-permute-start.13 = (f32[64,704]{1,0:T(8,128)S(1)}, f32[64,704]{1,0:T(8,128)S(1)}, u32[]{:S(2)}, u32[]{:S(2)}) collective-permute-start(f32[64,704]{1,0:T(8,128)S(1)} %pad_maximum_fusion.10), channel_id=1, source_target_pairs={{0,1},{1,0},{2,3},{3,2},{4,5},{5,4},{6,7},{7,6},{8,9},{9,8},{10,11... | collective-permute-start | bytes 540680 | tf_op jit(solution)/shard_map/ppermute | solution.py:192
  77.0 11.5 %collective-permute-start.20 = (f32[64,1280]{1,0:T(8,128)S(1)}, f32[64,1280]{1,0:T(8,128)S(1)}, u32[]{:S(2)}, u32[]{:S(2)}) collective-permute-start(f32[64,1280]{1,0:T(8,128)S(1)} %fusion.19), channel_id=1, source_target_pairs={{0,24},{8,16},{16,8},{24,0},{1,25},{9,17},{17,9},{25,1},{2,26},{10... | collective-permute-start | bytes 983048 | tf_op jit(solution)/shard_map/ppermute | solution.py:192
  78.6 17.0 %collective-permute-start.19 = (f32[64,1280]{1,0:T(8,128)S(1)}, f32[64,1280]{1,0:T(8,128)S(1)}, u32[]{:S(2)}, u32[]{:S(2)}) collective-permute-start(f32[64,1280]{1,0:T(8,128)S(1)} %fusion.19), channel_id=1, source_target_pairs={{0,16},{8,24},{16,0},{24,8},{1,17},{9,25},{17,1},{25,9},{2,18},{10... | collective-permute-start | bytes 983048 | tf_op jit(solution)/shard_map/ppermute | solution.py:192
  80.0 15.5 %collective-permute-start.18 = (f32[64,1280]{1,0:T(8,128)S(1)}, f32[64,1280]{1,0:T(8,128)S(1)}, u32[]{:S(2)}, u32[]{:S(2)}) collective-permute-start(f32[64,1280]{1,0:T(8,128)S(1)} %fusion.19), channel_id=1, source_target_pairs={{0,8},{8,0},{16,24},{24,16},{1,9},{9,1},{17,25},{25,17},{2,10},{10... | collective-permute-start | bytes 983048 | tf_op jit(solution)/shard_map/ppermute | solution.py:192
  80.6 19.2 %collective-permute-start.16 = (f32[64,704]{1,0:T(8,128)S(1)}, f32[64,704]{1,0:T(8,128)S(1)}, u32[]{:S(2)}, u32[]{:S(2)}) collective-permute-start(f32[64,704]{1,0:T(8,128)S(1)} %fusion.28), channel_id=1, source_target_pairs={{0,24},{8,16},{16,8},{24,0},{1,25},{9,17},{17,9},{25,1},{2,26},{10... | collective-permute-start | bytes 540680 | tf_op jit(solution)/shard_map/ppermute | solution.py:192
  82.2 21.3 %collective-permute-start.15 = (f32[64,704]{1,0:T(8,128)S(1)}, f32[64,704]{1,0:T(8,128)S(1)}, u32[]{:S(2)}, u32[]{:S(2)}) collective-permute-start(f32[64,704]{1,0:T(8,128)S(1)} %fusion.28), channel_id=1, source_target_pairs={{0,16},{8,24},{16,0},{24,8},{1,17},{9,25},{17,1},{25,9},{2,18},{10... | collective-permute-start | bytes 540680 | tf_op jit(solution)/shard_map/ppermute | solution.py:192
  88.5 15.1 %collective-permute-start.14 = (f32[64,704]{1,0:T(8,128)S(1)}, f32[64,704]{1,0:T(8,128)S(1)}, u32[]{:S(2)}, u32[]{:S(2)}) collective-permute-start(f32[64,704]{1,0:T(8,128)S(1)} %fusion.28), channel_id=1, source_target_pairs={{0,8},{8,0},{16,24},{24,16},{1,9},{9,1},{17,25},{25,17},{2,10},{10... | collective-permute-start | bytes 540680 | tf_op jit(solution)/shard_map/ppermute | solution.py:192
  105.0 6.1 %collective-permute-start.21 = (f32[32,448]{1,0:T(8,128)S(1)}, f32[32,448]{1,0:T(8,128)S(1)}, u32[]{:S(2)}, u32[]{:S(2)}) collective-permute-start(f32[32,448]{1,0:T(8,128)S(1)} %constant_dynamic-slice_fusion.3), channel_id=1, source_target_pairs={{0,1},{1,0},{2,3},{3,2},{4,5},{5,4},{6,7},{7,6},{8,9},{9,8},{10,11... | collective-permute-start | bytes 172040 | tf_op jit(solution)/shard_map/ppermute | solution.py:192
  111.1 6.8 %collective-permute-start.25 = (f32[32,448]{1,0:T(8,128)S(1)}, f32[32,448]{1,0:T(8,128)S(1)}, u32[]{:S(2)}, u32[]{:S(2)}) collective-permute-start(f32[32,448]{1,0:T(8,128)S(1)} %dynamic-slice_add_fusion.2), channel_id=1, source_target_pairs={{0,6},{2,4},{4,2},{6,0},{1,7},{3,5},{5,3},{7,1},{8,14},{10,12},{12... | collective-permute-start | bytes 172040 | tf_op jit(solution)/shard_map/ppermute | solution.py:192
  113.1 7.7 %collective-permute-start.24 = (f32[32,448]{1,0:T(8,128)S(1)}, f32[32,448]{1,0:T(8,128)S(1)}, u32[]{:S(2)}, u32[]{:S(2)}) collective-permute-start(f32[32,448]{1,0:T(8,128)S(1)} %dynamic-slice_add_fusion.2), channel_id=1, source_target_pairs={{0,4},{2,6},{4,0},{6,2},{1,5},{3,7},{5,1},{7,3},{8,12},{10,14},{12... | collective-permute-start | bytes 172040 | tf_op jit(solution)/shard_map/ppermute | solution.py:192
  113.1 7.7 %collective-permute-start.23 = (f32[32,448]{1,0:T(8,128)S(1)}, f32[32,448]{1,0:T(8,128)S(1)}, u32[]{:S(2)}, u32[]{:S(2)}) collective-permute-start(f32[32,448]{1,0:T(8,128)S(1)} %dynamic-slice_add_fusion.2), channel_id=1, source_target_pairs={{0,2},{2,0},{4,6},{6,4},{1,3},{3,1},{5,7},{7,5},{8,10},{10,8},{12,... | collective-permute-start | bytes 172040 | tf_op jit(solution)/shard_map/ppermute | solution.py:192
  116.2 10.0 %collective-permute-start.22 = (bf16[64,1024]{1,0:T(8,128)(2,1)S(1)}, bf16[64,1024]{1,0:T(8,128)(2,1)S(1)}, u32[]{:S(2)}, u32[]{:S(2)}) collective-permute-start(bf16[64,1024]{1,0:T(8,128)(2,1)S(1)} %pad_maximum_fusion.26), channel_id=1, source_target_pairs={{0,4},{2,6},{4,0},{6,2},{1,5},{3,7},{5,1},{7,3},{8,12},{10,14},{12... | collective-permute-start | bytes 393224 | tf_op jit(solution)/shard_map/ppermute | solution.py:192
  120.8 4.1 %collective-permute-start.26 = (f32[32,448]{1,0:T(8,128)S(1)}, f32[32,448]{1,0:T(8,128)S(1)}, u32[]{:S(2)}, u32[]{:S(2)}) collective-permute-start(f32[32,448]{1,0:T(8,128)S(1)} %add_multiply_fusion), channel_id=1, source_target_pairs={{0,1},{1,0},{2,3},{3,2},{4,5},{5,4},{6,7},{7,6},{8,9},{9,8},{10,11... | collective-permute-start | bytes 172040 | tf_op jit(solution)/shard_map/ppermute | solution.py:192
  126.3 9.5 %collective-permute-start.27 = (bf16[64,2048]{1,0:T(8,128)(2,1)S(1)}, bf16[64,2048]{1,0:T(8,128)(2,1)S(1)}, u32[]{:S(2)}, u32[]{:S(2)}) collective-permute-start(bf16[64,2048]{1,0:T(8,128)(2,1)S(1)} %pad_maximum_fusion.16), channel_id=1, source_target_pairs={{0,2},{2,0},{4,6},{6,4},{1,3},{3,1},{5,7},{7,5},{8,10},{10,8},{12,... | collective-permute-start | bytes 786440 | tf_op jit(solution)/shard_map/ppermute | solution.py:192
  135.8 1.2 copy-start.1
  135.8 1.2 copy-start.7

commit v5 on v4

--- a/solution.py
+++ b/solution.py
@@ -329,8 +329,14 @@
     ]
     highs = [rounded(residual) for residual in residuals]
     high_b = [high.astype(jnp.bfloat16) for high in highs]
-    search = [gather_halves(high, "token") for high in high_b]
     joined = reduce_all(joined, "layer")
+    search = []
+    for number, rows in enumerate(high_b):
+        for step in reversed(token_steps):
+            if step == token_steps[-1] and number + 1 == CHUNKS:
+                rows = after(rows, joined)
+            rows = joined_halves(rows, "token", step)
+        search.append(rows)
     r_part = sum(probe_of(rows, slab) for rows, slab in zip(search, slabs))
     search_rows = jnp.concatenate(search, axis=1)
     gram_rest = jnp.concatenate(
@@ -358,7 +364,7 @@
     residual_lo = jnp.concatenate(
         [(residual - high).astype(jnp.bfloat16) for residual, high in zip(residuals, highs)], axis=1
     )
-    r_joined = reduce_all(r_joined, "layer")
+    r_joined = after(reduce_all(r_joined, "layer"), given_inverse)
     r_probe = r_joined[:, :half_rows]
     gram_rest = r_joined[:, half_rows:]
     r_probe_b = rounded(r_probe)
@@ -377,7 +383,9 @@
     )
     rest_inverse = whiten_rest(given_inverse, after(gram_rest, raw) / feat_total)
     residual_lo = after(residual_lo, raw)
-    raw = reduce_all(raw, "token") * ritz_scale
+    for step in reversed(token_steps[1:]):
+        residual_lo = joined_halves(residual_lo, "token", step)
+    raw = after(reduce_all(raw, "token") * ritz_scale, rest_inverse, residual_lo)
     other = swap(raw, "fhalf", near)
     raw = jnp.concatenate(
         [jnp.where(side == 0, raw, other), jnp.where(side == 0, other, raw)], axis=0
@@ -385,10 +393,7 @@
     raw_rest = raw[:, : 3 * cols]
     raw_given = jnp.concatenate([raw[:, 3 * cols : 5 * cols], raw[:, 5 * cols :]], axis=0)
     all_coeffs, ritz_values = ritz_of(given_inverse, rest_inverse, raw_given, raw_rest)
-    for step in reversed(token_steps):
-        if step == token_steps[0]:
-            residual_lo = after(residual_lo, raw)
-        residual_lo = joined_halves(residual_lo, "token", step)
+    residual_lo = joined_halves(after(residual_lo, raw), "token", token_steps[0])
     residual_rows = search_rows.astype(jnp.float32) + reordered(residual_lo, CHUNKS).astype(jnp.float32)
     search_basis = jnp.concatenate([x_rows, d_rows, residual_rows], axis=0)
     new_block = moved(all_coeffs[:, :cols], search_basis)

time: 142 us -> 153 us (1.077)
  waiting for transfers between devices: 59.6 us -> 48.6 us
  starting transfers between devices: 27.9 us -> 36.8 us
  other arithmetic: 5.53 us -> 10.7 us
  matrix products: 25 us -> 29.6 us
  local copies, waits for them, and re-layouts: 2.34 us -> 5.64 us
    ppermute x28, waiting for transfers between devices: 59.6 us -> 48.6 us  [swap(): lax.ppermute(value, axis, [(i, i ^ step) for i in range(lax.axis_size(axi...]
    ppermute x28, starting transfers between devices: 27.9 us -> 36.8 us  [swap(): lax.ppermute(value, axis, [(i, i ^ step) for i in range(lax.axis_size(axi...]
    dot_general x2, matrix products: 0.77 us -> 3.2 us  [exact_transposed(): lax.dot_general(left, right, (((0,), (0,)), ((), ())), precision=HIGHEST,...]
    dot_general x7, matrix products: 10.5 us -> 12.8 us  [probe_of(): lax.dot_general(rows_b, slab_part, (((1,), (1,)), ((), ())), preferred_el...]
    add x2, other arithmetic: 0.07 us -> 2.12 us  [local(): images.append(kept_half(parts[c], 'token', step) + got)]
    unnamed x27 -> x37, local copies, waits for them, and re-layouts: 1.98 us -> 3.54 us
  transfers between devices with their start and end apart: 28 -> 28, of which waited for: 19 -> 15; matrix products, arithmetic and copies ran while one was open for 7% -> 9% of each run, Pallas kernels for 14% -> 13%
where the time goes in v5:
time: 153 us; the launch traced here: 152 us
  waiting for transfers between devices  48.6 us (32%)
  starting transfers between devices  36.8 us (24%)
  matrix products  29.6 us (19%)
  Pallas kernels  19.6 us (13%)
  other arithmetic  10.7 us (7%)
  local copies, waits for them, and re-layouts  5.64 us (4%)
    ppermute x28, waiting for transfers between devices, swap(): lax.ppermute(value, axis, [(i, i ^ step) for i in range(lax.axis_size(axi...  48.6 us
    ppermute x28, starting transfers between devices, swap(): lax.ppermute(value, axis, [(i, i ^ step) for i in range(lax.axis_size(axi...  36.8 us
    dot_general x7, matrix products, probe_of(): lax.dot_general(rows_b, slab_part, (((1,), (1,)), ((), ())), preferred_el...  12.8 us
    pallas_call x1, Pallas kernels, ritz_of(): pl.pallas_call(ritz_kernel, out_shape=(jax.ShapeDtypeStruct((size, 2 * co...  9.42 us
    pallas_call x1, Pallas kernels, whiten_given(): pl.pallas_call(whiten_given_kernel, out_shape=jax.ShapeDtypeStruct(gram_m...  6.2 us
    dot_general x2, matrix products, local(): part = jnp.dot(probe, slab, preferred_element_type=jnp.float32)  6.09 us
    dot_general x2, matrix products, moved(): lax.dot_general(coeffs, rows, (((0,), (0,)), ((), ())), precision=lax.Pre...  4.26 us
    pallas_call x1, Pallas kernels, whiten_rest(): pl.pallas_call(whiten_rest_kernel, out_shape=jax.ShapeDtypeStruct(gram_ro...  3.98 us
  transfers between devices with their start and end apart: 28, of which 15 were waited for; matrix products, arithmetic and copies ran while one was open for 9% of the time, Pallas kernels for 13%

profile of v5, /device:TPU:0, one launch (start us, length us, event | category | flops | bytes accessed | tf_op | source)
XLA Modules:
  0.0 152.3 jit_solution(4258289470425246611)
XLA Ops:
  0.6 1.9 %pad_maximum_fusion.3 = (f32[128,4096]{1,0:T(8,128)S(1)}, bf16[128,4096]{1,0:T(8,128)(2,1)S(1)}, bf16[128,4096]{1,0:T(8,128)(2,1)S(1)}) fusion(f32[64,4096]{1,0:T(8,128)} %bitcast.13, f32[64,4096]{1,0:T(8,128)} %bitcast.9), kind=kLoop, calls=%fused_computation.14 | loop fusion | flops 2621440 | bytes 6291456 | tf_op jit(solution)/shard_map/concatenate | solution.py:282
  2.6 0.9 copy-done.2
  3.6 6.3 %fusion.11 = f32[192,1024]{1,0:T(8,128)S(1)} fusion(bf16[1024,4096]{1,0:T(8,128)(2,1)} %param.3, bf16[64,4096]{1,0:T(8,128)(2,1)S(1)} %slice.155, bf16[128,4096]{1,0:T(8,128)(2,1)S(1)} %get-tuple-element.32), kind=kOutput, calls=%fused_computation.15 | convolution fusion | flops 1613758464 | bytes 10747904 | tf_op jit(solution)/shard_map/dot_general | solution.py:251
  9.9 0.9 copy-done.4
  10.9 0.5 collective-permute-start
  11.4 1.0 collective-permute-done
  12.4 2.9 %collective-permute-start.1 = (f32[64,512]{1,0:T(8,128)S(1)}, f32[64,512]{1,0:T(8,128)S(1)}, u32[]{:S(2)}, u32[]{:S(2)}) collective-permute-start(f32[64,512]{1,0:T(8,128)S(1)} %dynamic-slice_add_fusion.1), channel_id=1, source_target_pairs={{0,8},{8,0},{16,24},{24,16},{1,9},{9,1},{17,25},{25,17},{2,10},{10... | collective-permute-start | bytes 393224 | tf_op jit(solution)/shard_map/ppermute | solution.py:192
  15.3 1.5 collective-permute-start.2
  16.8 2.4 %collective-permute-done.1 = f32[64,512]{1,0:T(8,128)S(1)} collective-permute-done((f32[64,512]{1,0:T(8,128)S(1)}, f32[64,512]{1,0:T(8,128)S(1)}, u32[]{:S(2)}, u32[]{:S(2)}) %collective-permute-start.1) | collective-permute-done | bytes 131104 | tf_op jit(solution)/shard_map/ppermute | solution.py:192
  19.2 4.2 %collective-permute-done.2 = f32[64,512]{1,0:T(8,128)S(1)} collective-permute-done((f32[64,512]{1,0:T(8,128)S(1)}, f32[64,512]{1,0:T(8,128)S(1)}, u32[]{:S(2)}, u32[]{:S(2)}) %collective-permute-start.2) | collective-permute-done | bytes 131104 | tf_op jit(solution)/shard_map/ppermute | solution.py:192
  23.6 1.2 collective-permute-done.4
  24.8 3.1 %fusion.6 = f32[64,2048]{1,0:T(8,128)S(1)} fusion(bf16[1024,4096]{1,0:T(8,128)(2,1)} %param.3, bf16[64,512]{1,0:T(8,128)(2,1)S(1)} %get-tuple-element.68, bf16[64,512]{1,0:T(8,128)(2,1)S(1)} %get-tuple-element.67), kind=kOutput, calls=%fused_computation.6 | convolution fusion | flops 268697600 | bytes 4849664 | tf_op jit(solution)/shard_map/dot_general | solution.py:294
  28.1 0.7 pad_maximum_fusion.9
  28.9 1.6 %collective-permute-start.5 = (f32[64,1088]{1,0:T(8,128)}, f32[64,1088]{1,0:T(8,128)}, u32[]{:S(2)}, u32[]{:S(2)}) collective-permute-start(f32[64,1088]{1,0:T(8,128)} %pad_maximum_fusion.9), channel_id=1, source_target_pairs={{0,2},{2,0},{4,6},{6,4},{1,3},{3,1},{5,7},{7,5},{8,10},{10,8},{12,... | collective-permute-start | bytes 835592 | tf_op jit(solution)/shard_map/ppermute | solution.py:192
  30.4 3.0 %fusion.2 = f32[64,2048]{1,0:T(8,128)S(1)} fusion(bf16[64,1024]{1,0:T(8,128)(2,1)S(1)} %pad_maximum_fusion.23, bf16[1024,4096]{1,0:T(8,128)(2,1)} %param.3), kind=kOutput, calls=%fused_computation.2 | convolution fusion | flops 268435456 | bytes 4849664 | tf_op jit(solution)/shard_map/dot_general | solution.py:294
  33.5 0.8 constant_dynamic-slice_fusion.5
  34.4 0.5 collective-permute-start.9
  34.8 1.0 fusion.73
  35.9 8.0 %collective-permute-done.9 = f32[64,1024]{1,0:T(8,128)} collective-permute-done((f32[64,1024]{1,0:T(8,128)}, f32[64,1024]{1,0:T(8,128)}, u32[]{:S(2)}, u32[]{:S(2)}) %collective-permute-start.9) | collective-permute-done | bytes 262176 | tf_op jit(solution)/shard_map/ppermute | solution.py:192
  43.9 1.1 dynamic-slice_add_fusion
  44.9 1.1 slice_add_fusion
  46.0 0.8 slice_add_fusion.4
  46.8 2.6 %collective-permute-start.6 = (f32[64,576]{1,0:T(8,128)S(1)}, f32[64,576]{1,0:T(8,128)S(1)}, u32[]{:S(2)}, u32[]{:S(2)}) collective-permute-start(f32[64,576]{1,0:T(8,128)S(1)} %pad_maximum_fusion.22), channel_id=1, source_target_pairs={{0,4},{2,6},{4,0},{6,2},{1,5},{3,7},{5,1},{7,3},{8,12},{10,14},{12... | collective-permute-start | bytes 442376 | tf_op jit(solution)/shard_map/ppermute | solution.py:192
  49.5 1.8 %fusion.77 = f32[128,128]{1,0:T(8,128)S(1)} fusion(f32[128,4096]{1,0:T(8,128)S(1)} %get-tuple-element.18), kind=kOutput, calls=%fused_computation.156 | convolution fusion | flops 805306368 | bytes 2162688 | tf_op jit(solution)/shard_map/dot_general | solution.py:22
  51.9 8.8 %collective-permute-done.6 = f32[64,576]{1,0:T(8,128)S(1)} collective-permute-done((f32[64,576]{1,0:T(8,128)S(1)}, f32[64,576]{1,0:T(8,128)S(1)}, u32[]{:S(2)}, u32[]{:S(2)}) %collective-permute-start.6) | collective-permute-done | bytes 147488 | tf_op jit(solution)/shard_map/ppermute | solution.py:192
  60.7 1.3 reduce-precision_convert_fusion.2
  62.1 1.3 collective-permute-start.12
  63.4 0.8 collective-permute-start.13
  64.2 1.4 collective-permute-start.14
  65.7 1.9 %reduce-precision_convert_fusion.1 = (bf16[64,512]{1,0:T(8,128)(2,1)S(1)}, bf16[64,512]{1,0:T(8,128)(2,1)}) fusion(f32[64,2048]{1,0:T(8,128)} %get-tuple-element.35, s32[]{:T(128)S(6)} %dynamic_slice.66, f32[64,64]{1,0:T(8,128)S(1)} %slice_add_fusion.4, f32[64,576]{1,0:T(8,128)S(1)} %collective-permute-done.6, f32[64,512]{1,0:T(8,128)S(1)} %collective-permute-done.10, ...), kind=kOutput, calls=%fused_computation.64 | convolution fusion | flops 25403392 | bytes 589832 | tf_op jit(solution)/shard_map/dot_general | solution.py:16
  68.1 2.3 %collective-permute-done.12 = f32[64,1280]{1,0:T(8,128)S(1)} collective-permute-done((f32[64,1280]{1,0:T(8,128)S(1)}, f32[64,1280]{1,0:T(8,128)S(1)}, u32[]{:S(2)}, u32[]{:S(2)}) %collective-permute-start.12) | collective-permute-done | bytes 327712 | tf_op jit(solution)/shard_map/ppermute | solution.py:192
  70.3 4.5 %collective-permute-done.13 = f32[64,1280]{1,0:T(8,128)S(1)} collective-permute-done((f32[64,1280]{1,0:T(8,128)S(1)}, f32[64,1280]{1,0:T(8,128)S(1)}, u32[]{:S(2)}, u32[]{:S(2)}) %collective-permute-start.13) | collective-permute-done | bytes 327712 | tf_op jit(solution)/shard_map/ppermute | solution.py:192
  74.9 2.7 %collective-permute-start.15 = (bf16[64,512]{1,0:T(8,128)(2,1)S(1)}, bf16[64,512]{1,0:T(8,128)(2,1)S(1)}, u32[]{:S(2)}, u32[]{:S(2)}) collective-permute-start(bf16[64,512]{1,0:T(8,128)(2,1)S(1)} %get-tuple-element.20), channel_id=1, source_target_pairs={{0,4},{2,6},{4,0},{6,2},{1,5},{3,7},{5,1},{7,3},{8,12},{10,14},{12... | collective-permute-start | bytes 196616 | tf_op jit(solution)/shard_map/ppermute | solution.py:192
  77.6 6.0 %collective-permute-start.8 = (bf16[64,1024]{1,0:T(8,128)(2,1)S(1)}, bf16[64,1024]{1,0:T(8,128)(2,1)S(1)}, u32[]{:S(2)}, u32[]{:S(2)}) collective-permute-start(bf16[64,1024]{1,0:T(8,128)(2,1)S(1)} %pad_maximum_fusion.24), channel_id=1, source_target_pairs={{0,2},{2,0},{4,6},{6,4},{1,3},{3,1},{5,7},{7,5},{8,10},{10,8},{12,... | collective-permute-start | bytes 393224 | tf_op jit(solution)/shard_map/ppermute | solution.py:192
  83.6 5.5 %collective-permute-start.16 = (bf16[64,1024]{1,0:T(8,128)(2,1)S(1)}, bf16[64,1024]{1,0:T(8,128)(2,1)S(1)}, u32[]{:S(2)}, u32[]{:S(2)}) collective-permute-start(bf16[64,1024]{1,0:T(8,128)(2,1)S(1)} %pad_maximum_fusion.25), channel_id=1, source_target_pairs={{0,2},{2,0},{4,6},{6,4},{1,3},{3,1},{5,7},{7,5},{8,10},{10,8},{12,... | collective-permute-start | bytes 393224 | tf_op jit(solution)/shard_map/ppermute | solution.py:192
  89.2 2.9 %collective-permute-done.16 = bf16[64,1024]{1,0:T(8,128)(2,1)S(1)} collective-permute-done((bf16[64,1024]{1,0:T(8,128)(2,1)S(1)}, bf16[64,1024]{1,0:T(8,128)(2,1)S(1)}, u32[]{:S(2)}, u32[]{:S(2)}) %collective-permute-start.16) | collective-permute-done | bytes 131104 | tf_op jit(solution)/shard_map/ppermute | solution.py:192
  92.2 3.7 %fusion = f32[64,1024]{1,0:T(8,128)S(1)} fusion(bf16[1024,4096]{1,0:T(8,128)(2,1)} %param.3, bf16[64,1024]{1,0:T(8,128)(2,1)S(1)} %get-tuple-element.54, bf16[64,1024]{1,0:T(8,128)(2,1)S(1)} %get-tuple-element.53), kind=kOutput, calls=%fused_computation | convolution fusion | flops 268959744 | bytes 4718592 | tf_op jit(solution)/shard_map/dot_general | solution.py:251
  95.9 0.5 fusion.71
  96.8 1.4 fusion.15
  98.2 0.5 convolution_add_fusion
  98.7 0.6 copy-done.12
  99.3 1.4 collective-permute-done.17
  100.7 0.8 fusion.28
  101.5 0.9 collective-permute-start.18
  102.4 1.5 collective-permute-start.19
  103.9 1.2 collective-permute-start.20
  105.1 0.6 maximum_multiply_fusion.gram_ref
  105.8 6.2 %whiten_given.1.given_ref = f32[128,128]{1,0:T(8,128)} custom-call(f32[128,128]{1,0:T(8,128)} %maximum_multiply_fusion.gram_ref), custom_call_target="tpu_custom_call" | custom-call | flops 4000000000 | bytes 131072 | tf_op jit(solution)/shard_map/whiten_given/pallas_call | solution.py:81
  112.4 0.9 collective-permute-done.19
  113.3 1.0 add_add_fusion.1
  115.6 1.2 collective-permute-done.21
  116.8 2.1 %collective-permute-start.23 = (f32[32,448]{1,0:T(8,128)S(1)}, f32[32,448]{1,0:T(8,128)S(1)}, u32[]{:S(2)}, u32[]{:S(2)}) collective-permute-start(f32[32,448]{1,0:T(8,128)S(1)} %dynamic-slice_add_fusion.2), channel_id=1, source_target_pairs={{0,2},{2,0},{4,6},{6,4},{1,3},{3,1},{5,7},{7,5},{8,10},{10,8},{12,... | collective-permute-start | bytes 172040 | tf_op jit(solution)/shard_map/ppermute | solution.py:192
  118.9 2.4 %collective-permute-start.25 = (f32[32,448]{1,0:T(8,128)S(1)}, f32[32,448]{1,0:T(8,128)S(1)}, u32[]{:S(2)}, u32[]{:S(2)}) collective-permute-start(f32[32,448]{1,0:T(8,128)S(1)} %dynamic-slice_add_fusion.2), channel_id=1, source_target_pairs={{0,6},{2,4},{4,2},{6,0},{1,7},{3,5},{5,3},{7,1},{8,14},{10,12},{12... | collective-permute-start | bytes 172040 | tf_op jit(solution)/shard_map/ppermute | solution.py:192
  121.3 0.6 broadcast_multiply_fusion.gram_ref
  121.9 4.0 %whiten_rest.1.rest_ref = f32[64,192]{1,0:T(8,128)} custom-call(f32[128,128]{1,0:T(8,128)} %whiten_given.1.given_ref, f32[64,192]{1,0:T(8,128)} %broadcast_multiply_fusion.gram_ref), custom_call_target="tpu_custom_call" | custom-call | flops 3000000000 | bytes 131072 | tf_op jit(solution)/shard_map/whiten_rest/pallas_call | solution.py:98
  125.9 0.5 collective-permute-start.22
  126.4 8.2 %collective-permute-done.22 = bf16[64,1024]{1,0:T(8,128)(2,1)S(1)} collective-permute-done((bf16[64,1024]{1,0:T(8,128)(2,1)S(1)}, bf16[64,1024]{1,0:T(8,128)(2,1)S(1)}, u32[]{:S(2)}, u32[]{:S(2)}) %collective-permute-start.22) | collective-permute-done | bytes 131104 | tf_op jit(solution)/shard_map/ppermute | solution.py:192
  134.8 1.2 collective-permute-done.26
  136.0 0.6 fusion.47.raw_rest_ref
  136.7 0.6 pad_maximum_fusion.28.raw_given_ref
  137.3 9.4 %ritz.1 = (f32[192,128]{1,0:T(8,128)}, f32[1,64]{1,0:T(1,128)}) custom-call(f32[128,128]{1,0:T(8,128)} %whiten_given.1.given_ref, f32[64,192]{1,0:T(8,128)} %whiten_rest.1.rest_ref, f32[128,128]{1,0:T(8,128)} %pad_maximum_fusion.28.raw_given_ref, f32[64,192]{1,0:T(8,128)} %fusion.47.raw_rest_ref), custom_call_target="tpu_custom_call" | custom-call | flops 10000000000 | bytes 524288 | tf_op jit(solution)/shard_map/ritz/pallas_call | solution.py:159
  147.1 0.9 copy-done.1
  148.0 2.2 %fusion.8 = f32[4096,64]{0,1:T(8,128)} fusion(f32[64,4096]{1,0:T(8,128)S(1)} %convert_add_fusion, f32[64,4096]{1,0:T(8,128)S(1)} %bitcast.14, f32[64,4096]{1,0:T(8,128)S(1)} %bitcast.11, f32[192,128]{1,0:T(8,128)S(1)} %copy-done.9), kind=kOutput, calls=%fused_computation.11 | convolution fusion | flops 303562752 | bytes 4292608 | tf_op jit(solution)/shard_map/dot_general | solution.py:182
  150.2 2.1 %fusion.9 = f32[4096,64]{0,1:T(8,128)} fusion(f32[64,4096]{1,0:T(8,128)S(1)} %convert_add_fusion, f32[64,4096]{1,0:T(8,128)S(1)} %bitcast.15, f32[64,4096]{1,0:T(8,128)S(1)} %bitcast.12, f32[192,128]{1,0:T(8,128)S(1)} %copy-done.9), kind=kOutput, calls=%fused_computation.12 | convolution fusion | flops 303562752 | bytes 4292608 | tf_op jit(solution)/shard_map/dot_general | solution.py:182
  (107 shorter events, 4.5 us)
Async XLA Ops:
  2.6 1.0 copy-start.2
  2.6 7.3 %copy-start.5 = (bf16[128,4096]{1,0:T(8,128)(2,1)}, bf16[128,4096]{1,0:T(8,128)(2,1)S(1)}, u32[]{:S(2)}) copy-start(bf16[128,4096]{1,0:T(8,128)(2,1)S(1)} %get-tuple-element.32) | copy-start | bytes 3145732
  9.9 0.9 copy-start.4
  10.9 1.5 collective-permute-start
  12.4 6.8 %collective-permute-start.1 = (f32[64,512]{1,0:T(8,128)S(1)}, f32[64,512]{1,0:T(8,128)S(1)}, u32[]{:S(2)}, u32[]{:S(2)}) collective-permute-start(f32[64,512]{1,0:T(8,128)S(1)} %dynamic-slice_add_fusion.1), channel_id=1, source_target_pairs={{0,8},{8,0},{16,24},{24,16},{1,9},{9,1},{17,25},{25,17},{2,10},{10... | collective-permute-start | bytes 393224 | tf_op jit(solution)/shard_map/ppermute | solution.py:192
  15.3 8.1 %collective-permute-start.2 = (f32[64,512]{1,0:T(8,128)S(1)}, f32[64,512]{1,0:T(8,128)S(1)}, u32[]{:S(2)}, u32[]{:S(2)}) collective-permute-start(f32[64,512]{1,0:T(8,128)S(1)} %dynamic-slice_add_fusion.1), channel_id=1, source_target_pairs={{0,16},{8,24},{16,0},{24,8},{1,17},{9,25},{17,1},{25,9},{2,18},{10... | collective-permute-start | bytes 393224 | tf_op jit(solution)/shard_map/ppermute | solution.py:192
  16.8 6.6 %collective-permute-start.3 = (f32[64,512]{1,0:T(8,128)S(1)}, f32[64,512]{1,0:T(8,128)S(1)}, u32[]{:S(2)}, u32[]{:S(2)}) collective-permute-start(f32[64,512]{1,0:T(8,128)S(1)} %dynamic-slice_add_fusion.1), channel_id=1, source_target_pairs={{0,24},{8,16},{16,8},{24,0},{1,25},{9,17},{17,9},{25,1},{2,26},{10... | collective-permute-start | bytes 393224 | tf_op jit(solution)/shard_map/ppermute | solution.py:192
  23.5 1.3 collective-permute-start.4
  27.9 5.6 %copy-start.7 = (f32[64,2048]{1,0:T(8,128)}, f32[64,2048]{1,0:T(8,128)S(1)}, u32[]{:S(2)}) copy-start(f32[64,2048]{1,0:T(8,128)S(1)} %fusion.6) | copy-start | bytes 1572868
  28.1 6.7 %copy-start = (f32[4096,64]{0,1:T(8,128)S(1)}, f32[4096,64]{0,1:T(8,128)}, u32[]{:S(2)}) copy-start(f32[4096,64]{0,1:T(8,128)} %param.4) | copy-start | bytes 3145732
  28.9 16.1 %collective-permute-start.5 = (f32[64,1088]{1,0:T(8,128)}, f32[64,1088]{1,0:T(8,128)}, u32[]{:S(2)}, u32[]{:S(2)}) collective-permute-start(f32[64,1088]{1,0:T(8,128)} %pad_maximum_fusion.9), channel_id=1, source_target_pairs={{0,2},{2,0},{4,6},{6,4},{1,3},{3,1},{5,7},{7,5},{8,10},{10,8},{12,... | collective-permute-start | bytes 835592 | tf_op jit(solution)/shard_map/ppermute | solution.py:192
  33.5 0.9 copy-start.8
  34.4 9.5 %collective-permute-start.9 = (f32[64,1024]{1,0:T(8,128)}, f32[64,1024]{1,0:T(8,128)}, u32[]{:S(2)}, u32[]{:S(2)}) collective-permute-start(f32[64,1024]{1,0:T(8,128)} %constant_dynamic-slice_fusion.5), channel_id=1, source_target_pairs={{0,2},{2,0},{4,6},{6,4},{1,3},{3,1},{5,7},{7,5},{8,10},{10,8},{12,... | collective-permute-start | bytes 786440 | tf_op jit(solution)/shard_map/ppermute | solution.py:192
  35.9 15.4 %slice-start = ((f32[192,1024]{1,0:T(8,128)}), f32[128,1024]{1,0:T(8,128)S(1)}, s32[]{:S(2)}) async-start(f32[192,1024]{1,0:T(8,128)} %copy-done.4), calls=%async_computation | async-start | bytes 1048576 | tf_op jit(solution)/shard_map/slice | solution.py:314
  46.8 13.9 %collective-permute-start.6 = (f32[64,576]{1,0:T(8,128)S(1)}, f32[64,576]{1,0:T(8,128)S(1)}, u32[]{:S(2)}, u32[]{:S(2)}) collective-permute-start(f32[64,576]{1,0:T(8,128)S(1)} %pad_maximum_fusion.22), channel_id=1, source_target_pairs={{0,4},{2,6},{4,0},{6,2},{1,5},{3,7},{5,1},{7,3},{8,12},{10,14},{12... | collective-permute-start | bytes 442376 | tf_op jit(solution)/shard_map/ppermute | solution.py:192
  51.3 45.4 %slice-start.1 = ((s8[8388608]{0:T(1024)(128)(4,1)}), s8[4194304]{0:T(1024)(128)(4,1)S(1)}, s32[]{:S(2)}) async-start(s8[8388608]{0:T(1024)(128)(4,1)} %bitcast.16), calls=%async_computation.1 | async-start | bytes 8388608
  51.4 10.7 %collective-permute-start.11 = (f32[64,1280]{1,0:T(8,128)S(1)}, f32[64,1280]{1,0:T(8,128)S(1)}, u32[]{:S(2)}, u32[]{:S(2)}) collective-permute-start(f32[64,1280]{1,0:T(8,128)S(1)} %pad_maximum_fusion.5), channel_id=1, source_target_pairs={{0,1},{1,0},{2,3},{3,2},{4,5},{5,4},{6,7},{7,6},{8,9},{9,8},{10,11... | collective-permute-start | bytes 983048 | tf_op jit(solution)/shard_map/ppermute | solution.py:192
  51.5 14.2 %collective-permute-start.10 = (f32[64,512]{1,0:T(8,128)S(1)}, f32[64,512]{1,0:T(8,128)S(1)}, u32[]{:S(2)}, u32[]{:S(2)}) collective-permute-start(f32[64,512]{1,0:T(8,128)S(1)} %constant_dynamic-slice_fusion.4), channel_id=1, source_target_pairs={{0,4},{2,6},{4,0},{6,2},{1,5},{3,7},{5,1},{7,3},{8,12},{10,14},{12... | collective-permute-start | bytes 393224 | tf_op jit(solution)/shard_map/ppermute | solution.py:192
  62.0 6.0 %collective-permute-start.7 = (bf16[64,512]{1,0:T(8,128)(2,1)S(1)}, bf16[64,512]{1,0:T(8,128)(2,1)S(1)}, u32[]{:S(2)}, u32[]{:S(2)}) collective-permute-start(bf16[64,512]{1,0:T(8,128)(2,1)S(1)} %get-tuple-element.61), channel_id=1, source_target_pairs={{0,4},{2,6},{4,0},{6,2},{1,5},{3,7},{5,1},{7,3},{8,12},{10,14},{12... | collective-permute-start | bytes 196616 | tf_op jit(solution)/shard_map/ppermute | solution.py:192
  62.1 8.2 %collective-permute-start.12 = (f32[64,1280]{1,0:T(8,128)S(1)}, f32[64,1280]{1,0:T(8,128)S(1)}, u32[]{:S(2)}, u32[]{:S(2)}) collective-permute-start(f32[64,1280]{1,0:T(8,128)S(1)} %fusion.19), channel_id=1, source_target_pairs={{0,8},{8,0},{16,24},{24,16},{1,9},{9,1},{17,25},{25,17},{2,10},{10... | collective-permute-start | bytes 983048 | tf_op jit(solution)/shard_map/ppermute | solution.py:192
  63.4 11.4 %collective-permute-start.13 = (f32[64,1280]{1,0:T(8,128)S(1)}, f32[64,1280]{1,0:T(8,128)S(1)}, u32[]{:S(2)}, u32[]{:S(2)}) collective-permute-start(f32[64,1280]{1,0:T(8,128)S(1)} %fusion.19), channel_id=1, source_target_pairs={{0,16},{8,24},{16,0},{24,8},{1,17},{9,25},{17,1},{25,9},{2,18},{10... | collective-permute-start | bytes 983048 | tf_op jit(solution)/shard_map/ppermute | solution.py:192
  64.2 10.6 %collective-permute-start.14 = (f32[64,1280]{1,0:T(8,128)S(1)}, f32[64,1280]{1,0:T(8,128)S(1)}, u32[]{:S(2)}, u32[]{:S(2)}) collective-permute-start(f32[64,1280]{1,0:T(8,128)S(1)} %fusion.19), channel_id=1, source_target_pairs={{0,24},{8,16},{16,8},{24,0},{1,25},{9,17},{17,9},{25,1},{2,26},{10... | collective-permute-start | bytes 983048 | tf_op jit(solution)/shard_map/ppermute | solution.py:192
  74.9 8.7 %collective-permute-start.15 = (bf16[64,512]{1,0:T(8,128)(2,1)S(1)}, bf16[64,512]{1,0:T(8,128)(2,1)S(1)}, u32[]{:S(2)}, u32[]{:S(2)}) collective-permute-start(bf16[64,512]{1,0:T(8,128)(2,1)S(1)} %get-tuple-element.20), channel_id=1, source_target_pairs={{0,4},{2,6},{4,0},{6,2},{1,5},{3,7},{5,1},{7,3},{8,12},{10,14},{12... | collective-permute-start | bytes 196616 | tf_op jit(solution)/shard_map/ppermute | solution.py:192
  77.6 11.6 %collective-permute-start.8 = (bf16[64,1024]{1,0:T(8,128)(2,1)S(1)}, bf16[64,1024]{1,0:T(8,128)(2,1)S(1)}, u32[]{:S(2)}, u32[]{:S(2)}) collective-permute-start(bf16[64,1024]{1,0:T(8,128)(2,1)S(1)} %pad_maximum_fusion.24), channel_id=1, source_target_pairs={{0,2},{2,0},{4,6},{6,4},{1,3},{3,1},{5,7},{7,5},{8,10},{10,8},{12,... | collective-permute-start | bytes 393224 | tf_op jit(solution)/shard_map/ppermute | solution.py:192
  83.6 12.3 %copy-start.3 = (bf16[128,4096]{1,0:T(8,128)(2,1)S(1)}, bf16[128,4096]{1,0:T(8,128)(2,1)}, u32[]{:S(2)}) copy-start(bf16[128,4096]{1,0:T(8,128)(2,1)} %copy-done.2) | copy-start | bytes 3145732
  83.6 8.5 %collective-permute-start.16 = (bf16[64,1024]{1,0:T(8,128)(2,1)S(1)}, bf16[64,1024]{1,0:T(8,128)(2,1)S(1)}, u32[]{:S(2)}, u32[]{:S(2)}) collective-permute-start(bf16[64,1024]{1,0:T(8,128)(2,1)S(1)} %pad_maximum_fusion.25), channel_id=1, source_target_pairs={{0,2},{2,0},{4,6},{6,4},{1,3},{3,1},{5,7},{7,5},{8,10},{10,8},{12,... | collective-permute-start | bytes 393224 | tf_op jit(solution)/shard_map/ppermute | solution.py:192
  92.2 4.5 %slice-start.2 = ((s8[8388608]{0:T(1024)(128)(4,1)}), s8[4194304]{0:T(1024)(128)(4,1)S(1)}, s32[]{:S(2)}) async-start(s8[8388608]{0:T(1024)(128)(4,1)} %bitcast.16), calls=%async_computation.2 | async-start | bytes 8388608
  96.7 2.0 %copy-start.11 = (f32[64,64]{1,0:T(8,128)}, f32[64,64]{1,0:T(8,128)S(1)}, u32[]{:S(2)}) copy-start(f32[64,64]{1,0:T(8,128)S(1)} %fusion.70) | copy-start | bytes 49156
  96.7 1.4 copy-start.6
  98.7 0.6 copy-start.12
  99.3 1.4 collective-permute-start.17
  101.5 10.8 %collective-permute-start.18 = (f32[64,704]{1,0:T(8,128)S(1)}, f32[64,704]{1,0:T(8,128)S(1)}, u32[]{:S(2)}, u32[]{:S(2)}) collective-permute-start(f32[64,704]{1,0:T(8,128)S(1)} %fusion.28), channel_id=1, source_target_pairs={{0,8},{8,0},{16,24},{24,16},{1,9},{9,1},{17,25},{25,17},{2,10},{10... | collective-permute-start | bytes 540680 | tf_op jit(solution)/shard_map/ppermute | solution.py:192
  102.4 10.9 %collective-permute-start.19 = (f32[64,704]{1,0:T(8,128)S(1)}, f32[64,704]{1,0:T(8,128)S(1)}, u32[]{:S(2)}, u32[]{:S(2)}) collective-permute-start(f32[64,704]{1,0:T(8,128)S(1)} %fusion.28), channel_id=1, source_target_pairs={{0,16},{8,24},{16,0},{24,8},{1,17},{9,25},{17,1},{25,9},{2,18},{10... | collective-permute-start | bytes 540680 | tf_op jit(solution)/shard_map/ppermute | solution.py:192
  103.9 9.4 %collective-permute-start.20 = (f32[64,704]{1,0:T(8,128)S(1)}, f32[64,704]{1,0:T(8,128)}, u32[]{:S(2)}, u32[]{:S(2)}) collective-permute-start(f32[64,704]{1,0:T(8,128)S(1)} %fusion.28), channel_id=1, source_target_pairs={{0,24},{8,16},{16,8},{24,0},{1,25},{9,17},{17,9},{25,1},{2,26},{10... | collective-permute-start | bytes 540680 | tf_op jit(solution)/shard_map/ppermute | solution.py:192
  112.0 3.5 %copy-start.10 = (bf16[64,512]{1,0:T(8,128)(2,1)S(1)}, bf16[64,512]{1,0:T(8,128)(2,1)}, u32[]{:S(2)}) copy-start(bf16[64,512]{1,0:T(8,128)(2,1)} %get-tuple-element.66) | copy-start | bytes 196612
  115.4 1.3 collective-permute-start.21
  116.8 9.6 %collective-permute-start.23 = (f32[32,448]{1,0:T(8,128)S(1)}, f32[32,448]{1,0:T(8,128)S(1)}, u32[]{:S(2)}, u32[]{:S(2)}) collective-permute-start(f32[32,448]{1,0:T(8,128)S(1)} %dynamic-slice_add_fusion.2), channel_id=1, source_target_pairs={{0,2},{2,0},{4,6},{6,4},{1,3},{3,1},{5,7},{7,5},{8,10},{10,8},{12,... | collective-permute-start | bytes 172040 | tf_op jit(solution)/shard_map/ppermute | solution.py:192
  118.9 7.5 %collective-permute-start.24 = (f32[32,448]{1,0:T(8,128)S(1)}, f32[32,448]{1,0:T(8,128)S(1)}, u32[]{:S(2)}, u32[]{:S(2)}) collective-permute-start(f32[32,448]{1,0:T(8,128)S(1)} %dynamic-slice_add_fusion.2), channel_id=1, source_target_pairs={{0,4},{2,6},{4,0},{6,2},{1,5},{3,7},{5,1},{7,3},{8,12},{10,14},{12... | collective-permute-start | bytes 172040 | tf_op jit(solution)/shard_map/ppermute | solution.py:192
  118.9 7.5 %collective-permute-start.25 = (f32[32,448]{1,0:T(8,128)S(1)}, f32[32,448]{1,0:T(8,128)S(1)}, u32[]{:S(2)}, u32[]{:S(2)}) collective-permute-start(f32[32,448]{1,0:T(8,128)S(1)} %dynamic-slice_add_fusion.2), channel_id=1, source_target_pairs={{0,6},{2,4},{4,2},{6,0},{1,7},{3,5},{5,3},{7,1},{8,14},{10,12},{12... | collective-permute-start | bytes 172040 | tf_op jit(solution)/shard_map/ppermute | solution.py:192
  125.9 8.7 %collective-permute-start.22 = (bf16[64,1024]{1,0:T(8,128)(2,1)S(1)}, bf16[64,1024]{1,0:T(8,128)(2,1)S(1)}, u32[]{:S(2)}, u32[]{:S(2)}) collective-permute-start(bf16[64,1024]{1,0:T(8,128)(2,1)S(1)} %pad_maximum_fusion.26), channel_id=1, source_target_pairs={{0,4},{2,6},{4,0},{6,2},{1,5},{3,7},{5,1},{7,3},{8,12},{10,14},{12... | collective-permute-start | bytes 393224 | tf_op jit(solution)/shard_map/ppermute | solution.py:192
  134.7 1.3 collective-permute-start.26
  134.8 12.0 %collective-permute-start.27 = (bf16[64,2048]{1,0:T(8,128)(2,1)S(1)}, bf16[64,2048]{1,0:T(8,128)(2,1)S(1)}, u32[]{:S(2)}, u32[]{:S(2)}) collective-permute-start(bf16[64,2048]{1,0:T(8,128)(2,1)S(1)} %pad_maximum_fusion.16), channel_id=1, source_target_pairs={{0,2},{2,0},{4,6},{6,4},{1,3},{3,1},{5,7},{7,5},{8,10},{10,8},{12,... | collective-permute-start | bytes 786440 | tf_op jit(solution)/shard_map/ppermute | solution.py:192
  146.8 1.2 copy-start.1
  146.8 1.2 copy-start.9

commit v6 on v3

--- a/solution.py
+++ b/solution.py
@@ -235,8 +235,18 @@
     return value
 
 
+def gather_direct(value, axis):
+    if lax.axis_size(axis) != 4:
+        return gather_halves(value, axis)
+    near, far, across = (swap(value, axis, step) for step in (1, 2, 3))
+    return beside(beside(value, far, axis, 2), beside(near, across, axis, 2), axis, 1)
+
+
 def joined_halves(value, axis, step):
-    other = swap(value, axis, step)
+    return beside(value, swap(value, axis, step), axis, step)
+
+
+def beside(value, other, axis, step):
     first = side_of(axis, step) == 0
     return jnp.concatenate([jnp.where(first, value, other), jnp.where(first, other, value)], axis=1)
 
@@ -385,10 +395,7 @@
     raw_rest = raw[:, : 3 * cols]
     raw_given = jnp.concatenate([raw[:, 3 * cols : 5 * cols], raw[:, 5 * cols :]], axis=0)
     all_coeffs, ritz_values = ritz_of(given_inverse, rest_inverse, raw_given, raw_rest)
-    for step in reversed(token_steps):
-        if step == token_steps[0]:
-            residual_lo = after(residual_lo, raw)
-        residual_lo = joined_halves(residual_lo, "token", step)
+    residual_lo = gather_direct(residual_lo, "token")
     residual_rows = search_rows.astype(jnp.float32) + reordered(residual_lo, CHUNKS).astype(jnp.float32)
     search_basis = jnp.concatenate([x_rows, d_rows, residual_rows], axis=0)
     new_block = moved(all_coeffs[:, :cols], search_basis)

time: 131 us -> 138 us (1.053)
  waiting for transfers between devices: 47.4 us -> 52.5 us
  starting transfers between devices: 27.3 us -> 30.9 us
  other arithmetic: 7.43 us -> 5.6 us
    ppermute x28 -> x29, waiting for transfers between devices: 47.4 us -> 52.5 us  [swap(): lax.ppermute(value, axis, [(i, i ^ step) for i in range(lax.axis_size(axi...]
    ppermute x28 -> x29, starting transfers between devices: 27.3 us -> 30.9 us  [swap(): lax.ppermute(value, axis, [(i, i ^ step) for i in range(lax.axis_size(axi...]
  transfers between devices with their start and end apart: 28 -> 29, of which waited for: 16 -> 17; matrix products, arithmetic and copies ran while one was open for 9% -> 7% of each run, Pallas kernels for 8% -> 7%
where the time goes in v6:
time: 138 us; the launch traced here: 137 us
  waiting for transfers between devices  52.5 us (38%)
  starting transfers between devices  30.9 us (22%)
  matrix products  26 us (19%)
  Pallas kernels  19.3 us (14%)
  other arithmetic  5.6 us (4%)
  between operations  1.43 us (1%)
  local copies, waits for them, and re-layouts  1.4 us (1%)
    ppermute x29, waiting for transfers between devices, swap(): lax.ppermute(value, axis, [(i, i ^ step) for i in range(lax.axis_size(axi...  52.5 us
    ppermute x29, starting transfers between devices, swap(): lax.ppermute(value, axis, [(i, i ^ step) for i in range(lax.axis_size(axi...  30.9 us
    dot_general x7, matrix products, probe_of(): lax.dot_general(rows_b, slab_part, (((1,), (1,)), ((), ())), preferred_el...  10.5 us
    pallas_call x1, Pallas kernels, ritz_of(): pl.pallas_call(ritz_kernel, out_shape=(jax.ShapeDtypeStruct((size, 2 * co...  9.29 us
    dot_general x2, matrix products, local(): part = jnp.dot(probe, slab, preferred_element_type=jnp.float32)  6.21 us
    pallas_call x1, Pallas kernels, whiten_given(): pl.pallas_call(whiten_given_kernel, out_shape=jax.ShapeDtypeStruct(gram_m...  6.03 us
    dot_general x2, matrix products, moved(): lax.dot_general(coeffs, rows, (((0,), (0,)), ((), ())), precision=lax.Pre...  5.2 us
    pallas_call x1, Pallas kernels, whiten_rest(): pl.pallas_call(whiten_rest_kernel, out_shape=jax.ShapeDtypeStruct(gram_ro...  3.98 us
  transfers between devices with their start and end apart: 29, of which 17 were waited for; matrix products, arithmetic and copies ran while one was open for 7% of the time, Pallas kernels for 7%

profile of v6, /device:TPU:0, one launch (start us, length us, event | category | flops | bytes accessed | tf_op | source)
XLA Modules:
  0.0 137.2 jit_solution(4606535431546623796)
XLA Ops:
  0.6 1.9 %pad_maximum_fusion.3 = (f32[128,4096]{1,0:T(8,128)S(1)}, bf16[128,4096]{1,0:T(8,128)(2,1)S(1)}, bf16[128,4096]{1,0:T(8,128)(2,1)S(1)}) fusion(f32[64,4096]{1,0:T(8,128)} %bitcast.13, f32[64,4096]{1,0:T(8,128)} %bitcast.9), kind=kLoop, calls=%fused_computation.14 | loop fusion | flops 2621440 | bytes 6291456 | tf_op jit(solution)/shard_map/concatenate | solution.py:292
  2.6 0.9 copy-done.2
  3.6 6.3 %fusion.11 = f32[192,1024]{1,0:T(8,128)S(1)} fusion(bf16[1024,4096]{1,0:T(8,128)(2,1)} %param.3, bf16[64,4096]{1,0:T(8,128)(2,1)S(1)} %slice.155, bf16[128,4096]{1,0:T(8,128)(2,1)S(1)} %get-tuple-element.24), kind=kOutput, calls=%fused_computation.15 | convolution fusion | flops 1613758464 | bytes 10747904 | tf_op jit(solution)/shard_map/dot_general | solution.py:261
  10.0 0.5 collective-permute-start
  10.5 1.0 collective-permute-done
  11.5 3.9 %collective-permute-start.3 = (f32[64,512]{1,0:T(8,128)S(1)}, f32[64,512]{1,0:T(8,128)S(1)}, u32[]{:S(2)}, u32[]{:S(2)}) collective-permute-start(f32[64,512]{1,0:T(8,128)S(1)} %dynamic-slice_add_fusion.1), channel_id=1, source_target_pairs={{0,24},{8,16},{16,8},{24,0},{1,25},{9,17},{17,9},{25,1},{2,26},{10... | collective-permute-start | bytes 393224 | tf_op jit(solution)/shard_map/ppermute | solution.py:192
  15.4 0.5 collective-permute-start.2
  16.0 3.3 %collective-permute-done.3 = f32[64,512]{1,0:T(8,128)S(1)} collective-permute-done((f32[64,512]{1,0:T(8,128)S(1)}, f32[64,512]{1,0:T(8,128)S(1)}, u32[]{:S(2)}, u32[]{:S(2)}) %collective-permute-start.3) | collective-permute-done | bytes 131104 | tf_op jit(solution)/shard_map/ppermute | solution.py:192
  19.3 2.7 %collective-permute-done.2 = f32[64,512]{1,0:T(8,128)S(1)} collective-permute-done((f32[64,512]{1,0:T(8,128)S(1)}, f32[64,512]{1,0:T(8,128)S(1)}, u32[]{:S(2)}, u32[]{:S(2)}) %collective-permute-start.2) | collective-permute-done | bytes 131104 | tf_op jit(solution)/shard_map/ppermute | solution.py:192
  22.0 0.3 collective-permute-done.1
  22.5 1.2 collective-permute-done.4
  23.7 0.2 fusion.67
  23.9 3.0 %fusion.6 = f32[64,2048]{1,0:T(8,128)S(1)} fusion(bf16[1024,4096]{1,0:T(8,128)(2,1)} %param.3, bf16[64,512]{1,0:T(8,128)(2,1)S(1)} %get-tuple-element.60, bf16[64,512]{1,0:T(8,128)(2,1)S(1)} %get-tuple-element.59), kind=kOutput, calls=%fused_computation.6 | convolution fusion | flops 268697600 | bytes 4849664 | tf_op jit(solution)/shard_map/dot_general | solution.py:304
  27.0 3.2 %fusion.2 = f32[64,2048]{1,0:T(8,128)S(1)} fusion(bf16[64,1024]{1,0:T(8,128)(2,1)S(1)} %pad_maximum_fusion.23, bf16[1024,4096]{1,0:T(8,128)(2,1)} %param.3), kind=kOutput, calls=%fused_computation.2 | convolution fusion | flops 268435456 | bytes 4849664 | tf_op jit(solution)/shard_map/dot_general | solution.py:304
  30.2 1.6 %collective-permute-start.9 = (f32[64,1024]{1,0:T(8,128)S(1)}, f32[64,1024]{1,0:T(8,128)S(1)}, u32[]{:S(2)}, u32[]{:S(2)}) collective-permute-start(f32[64,1024]{1,0:T(8,128)S(1)} %constant_dynamic-slice_fusion.5), channel_id=1, source_target_pairs={{0,2},{2,0},{4,6},{6,4},{1,3},{3,1},{5,7},{7,5},{8,10},{10,8},{12,... | collective-permute-start | bytes 786440 | tf_op jit(solution)/shard_map/ppermute | solution.py:192
  32.0 0.5 collective-permute-start.5
  32.5 7.0 %collective-permute-done.9 = f32[64,1024]{1,0:T(8,128)S(1)} collective-permute-done((f32[64,1024]{1,0:T(8,128)S(1)}, f32[64,1024]{1,0:T(8,128)S(1)}, u32[]{:S(2)}, u32[]{:S(2)}) %collective-permute-start.9) | collective-permute-done | bytes 262176 | tf_op jit(solution)/shard_map/ppermute | solution.py:192
  39.5 2.7 %collective-permute-start.10 = (f32[64,512]{1,0:T(8,128)S(1)}, f32[64,512]{1,0:T(8,128)S(1)}, u32[]{:S(2)}, u32[]{:S(2)}) collective-permute-start(f32[64,512]{1,0:T(8,128)S(1)} %constant_dynamic-slice_fusion.4), channel_id=1, source_target_pairs={{0,4},{2,6},{4,0},{6,2},{1,5},{3,7},{5,1},{7,3},{8,12},{10,14},{12... | collective-permute-start | bytes 393224 | tf_op jit(solution)/shard_map/ppermute | solution.py:192
  42.2 5.6 %collective-permute-done.5 = f32[64,1088]{1,0:T(8,128)S(1)} collective-permute-done((f32[64,1088]{1,0:T(8,128)S(1)}, f32[64,1088]{1,0:T(8,128)S(1)}, u32[]{:S(2)}, u32[]{:S(2)}) %collective-permute-start.5) | collective-permute-done | bytes 278560 | tf_op jit(solution)/shard_map/ppermute | solution.py:192
  47.9 1.2 collective-permute-start.6
  49.1 1.8 %fusion.75 = f32[128,128]{1,0:T(8,128)S(1)} fusion(f32[128,4096]{1,0:T(8,128)S(1)} %get-tuple-element.15), kind=kOutput, calls=%fused_computation.152 | convolution fusion | flops 805306368 | bytes 2162688 | tf_op jit(solution)/shard_map/dot_general | solution.py:22
  51.1 6.7 %collective-permute-done.6 = f32[64,576]{1,0:T(8,128)S(1)} collective-permute-done((f32[64,576]{1,0:T(8,128)S(1)}, f32[64,576]{1,0:T(8,128)S(1)}, u32[]{:S(2)}, u32[]{:S(2)}) %collective-permute-start.6) | collective-permute-done | bytes 147488 | tf_op jit(solution)/shard_map/ppermute | solution.py:192
  57.8 0.4 reduce-precision_convert_fusion.2
  58.3 0.4 reduce-precision_convert_fusion.1
  58.7 3.0 %collective-permute-start.11 = (bf16[64,512]{1,0:T(8,128)(2,1)S(1)}, bf16[64,512]{1,0:T(8,128)(2,1)S(1)}, u32[]{:S(2)}, u32[]{:S(2)}) collective-permute-start(bf16[64,512]{1,0:T(8,128)(2,1)S(1)} %get-tuple-element.57), channel_id=1, source_target_pairs={{0,4},{2,6},{4,0},{6,2},{1,5},{3,7},{5,1},{7,3},{8,12},{10,14},{12... | collective-permute-start | bytes 196616 | tf_op jit(solution)/shard_map/ppermute | solution.py:192
  61.7 3.2 %collective-permute-done.7 = bf16[64,512]{1,0:T(8,128)(2,1)S(1)} collective-permute-done((bf16[64,512]{1,0:T(8,128)(2,1)S(1)}, bf16[64,512]{1,0:T(8,128)(2,1)S(1)}, u32[]{:S(2)}, u32[]{:S(2)}) %collective-permute-start.7) | collective-permute-done | bytes 65568 | tf_op jit(solution)/shard_map/ppermute | solution.py:192
  65.0 1.7 %collective-permute-done.11 = bf16[64,512]{1,0:T(8,128)(2,1)S(1)} collective-permute-done((bf16[64,512]{1,0:T(8,128)(2,1)S(1)}, bf16[64,512]{1,0:T(8,128)(2,1)S(1)}, u32[]{:S(2)}, u32[]{:S(2)}) %collective-permute-start.11) | collective-permute-done | bytes 65568 | tf_op jit(solution)/shard_map/ppermute | solution.py:192
  66.7 0.4 collective-permute-start.12
  67.1 1.6 %collective-permute-start.19 = (f32[64,1280]{1,0:T(8,128)S(1)}, f32[64,1280]{1,0:T(8,128)S(1)}, u32[]{:S(2)}, u32[]{:S(2)}) collective-permute-start(f32[64,1280]{1,0:T(8,128)S(1)} %fusion.19), channel_id=1, source_target_pairs={{0,24},{8,16},{16,8},{24,0},{1,25},{9,17},{17,9},{25,1},{2,26},{10... | collective-permute-start | bytes 983048 | tf_op jit(solution)/shard_map/ppermute | solution.py:192
  68.8 1.4 %collective-permute-start.18 = (f32[64,1280]{1,0:T(8,128)S(1)}, f32[64,1280]{1,0:T(8,128)S(1)}, u32[]{:S(2)}, u32[]{:S(2)}) collective-permute-start(f32[64,1280]{1,0:T(8,128)S(1)} %fusion.19), channel_id=1, source_target_pairs={{0,16},{8,24},{16,0},{24,8},{1,17},{9,25},{17,1},{25,9},{2,18},{10... | collective-permute-start | bytes 983048 | tf_op jit(solution)/shard_map/ppermute | solution.py:192
  70.2 0.5 collective-permute-start.17
  70.7 2.0 %collective-permute-done.12 = bf16[64,1024]{1,0:T(8,128)(2,1)S(1)} collective-permute-done((bf16[64,1024]{1,0:T(8,128)(2,1)S(1)}, bf16[64,1024]{1,0:T(8,128)(2,1)S(1)}, u32[]{:S(2)}, u32[]{:S(2)}) %collective-permute-start.12) | collective-permute-done | bytes 131104 | tf_op jit(solution)/shard_map/ppermute | solution.py:192
  72.8 1.4 %fusion = f32[64,1024]{1,0:T(8,128)S(1)} fusion(bf16[1024,4096]{1,0:T(8,128)(2,1)S(1)} %bitcast.17, bf16[64,1024]{1,0:T(8,128)(2,1)S(1)} %get-tuple-element.48, bf16[64,1024]{1,0:T(8,128)(2,1)S(1)} %get-tuple-element.47), kind=kOutput, calls=%fused_computation | convolution fusion | flops 268959744 | bytes 4718592 | tf_op jit(solution)/shard_map/dot_general | solution.py:261
  74.3 0.5 fusion.69
  74.8 1.4 %fusion.15 = f32[64,1024]{1,0:T(8,128)S(1)} fusion(f32[64,1024]{1,0:T(8,128)S(1)} %fusion, bf16[1024,4096]{1,0:T(8,128)(2,1)S(1)} %bitcast.17, bf16[64,1024]{1,0:T(8,128)(2,1)S(1)} %get-tuple-element.46, bf16[64,1024]{1,0:T(8,128)(2,1)S(1)} %get-tuple-element.45), kind=kOutput, calls=%fused_computation.19 | convolution fusion | flops 269025280 | bytes 4980736 | tf_op jit(solution)/shard_map/dot_general | solution.py:261
  76.2 2.4 %collective-permute-start.13 = (bf16[64,1024]{1,0:T(8,128)(2,1)S(1)}, bf16[64,1024]{1,0:T(8,128)(2,1)S(1)}, u32[]{:S(2)}, u32[]{:S(2)}) collective-permute-start(bf16[64,1024]{1,0:T(8,128)(2,1)S(1)} %pad_maximum_fusion.26), channel_id=1, source_target_pairs={{0,4},{2,6},{4,0},{6,2},{1,5},{3,7},{5,1},{7,3},{8,12},{10,14},{12... | collective-permute-start | bytes 393224 | tf_op jit(solution)/shard_map/ppermute | solution.py:192
  78.7 0.5 convolution_add_fusion
  79.2 0.3 fusion.68
  79.5 5.2 %collective-permute-done.13 = bf16[64,1024]{1,0:T(8,128)(2,1)S(1)} collective-permute-done((bf16[64,1024]{1,0:T(8,128)(2,1)S(1)}, bf16[64,1024]{1,0:T(8,128)(2,1)S(1)}, u32[]{:S(2)}, u32[]{:S(2)}) %collective-permute-start.13) | collective-permute-done | bytes 131104 | tf_op jit(solution)/shard_map/ppermute | solution.py:192
  84.8 1.9 %collective-permute-start.15 = (bf16[64,1024]{1,0:T(8,128)(2,1)S(1)}, bf16[64,1024]{1,0:T(8,128)(2,1)S(1)}, u32[]{:S(2)}, u32[]{:S(2)}) collective-permute-start(bf16[64,1024]{1,0:T(8,128)(2,1)S(1)} %pad_maximum_fusion.26), channel_id=1, source_target_pairs={{0,6},{2,4},{4,2},{6,0},{1,7},{3,5},{5,3},{7,1},{8,14},{10,12},{12... | collective-permute-start | bytes 393224 | tf_op jit(solution)/shard_map/ppermute | solution.py:192
  86.8 4.7 %collective-permute-done.15 = bf16[64,1024]{1,0:T(8,128)(2,1)S(1)} collective-permute-done((bf16[64,1024]{1,0:T(8,128)(2,1)S(1)}, bf16[64,1024]{1,0:T(8,128)(2,1)S(1)}, u32[]{:S(2)}, u32[]{:S(2)}) %collective-permute-start.15) | collective-permute-done | bytes 131104 | tf_op jit(solution)/shard_map/ppermute | solution.py:192
  91.9 1.9 %collective-permute-start.23 = (f32[64,704]{1,0:T(8,128)S(1)}, f32[64,704]{1,0:T(8,128)S(1)}, u32[]{:S(2)}, u32[]{:S(2)}) collective-permute-start(f32[64,704]{1,0:T(8,128)S(1)} %fusion.28), channel_id=1, source_target_pairs={{0,24},{8,16},{16,8},{24,0},{1,25},{9,17},{17,9},{25,1},{2,26},{10... | collective-permute-start | bytes 540680 | tf_op jit(solution)/shard_map/ppermute | solution.py:192
  93.8 1.1 collective-permute-start.22
  94.9 0.5 collective-permute-start.21
  95.6 0.6 maximum_multiply_fusion.gram_ref
  96.3 0.5 fusion.26
  96.8 1.8 %collective-permute-done.23 = f32[64,704]{1,0:T(8,128)S(1)} collective-permute-done((f32[64,704]{1,0:T(8,128)S(1)}, f32[64,704]{1,0:T(8,128)S(1)}, u32[]{:S(2)}, u32[]{:S(2)}) %collective-permute-start.23) | collective-permute-done | bytes 180256 | tf_op jit(solution)/shard_map/ppermute | solution.py:192
  98.7 2.0 %collective-permute-done.22 = f32[64,704]{1,0:T(8,128)S(1)} collective-permute-done((f32[64,704]{1,0:T(8,128)S(1)}, f32[64,704]{1,0:T(8,128)S(1)}, u32[]{:S(2)}, u32[]{:S(2)}) %collective-permute-start.22) | collective-permute-done | bytes 180256 | tf_op jit(solution)/shard_map/ppermute | solution.py:192
  100.7 0.3 fusion.29
  101.0 0.4 fusion.27
  101.4 0.4 fusion.18
  102.0 6.0 %whiten_given.1.given_ref = f32[128,128]{1,0:T(8,128)} custom-call(f32[128,128]{1,0:T(8,128)} %maximum_multiply_fusion.gram_ref), custom_call_target="tpu_custom_call" | custom-call | flops 4000000000 | bytes 131072 | tf_op jit(solution)/shard_map/whiten_given/pallas_call | solution.py:81
  108.0 2.0 %collective-permute-start.27 = (f32[32,448]{1,0:T(8,128)S(1)}, f32[32,448]{1,0:T(8,128)S(1)}, u32[]{:S(2)}, u32[]{:S(2)}) collective-permute-start(f32[32,448]{1,0:T(8,128)S(1)} %dynamic-slice_add_fusion.2), channel_id=1, source_target_pairs={{0,6},{2,4},{4,2},{6,0},{1,7},{3,5},{5,3},{7,1},{8,14},{10,12},{12... | collective-permute-start | bytes 172040 | tf_op jit(solution)/shard_map/ppermute | solution.py:192
  110.1 0.3 collective-permute-start.26
  110.4 2.1 %collective-permute-start.25 = (f32[32,448]{1,0:T(8,128)S(1)}, f32[32,448]{1,0:T(8,128)S(1)}, u32[]{:S(2)}, u32[]{:S(2)}) collective-permute-start(f32[32,448]{1,0:T(8,128)S(1)} %dynamic-slice_add_fusion.2), channel_id=1, source_target_pairs={{0,2},{2,0},{4,6},{6,4},{1,3},{3,1},{5,7},{7,5},{8,10},{10,8},{12,... | collective-permute-start | bytes 172040 | tf_op jit(solution)/shard_map/ppermute | solution.py:192
  112.5 0.6 broadcast_multiply_fusion.gram_ref
  113.1 1.8 %collective-permute-done.27 = f32[32,448]{1,0:T(8,128)S(1)} collective-permute-done((f32[32,448]{1,0:T(8,128)S(1)}, f32[32,448]{1,0:T(8,128)S(1)}, u32[]{:S(2)}, u32[]{:S(2)}) %collective-permute-start.27) | collective-permute-done | bytes 57376 | tf_op jit(solution)/shard_map/ppermute | solution.py:192
  114.9 2.3 %collective-permute-done.26 = f32[32,448]{1,0:T(8,128)S(1)} collective-permute-done((f32[32,448]{1,0:T(8,128)S(1)}, f32[32,448]{1,0:T(8,128)S(1)}, u32[]{:S(2)}, u32[]{:S(2)}) %collective-permute-start.26) | collective-permute-done | bytes 57376 | tf_op jit(solution)/shard_map/ppermute | solution.py:192
  117.3 4.0 %whiten_rest.1.rest_ref = f32[64,192]{1,0:T(8,128)} custom-call(f32[128,128]{1,0:T(8,128)} %whiten_given.1.given_ref, f32[64,192]{1,0:T(8,128)} %broadcast_multiply_fusion.gram_ref), custom_call_target="tpu_custom_call" | custom-call | flops 3000000000 | bytes 131072 | tf_op jit(solution)/shard_map/whiten_rest/pallas_call | solution.py:98
  121.3 0.7 fusion.47.raw_given_ref
  122.0 0.6 pad_maximum_fusion.28.raw_rest_ref
  122.7 9.3 %ritz.1 = (f32[192,128]{1,0:T(8,128)}, f32[1,64]{1,0:T(1,128)}) custom-call(f32[128,128]{1,0:T(8,128)} %whiten_given.1.given_ref, f32[64,192]{1,0:T(8,128)} %whiten_rest.1.rest_ref, f32[128,128]{1,0:T(8,128)} %fusion.47.raw_given_ref, f32[64,192]{1,0:T(8,128)} %pad_maximum_fusion.28.raw_rest_ref), custom_call_target="tpu_custom_call" | custom-call | flops 10000000000 | bytes 524288 | tf_op jit(solution)/shard_map/ritz/pallas_call | solution.py:159
  132.0 3.1 %fusion.8 = f32[4096,64]{0,1:T(8,128)} fusion(f32[64,4096]{1,0:T(8,128)S(1)} %convert_add_fusion, f32[64,4096]{1,0:T(8,128)S(1)} %bitcast.14, f32[64,4096]{1,0:T(8,128)S(1)} %bitcast.11, f32[192,128]{1,0:T(8,128)} %get-tuple-element.19), kind=kOutput, calls=%fused_computation.11 | convolution fusion | flops 303562752 | bytes 4292608 | tf_op jit(solution)/shard_map/dot_general | solution.py:182
  135.1 2.1 %fusion.9 = f32[4096,64]{0,1:T(8,128)} fusion(f32[64,4096]{1,0:T(8,128)S(1)} %convert_add_fusion, f32[64,4096]{1,0:T(8,128)S(1)} %bitcast.15, f32[64,4096]{1,0:T(8,128)S(1)} %bitcast.12, f32[192,128]{1,0:T(8,128)S(1)} %copy-done.7), kind=kOutput, calls=%fused_computation.12 | convolution fusion | flops 303562752 | bytes 4292608 | tf_op jit(solution)/shard_map/dot_general | solution.py:182
  (98 shorter events, 2.3 us)
Async XLA Ops:
  2.6 1.0 copy-start.2
  2.6 7.3 %copy-start.5 = (bf16[128,4096]{1,0:T(8,128)(2,1)}, bf16[128,4096]{1,0:T(8,128)(2,1)S(1)}, u32[]{:S(2)}) copy-start(bf16[128,4096]{1,0:T(8,128)(2,1)S(1)} %get-tuple-element.24) | copy-start | bytes 3145732
  9.9 17.0 %copy-start.4 = (f32[192,1024]{1,0:T(8,128)}, f32[192,1024]{1,0:T(8,128)S(1)}, u32[]{:S(2)}) copy-start(f32[192,1024]{1,0:T(8,128)S(1)} %fusion.11) | copy-start | bytes 2359300
  10.0 1.5 %collective-permute-start = (f32[64,512]{1,0:T(8,128)S(1)}, f32[64,512]{1,0:T(8,128)S(1)}, u32[]{:S(2)}, u32[]{:S(2)}) collective-permute-start(f32[64,512]{1,0:T(8,128)S(1)} %constant_dynamic-slice_fusion.9), channel_id=1, source_target_pairs={{0,1},{1,0},{2,3},{3,2},{4,5},{5,4},{6,7},{7,6},{8,9},{9,8},{10,11... | collective-permute-start | bytes 393224 | tf_op jit(solution)/shard_map/ppermute | solution.py:192
  11.5 7.8 %collective-permute-start.3 = (f32[64,512]{1,0:T(8,128)S(1)}, f32[64,512]{1,0:T(8,128)S(1)}, u32[]{:S(2)}, u32[]{:S(2)}) collective-permute-start(f32[64,512]{1,0:T(8,128)S(1)} %dynamic-slice_add_fusion.1), channel_id=1, source_target_pairs={{0,24},{8,16},{16,8},{24,0},{1,25},{9,17},{17,9},{25,1},{2,26},{10... | collective-permute-start | bytes 393224 | tf_op jit(solution)/shard_map/ppermute | solution.py:192
  15.4 6.6 %collective-permute-start.2 = (f32[64,512]{1,0:T(8,128)S(1)}, f32[64,512]{1,0:T(8,128)S(1)}, u32[]{:S(2)}, u32[]{:S(2)}) collective-permute-start(f32[64,512]{1,0:T(8,128)S(1)} %dynamic-slice_add_fusion.1), channel_id=1, source_target_pairs={{0,16},{8,24},{16,0},{24,8},{1,17},{9,25},{17,1},{25,9},{2,18},{10... | collective-permute-start | bytes 393224 | tf_op jit(solution)/shard_map/ppermute | solution.py:192
  15.9 6.4 %collective-permute-start.1 = (f32[64,512]{1,0:T(8,128)S(1)}, f32[64,512]{1,0:T(8,128)S(1)}, u32[]{:S(2)}, u32[]{:S(2)}) collective-permute-start(f32[64,512]{1,0:T(8,128)S(1)} %dynamic-slice_add_fusion.1), channel_id=1, source_target_pairs={{0,8},{8,0},{16,24},{24,16},{1,9},{9,1},{17,25},{25,17},{2,10},{10... | collective-permute-start | bytes 393224 | tf_op jit(solution)/shard_map/ppermute | solution.py:192
  22.3 1.3 collective-permute-start.4
  27.0 4.9 %copy-start = (f32[4096,64]{0,1:T(8,128)S(1)}, f32[4096,64]{0,1:T(8,128)}, u32[]{:S(2)}) copy-start(f32[4096,64]{0,1:T(8,128)} %param.4) | copy-start | bytes 3145732
  27.0 45.8 %slice-start.1 = ((s8[8388608]{0:T(1024)(128)(4,1)}), s8[4194304]{0:T(1024)(128)(4,1)S(1)}, s32[]{:S(2)}) async-start(s8[8388608]{0:T(1024)(128)(4,1)} %bitcast.16), calls=%async_computation.1 | async-start | bytes 8388608
  30.2 9.2 %collective-permute-start.9 = (f32[64,1024]{1,0:T(8,128)S(1)}, f32[64,1024]{1,0:T(8,128)S(1)}, u32[]{:S(2)}, u32[]{:S(2)}) collective-permute-start(f32[64,1024]{1,0:T(8,128)S(1)} %constant_dynamic-slice_fusion.5), channel_id=1, source_target_pairs={{0,2},{2,0},{4,6},{6,4},{1,3},{3,1},{5,7},{7,5},{8,10},{10,8},{12,... | collective-permute-start | bytes 786440 | tf_op jit(solution)/shard_map/ppermute | solution.py:192
  32.0 15.8 %collective-permute-start.5 = (f32[64,1088]{1,0:T(8,128)S(1)}, f32[64,1088]{1,0:T(8,128)S(1)}, u32[]{:S(2)}, u32[]{:S(2)}) collective-permute-start(f32[64,1088]{1,0:T(8,128)S(1)} %pad_maximum_fusion.9), channel_id=1, source_target_pairs={{0,2},{2,0},{4,6},{6,4},{1,3},{3,1},{5,7},{7,5},{8,10},{10,8},{12,... | collective-permute-start | bytes 835592 | tf_op jit(solution)/shard_map/ppermute | solution.py:192
  39.5 11.4 %slice-start = ((f32[192,1024]{1,0:T(8,128)}), f32[128,1024]{1,0:T(8,128)S(1)}, s32[]{:S(2)}) async-start(f32[192,1024]{1,0:T(8,128)} %copy-done.4), calls=%async_computation | async-start | bytes 1048576 | tf_op jit(solution)/shard_map/slice | solution.py:324
  39.5 18.8 %collective-permute-start.10 = (f32[64,512]{1,0:T(8,128)S(1)}, f32[64,512]{1,0:T(8,128)S(1)}, u32[]{:S(2)}, u32[]{:S(2)}) collective-permute-start(f32[64,512]{1,0:T(8,128)S(1)} %constant_dynamic-slice_fusion.4), channel_id=1, source_target_pairs={{0,4},{2,6},{4,0},{6,2},{1,5},{3,7},{5,1},{7,3},{8,12},{10,14},{12... | collective-permute-start | bytes 393224 | tf_op jit(solution)/shard_map/ppermute | solution.py:192
  47.9 24.9 %slice-start.2 = ((s8[8388608]{0:T(1024)(128)(4,1)}), s8[4194304]{0:T(1024)(128)(4,1)S(1)}, s32[]{:S(2)}) async-start(s8[8388608]{0:T(1024)(128)(4,1)} %bitcast.16), calls=%async_computation.2 | async-start | bytes 8388608
  47.9 9.9 %collective-permute-start.6 = (f32[64,576]{1,0:T(8,128)S(1)}, f32[64,576]{1,0:T(8,128)S(1)}, u32[]{:S(2)}, u32[]{:S(2)}) collective-permute-start(f32[64,576]{1,0:T(8,128)S(1)} %pad_maximum_fusion.22), channel_id=1, source_target_pairs={{0,4},{2,6},{4,0},{6,2},{1,5},{3,7},{5,1},{7,3},{8,12},{10,14},{12... | collective-permute-start | bytes 442376 | tf_op jit(solution)/shard_map/ppermute | solution.py:192
  51.0 16.1 %collective-permute-start.16 = (f32[64,1280]{1,0:T(8,128)S(1)}, f32[64,1280]{1,0:T(8,128)S(1)}, u32[]{:S(2)}, u32[]{:S(2)}) collective-permute-start(f32[64,1280]{1,0:T(8,128)S(1)} %pad_maximum_fusion.5), channel_id=1, source_target_pairs={{0,1},{1,0},{2,3},{3,2},{4,5},{5,4},{6,7},{7,6},{8,9},{9,8},{10,11... | collective-permute-start | bytes 983048 | tf_op jit(solution)/shard_map/ppermute | solution.py:192
  58.2 6.6 %collective-permute-start.7 = (bf16[64,512]{1,0:T(8,128)(2,1)S(1)}, bf16[64,512]{1,0:T(8,128)(2,1)S(1)}, u32[]{:S(2)}, u32[]{:S(2)}) collective-permute-start(bf16[64,512]{1,0:T(8,128)(2,1)S(1)} %get-tuple-element.53), channel_id=1, source_target_pairs={{0,4},{2,6},{4,0},{6,2},{1,5},{3,7},{5,1},{7,3},{8,12},{10,14},{12... | collective-permute-start | bytes 196616 | tf_op jit(solution)/shard_map/ppermute | solution.py:192
  58.7 8.0 %collective-permute-start.11 = (bf16[64,512]{1,0:T(8,128)(2,1)S(1)}, bf16[64,512]{1,0:T(8,128)(2,1)S(1)}, u32[]{:S(2)}, u32[]{:S(2)}) collective-permute-start(bf16[64,512]{1,0:T(8,128)(2,1)S(1)} %get-tuple-element.57), channel_id=1, source_target_pairs={{0,4},{2,6},{4,0},{6,2},{1,5},{3,7},{5,1},{7,3},{8,12},{10,14},{12... | collective-permute-start | bytes 196616 | tf_op jit(solution)/shard_map/ppermute | solution.py:192
  64.9 9.3 %collective-permute-start.8 = (bf16[64,1024]{1,0:T(8,128)(2,1)S(1)}, bf16[64,1024]{1,0:T(8,128)(2,1)S(1)}, u32[]{:S(2)}, u32[]{:S(2)}) collective-permute-start(bf16[64,1024]{1,0:T(8,128)(2,1)S(1)} %pad_maximum_fusion.24), channel_id=1, source_target_pairs={{0,2},{2,0},{4,6},{6,4},{1,3},{3,1},{5,7},{7,5},{8,10},{10,8},{12,... | collective-permute-start | bytes 393224 | tf_op jit(solution)/shard_map/ppermute | solution.py:192
  66.7 6.0 %collective-permute-start.12 = (bf16[64,1024]{1,0:T(8,128)(2,1)S(1)}, bf16[64,1024]{1,0:T(8,128)(2,1)S(1)}, u32[]{:S(2)}, u32[]{:S(2)}) collective-permute-start(bf16[64,1024]{1,0:T(8,128)(2,1)S(1)} %pad_maximum_fusion.25), channel_id=1, source_target_pairs={{0,2},{2,0},{4,6},{6,4},{1,3},{3,1},{5,7},{7,5},{8,10},{10,8},{12,... | collective-permute-start | bytes 393224 | tf_op jit(solution)/shard_map/ppermute | solution.py:192
  67.1 7.1 %copy-start.3 = (bf16[128,4096]{1,0:T(8,128)(2,1)S(1)}, bf16[128,4096]{1,0:T(8,128)(2,1)}, u32[]{:S(2)}) copy-start(bf16[128,4096]{1,0:T(8,128)(2,1)} %copy-done.2) | copy-start | bytes 3145732
  67.1 27.8 %collective-permute-start.19 = (f32[64,1280]{1,0:T(8,128)S(1)}, f32[64,1280]{1,0:T(8,128)S(1)}, u32[]{:S(2)}, u32[]{:S(2)}) collective-permute-start(f32[64,1280]{1,0:T(8,128)S(1)} %fusion.19), channel_id=1, source_target_pairs={{0,24},{8,16},{16,8},{24,0},{1,25},{9,17},{17,9},{25,1},{2,26},{10... | collective-permute-start | bytes 983048 | tf_op jit(solution)/shard_map/ppermute | solution.py:192
  68.8 26.7 %collective-permute-start.18 = (f32[64,1280]{1,0:T(8,128)S(1)}, f32[64,1280]{1,0:T(8,128)S(1)}, u32[]{:S(2)}, u32[]{:S(2)}) collective-permute-start(f32[64,1280]{1,0:T(8,128)S(1)} %fusion.19), channel_id=1, source_target_pairs={{0,16},{8,24},{16,0},{24,8},{1,17},{9,25},{17,1},{25,9},{2,18},{10... | collective-permute-start | bytes 983048 | tf_op jit(solution)/shard_map/ppermute | solution.py:192
  70.2 25.3 %collective-permute-start.17 = (f32[64,1280]{1,0:T(8,128)S(1)}, f32[64,1280]{1,0:T(8,128)S(1)}, u32[]{:S(2)}, u32[]{:S(2)}) collective-permute-start(f32[64,1280]{1,0:T(8,128)S(1)} %fusion.19), channel_id=1, source_target_pairs={{0,8},{8,0},{16,24},{24,16},{1,9},{9,1},{17,25},{25,17},{2,10},{10... | collective-permute-start | bytes 983048 | tf_op jit(solution)/shard_map/ppermute | solution.py:192
  74.8 3.9 %copy-start.6 = (bf16[128,4096]{1,0:T(8,128)(2,1)S(1)}, bf16[128,4096]{1,0:T(8,128)(2,1)}, u32[]{:S(2)}) copy-start(bf16[128,4096]{1,0:T(8,128)(2,1)} %copy-done.5) | copy-start | bytes 3145732
  76.2 10.6 %collective-permute-start.14 = (bf16[64,1024]{1,0:T(8,128)(2,1)S(1)}, bf16[64,1024]{1,0:T(8,128)(2,1)S(1)}, u32[]{:S(2)}, u32[]{:S(2)}) collective-permute-start(bf16[64,1024]{1,0:T(8,128)(2,1)S(1)} %pad_maximum_fusion.26), channel_id=1, source_target_pairs={{0,2},{2,0},{4,6},{6,4},{1,3},{3,1},{5,7},{7,5},{8,10},{10,8},{12,... | collective-permute-start | bytes 393224 | tf_op jit(solution)/shard_map/ppermute | solution.py:192
  76.2 8.5 %collective-permute-start.13 = (bf16[64,1024]{1,0:T(8,128)(2,1)S(1)}, bf16[64,1024]{1,0:T(8,128)(2,1)S(1)}, u32[]{:S(2)}, u32[]{:S(2)}) collective-permute-start(bf16[64,1024]{1,0:T(8,128)(2,1)S(1)} %pad_maximum_fusion.26), channel_id=1, source_target_pairs={{0,4},{2,6},{4,0},{6,2},{1,5},{3,7},{5,1},{7,3},{8,12},{10,14},{12... | collective-permute-start | bytes 393224 | tf_op jit(solution)/shard_map/ppermute | solution.py:192
  84.8 6.8 %collective-permute-start.15 = (bf16[64,1024]{1,0:T(8,128)(2,1)S(1)}, bf16[64,1024]{1,0:T(8,128)(2,1)S(1)}, u32[]{:S(2)}, u32[]{:S(2)}) collective-permute-start(bf16[64,1024]{1,0:T(8,128)(2,1)S(1)} %pad_maximum_fusion.26), channel_id=1, source_target_pairs={{0,6},{2,4},{4,2},{6,0},{1,7},{3,5},{5,3},{7,1},{8,14},{10,12},{12... | collective-permute-start | bytes 393224 | tf_op jit(solution)/shard_map/ppermute | solution.py:192
  86.7 5.1 %collective-permute-start.20 = (f32[64,704]{1,0:T(8,128)S(1)}, f32[64,704]{1,0:T(8,128)S(1)}, u32[]{:S(2)}, u32[]{:S(2)}) collective-permute-start(f32[64,704]{1,0:T(8,128)S(1)} %pad_maximum_fusion.10), channel_id=1, source_target_pairs={{0,1},{1,0},{2,3},{3,2},{4,5},{5,4},{6,7},{7,6},{8,9},{9,8},{10,11... | collective-permute-start | bytes 540680 | tf_op jit(solution)/shard_map/ppermute | solution.py:192
  91.9 6.7 %collective-permute-start.23 = (f32[64,704]{1,0:T(8,128)S(1)}, f32[64,704]{1,0:T(8,128)S(1)}, u32[]{:S(2)}, u32[]{:S(2)}) collective-permute-start(f32[64,704]{1,0:T(8,128)S(1)} %fusion.28), channel_id=1, source_target_pairs={{0,24},{8,16},{16,8},{24,0},{1,25},{9,17},{17,9},{25,1},{2,26},{10... | collective-permute-start | bytes 540680 | tf_op jit(solution)/shard_map/ppermute | solution.py:192
  93.8 6.9 %collective-permute-start.22 = (f32[64,704]{1,0:T(8,128)S(1)}, f32[64,704]{1,0:T(8,128)S(1)}, u32[]{:S(2)}, u32[]{:S(2)}) collective-permute-start(f32[64,704]{1,0:T(8,128)S(1)} %fusion.28), channel_id=1, source_target_pairs={{0,16},{8,24},{16,0},{24,8},{1,17},{9,25},{17,1},{25,9},{2,18},{10... | collective-permute-start | bytes 540680 | tf_op jit(solution)/shard_map/ppermute | solution.py:192
  94.9 5.7 %collective-permute-start.21 = (f32[64,704]{1,0:T(8,128)S(1)}, f32[64,704]{1,0:T(8,128)S(1)}, u32[]{:S(2)}, u32[]{:S(2)}) collective-permute-start(f32[64,704]{1,0:T(8,128)S(1)} %fusion.28), channel_id=1, source_target_pairs={{0,8},{8,0},{16,24},{24,16},{1,9},{9,1},{17,25},{25,17},{2,10},{10... | collective-permute-start | bytes 540680 | tf_op jit(solution)/shard_map/ppermute | solution.py:192
  101.9 6.1 %collective-permute-start.24 = (f32[32,448]{1,0:T(8,128)S(1)}, f32[32,448]{1,0:T(8,128)S(1)}, u32[]{:S(2)}, u32[]{:S(2)}) collective-permute-start(f32[32,448]{1,0:T(8,128)S(1)} %constant_dynamic-slice_fusion.3), channel_id=1, source_target_pairs={{0,1},{1,0},{2,3},{3,2},{4,5},{5,4},{6,7},{7,6},{8,9},{9,8},{10,11... | collective-permute-start | bytes 172040 | tf_op jit(solution)/shard_map/ppermute | solution.py:192
  108.0 6.8 %collective-permute-start.27 = (f32[32,448]{1,0:T(8,128)S(1)}, f32[32,448]{1,0:T(8,128)S(1)}, u32[]{:S(2)}, u32[]{:S(2)}) collective-permute-start(f32[32,448]{1,0:T(8,128)S(1)} %dynamic-slice_add_fusion.2), channel_id=1, source_target_pairs={{0,6},{2,4},{4,2},{6,0},{1,7},{3,5},{5,3},{7,1},{8,14},{10,12},{12... | collective-permute-start | bytes 172040 | tf_op jit(solution)/shard_map/ppermute | solution.py:192
  110.1 7.1 %collective-permute-start.26 = (f32[32,448]{1,0:T(8,128)S(1)}, f32[32,448]{1,0:T(8,128)S(1)}, u32[]{:S(2)}, u32[]{:S(2)}) collective-permute-start(f32[32,448]{1,0:T(8,128)S(1)} %dynamic-slice_add_fusion.2), channel_id=1, source_target_pairs={{0,4},{2,6},{4,0},{6,2},{1,5},{3,7},{5,1},{7,3},{8,12},{10,14},{12... | collective-permute-start | bytes 172040 | tf_op jit(solution)/shard_map/ppermute | solution.py:192
  110.4 6.8 %collective-permute-start.25 = (f32[32,448]{1,0:T(8,128)S(1)}, f32[32,448]{1,0:T(8,128)S(1)}, u32[]{:S(2)}, u32[]{:S(2)}) collective-permute-start(f32[32,448]{1,0:T(8,128)S(1)} %dynamic-slice_add_fusion.2), channel_id=1, source_target_pairs={{0,2},{2,0},{4,6},{6,4},{1,3},{3,1},{5,7},{7,5},{8,10},{10,8},{12,... | collective-permute-start | bytes 172040 | tf_op jit(solution)/shard_map/ppermute | solution.py:192
  117.2 4.1 %collective-permute-start.28 = (f32[32,448]{1,0:T(8,128)S(1)}, f32[32,448]{1,0:T(8,128)S(1)}, u32[]{:S(2)}, u32[]{:S(2)}) collective-permute-start(f32[32,448]{1,0:T(8,128)S(1)} %add_multiply_fusion), channel_id=1, source_target_pairs={{0,1},{1,0},{2,3},{3,2},{4,5},{5,4},{6,7},{7,6},{8,9},{9,8},{10,11... | collective-permute-start | bytes 172040 | tf_op jit(solution)/shard_map/ppermute | solution.py:192
  122.7 9.3 %copy-start.1 = (f32[4096,64]{0,1:T(8,128)S(1)}, f32[4096,64]{0,1:T(8,128)}, u32[]{:S(2)}) copy-start(f32[4096,64]{0,1:T(8,128)} %param.5) | copy-start | bytes 3145732
  132.0 3.1 %copy-start.7 = (f32[192,128]{1,0:T(8,128)S(1)}, f32[192,128]{1,0:T(8,128)}, u32[]{:S(2)}) copy-start(f32[192,128]{1,0:T(8,128)} %get-tuple-element.19) | copy-start | bytes 294916
